TPU v7x, 512 devices: a whole 4x4x16 slice. The times are simulated.
512 devices in a mesh: lon: 32 (over x_lo, z), lat: 16 (over x_hi, y, core).
Axes of the slice: x: 4 (x_hi: 2, x_lo: 2; x = x_hi * 2 + x_lo), y: 4, z: 16, core: 2. Of those that a mesh axis runs over, the one named last changes fastest.
Arguments:
- fields: float32 [6, 4, 2048, 4096], P(None, None, 'lat', 'lon'), may hold values from -6 to 6
- face_weights: float32 [2, 2048, 4096], P(None, 'lat', 'lon'), may hold values from 0.5 to 1.5
- inv_area: float32 [2048, 4096], P('lat', 'lon'), may hold values from 0.5 to 1.5
- cell_mask: int32 [2048, 4096], P('lat', 'lon'), may hold values 0 or 1
- land_blocks: int32 [16, 32], P('lat', 'lon'), may hold values 0 or 1
Outputs:
- new_fields: float32 [6, 4, 2048, 4096], P(None, None, 'lat', 'lon')
All inputs are finite; a program needn't handle non-finite values. No bound on the sum of `cell_mask` or of `land_blocks` on one device may be relied on, other than what follows from the above.
Results may differ from a plain program's by a relative error of at most 0.00002.
Values sent between devices are 32-bit elements; how exact they have to be, the bound alone decides.
No kernel may reach another device: no remote copies, remote signals or barrier semaphores. Data moves between devices by JAX's collectives and lax.ppermute only.
A program may use at most 64 MiB of HBM per device.

v0:
```python
import jax
import jax.numpy as jnp
from jax import lax
from jax.sharding import PartitionSpec as P

SUBSTEPS = 2


TIME_STEP = 0.1
ADVECTION = 0.5


def swapped(value, axis, bit):
    mask = 2**bit
    pairs = [(source, source ^ mask) for source in range(lax.axis_size(axis))]
    return lax.ppermute(value, axis, pairs)


def with_halo(cells, sides, width, closed):
    for axis, dim in sides:
        count = lax.axis_size(axis)
        ends = count if closed else count - 1
        head = lax.slice_in_dim(cells, 0, width, axis=dim)
        tail = lax.slice_in_dim(cells, cells.shape[dim] - width, cells.shape[dim], axis=dim)
        cells = jnp.concatenate(
            [
                lax.ppermute(tail, axis, [(i, (i + 1) % count) for i in range(ends)]),
                cells,
                lax.ppermute(head, axis, [((i + 1) % count, i) for i in range(ends)]),
            ],
            axis=dim,
        )
    return cells


def face_flux(near_side, far_side, face_speed, face_weight):
    return face_weight * (
        ADVECTION * face_speed * (near_side + far_side) * 0.5 - (far_side - near_side)
    )


def tendency(lon_fields, lat_fields, east_ext, north_ext, inv_area):
    u_speed = lon_fields[4]
    east_speed = 0.5 * (u_speed[..., :-1] + u_speed[..., 1:])
    flux_east = face_flux(lon_fields[..., :-1], lon_fields[..., 1:], east_speed, east_ext)
    v_speed = lat_fields[5]
    north_speed = 0.5 * (v_speed[:, :-1, :] + v_speed[:, 1:, :])
    flux_north = face_flux(
        lat_fields[:, :, :-1, :], lat_fields[:, :, 1:, :], north_speed, north_ext
    )
    return inv_area * (
        flux_east[..., :-1]
        - flux_east[..., 1:]
        + (flux_north[:, :, :-1, :] - flux_north[:, :, 1:, :])
    )


def mirror_row(top_row):
    bit_total = lax.axis_size("lon").bit_length() - 1
    bit_order = list(range(bit_total))
    partner_row = top_row
    for bit_number in bit_order:
        partner_row = swapped(partner_row, "lon", bit_number)
    return partner_row[:, ::-1]


def advance_tile(values, lon_planes, lat_planes, east_ext, north_ext, area, mask, nfield, nlevel):
    shape_out = values.shape
    lon_fields = lon_planes.reshape((nfield, nlevel) + lon_planes.shape[1:])
    lat_fields = lat_planes.reshape((nfield, nlevel) + lat_planes.shape[1:])
    change = tendency(lon_fields, lat_fields, east_ext, north_ext, area)
    return values + TIME_STEP * mask * change.reshape(shape_out)


def local(fields, face_weights, inv_area, cell_mask, land_blocks):
    nfield, nlevel, row_count, col_count = fields.shape
    plane_count = nfield * nlevel
    is_top = lax.axis_index("lat") == lax.axis_size("lat") - 1
    ocean_mask = cell_mask.astype(jnp.float32) * (1 - land_blocks[0, 0]).astype(jnp.float32)
    flip_sign = jnp.where(jnp.arange(plane_count) // nlevel >= 4, -1.0, 1.0).astype(jnp.float32)[
        :, None
    ]
    planes = fields.reshape(plane_count, row_count, col_count)
    current = planes
    east_ext = face_weights[0]
    north_ext = face_weights[1]
    for substep in range(SUBSTEPS):
        if substep == 0:
            sending = jnp.concatenate([current, face_weights], axis=0)
        else:
            sending = current
        lon_ext = with_halo(sending, (("lon", 2),), 1, True)
        lat_ext = with_halo(sending, (("lat", 1),), 1, False)
        if substep == 0:
            east_ext = lon_ext[plane_count, :, :-1]
            north_ext = lat_ext[plane_count + 1, :-1, :]
        mirrored = mirror_row(current[:, row_count - 1, :])
        north_row = jnp.where(is_top, mirrored * flip_sign, lat_ext[:plane_count, -1, :])
        lat_full = jnp.concatenate([lat_ext[:plane_count, :-1, :], north_row[:, None, :]], axis=1)
        current = advance_tile(
            current,
            lon_ext[:plane_count],
            lat_full,
            east_ext,
            north_ext,
            inv_area,
            ocean_mask,
            nfield,
            nlevel,
        )
    return current.reshape(nfield, nlevel, row_count, col_count)


def solution(mesh):
    in_specs = (
        P(None, None, "lat", "lon"),
        P(None, "lat", "lon"),
        P("lat", "lon"),
        P("lat", "lon"),
        P("lat", "lon"),
    )
    out_specs = P(None, None, "lat", "lon")
    return jax.shard_map(local, mesh=mesh, in_specs=in_specs, out_specs=out_specs, check_vma=False)
```

profile of v0, /device:TPU:6, one launch (start us, length us, event | category | flops | bytes accessed | tf_op | source)
XLA Modules:
  0.0 158.5 jit_solution(12519006439694092602)
XLA Ops:
  0.0 1.9 %copy.226 = f32[6,4,128,128]{2,3,1,0:T(8,128)S(1)} copy(f32[6,4,128,128]{3,2,1,0:T(8,128)} %param.5) | data formatting | bytes 3145728 | tf_op args[0]
  3.9 2.0 %copy.230 = f32[26,1,128]{2,1,0:T(1,128)S(1)} copy(f32[26,1,128]{1,2,0:T(8,128)} %get-tuple-element.10) | data formatting | bytes 26624 | tf_op jit(solution)/shard_map/slice | solution.py:24
  5.8 1.9 %collective-permute-start.2 = (f32[26,1,128]{2,1,0:T(1,128)S(1)}, f32[26,1,128]{2,1,0:T(1,128)S(1)}, u32[]{:S(2)}, u32[]{:S(2)}) collective-permute-start(f32[26,1,128]{2,1,0:T(1,128)S(1)} %copy.230), channel_id=1, source_target_pairs={{0,1},{1,2},{2,3},{3,4},{4,5},{5,6},{6,7},{7,8},{8,9},{9,10},{10,1... | collective-permute-start | bytes 39944 | tf_op jit(solution)/shard_map/ppermute | solution.py:27
  8.3 7.4 %collective-permute-start.8 = (f32[26,1,128]{2,1,0:T(1,128)S(1)}, f32[26,1,128]{2,1,0:T(1,128)}, u32[]{:S(2)}, u32[]{:S(2)}) collective-permute-start(f32[26,1,128]{2,1,0:T(1,128)S(1)} %copy.232), channel_id=1, source_target_pairs={{1,0},{2,1},{3,2},{4,3},{5,4},{6,5},{7,6},{8,7},{9,8},{10,9},{11,1... | collective-permute-start | bytes 39944 | tf_op jit(solution)/shard_map/ppermute | solution.py:29
  16.6 3.8 %collective-permute-start.3 = (f32[24,128]{1,0:T(8,128)S(1)}, f32[24,128]{1,0:T(8,128)S(1)}, u32[]{:S(2)}, u32[]{:S(2)}) collective-permute-start(f32[24,128]{1,0:T(8,128)S(1)} %slice_reduce_fusion), channel_id=1, source_target_pairs={{0,16},{16,0},{32,48},{48,32},{64,80},{80,64},{96,112},{112,96},{1... | collective-permute-start | bytes 36872 | tf_op jit(solution)/shard_map/ppermute | solution.py:16
  20.4 2.0 %collective-permute-start = (f32[26,128,1]{1,2,0:T(1,128)S(1)}, f32[26,128,1]{1,2,0:T(1,128)S(1)}, u32[]{:S(2)}, u32[]{:S(2)}) collective-permute-start(f32[26,128,1]{1,2,0:T(1,128)S(1)} %get-tuple-element.7), channel_id=1, source_target_pairs={{0,16},{16,32},{32,48},{48,64},{64,80},{80,96},{96,112},{112,128},... | collective-permute-start | bytes 39944 | tf_op jit(solution)/shard_map/ppermute | solution.py:27
  22.4 10.7 %collective-permute-start.1 = (f32[26,128,1]{1,2,0:T(1,128)S(1)}, f32[26,128,1]{1,2,0:T(1,128)S(1)}, u32[]{:S(2)}, u32[]{:S(2)}) collective-permute-start(f32[26,128,1]{1,2,0:T(1,128)S(1)} %get-tuple-element.8), channel_id=1, source_target_pairs={{16,0},{32,16},{48,32},{64,48},{80,64},{96,80},{112,96},{128,112},... | collective-permute-start | bytes 39944 | tf_op jit(solution)/shard_map/ppermute | solution.py:29
  37.4 1.9 %collective-permute-start.4 = (f32[24,128]{1,0:T(8,128)S(1)}, f32[24,128]{1,0:T(8,128)S(1)}, u32[]{:S(2)}, u32[]{:S(2)}) collective-permute-start(f32[24,128]{1,0:T(8,128)S(1)} %collective-permute-done.3), channel_id=1, source_target_pairs={{0,32},{16,48},{32,0},{48,16},{64,96},{80,112},{96,64},{112,80},{1... | collective-permute-start | bytes 36872 | tf_op jit(solution)/shard_map/ppermute | solution.py:16
  40.0 3.9 %collective-permute-done.4 = f32[24,128]{1,0:T(8,128)S(1)} collective-permute-done((f32[24,128]{1,0:T(8,128)S(1)}, f32[24,128]{1,0:T(8,128)S(1)}, u32[]{:S(2)}, u32[]{:S(2)}) %collective-permute-start.4) | collective-permute-done | bytes 12320 | tf_op jit(solution)/shard_map/ppermute | solution.py:16
  43.9 3.4 %collective-permute-start.5 = (f32[24,128]{1,0:T(8,128)S(1)}, f32[24,128]{1,0:T(8,128)S(1)}, u32[]{:S(2)}, u32[]{:S(2)}) collective-permute-start(f32[24,128]{1,0:T(8,128)S(1)} %collective-permute-done.4), channel_id=1, source_target_pairs={{0,64},{16,80},{32,96},{48,112},{64,0},{80,16},{96,32},{112,48},{1... | collective-permute-start | bytes 36872 | tf_op jit(solution)/shard_map/ppermute | solution.py:16
  49.8 3.6 %collective-permute-done.5 = f32[24,128]{1,0:T(8,128)S(1)} collective-permute-done((f32[24,128]{1,0:T(8,128)S(1)}, f32[24,128]{1,0:T(8,128)S(1)}, u32[]{:S(2)}, u32[]{:S(2)}) %collective-permute-start.5) | collective-permute-done | bytes 12320 | tf_op jit(solution)/shard_map/ppermute | solution.py:16
  53.4 9.2 %collective-permute-start.6 = (f32[24,128]{1,0:T(8,128)S(1)}, f32[24,128]{1,0:T(8,128)S(1)}, u32[]{:S(2)}, u32[]{:S(2)}) collective-permute-start(f32[24,128]{1,0:T(8,128)S(1)} %collective-permute-done.5), channel_id=1, source_target_pairs={{0,128},{16,144},{32,160},{48,176},{64,192},{80,208},{96,224},{112... | collective-permute-start | bytes 36872 | tf_op jit(solution)/shard_map/ppermute | solution.py:16
  63.4 4.2 %collective-permute-done.6 = f32[24,128]{1,0:T(8,128)S(1)} collective-permute-done((f32[24,128]{1,0:T(8,128)S(1)}, f32[24,128]{1,0:T(8,128)S(1)}, u32[]{:S(2)}, u32[]{:S(2)}) %collective-permute-start.6) | collective-permute-done | bytes 12320 | tf_op jit(solution)/shard_map/ppermute | solution.py:16
  67.7 3.3 %collective-permute-start.7 = (f32[24,128]{1,0:T(8,128)S(1)}, f32[24,128]{1,0:T(8,128)}, u32[]{:S(2)}, u32[]{:S(2)}) collective-permute-start(f32[24,128]{1,0:T(8,128)S(1)} %collective-permute-done.6), channel_id=1, source_target_pairs={{0,256},{16,272},{32,288},{48,304},{64,320},{80,336},{96,352},{112... | collective-permute-start | bytes 36872 | tf_op jit(solution)/shard_map/ppermute | solution.py:16
  71.0 3.7 %copy.238 = f32[6,4,129,128]{2,1,0,3:T(4,128)} copy(f32[6,4,129,128]{2,3,1,0:T(8,128)S(1)} %bitcast.33) | data formatting | bytes 3170304 | tf_op jit(solution)/shard_map/concatenate | solution.py:99
  83.3 5.2 %fusion.3 = f32[6,4,129,128]{2,1,0,3:T(4,128)S(1)} fusion(f32[6,4,129,128]{2,1,0,3:T(4,128)} %copy.238, f32[6,4,1,128]{2,1,0,3:T(4,128)S(1)} %copy.237, f32[4,129,128]{1,0,2:T(4,128)} %copy.235, f32[129,128]{0,1:T(8,128)S(1)} %maximum_bitcast_fusion), kind=kLoop, calls=%fused_computation.4 | loop fusion | flops 2774016 | bytes 3512832 | tf_op jit(solution)/shard_map/mul | solution.py:37
  88.6 2.6 %multiply_add_fusion = (f32[6,4,128,128]{2,1,0,3:T(4,128)}, f32[6,4,128,128]{2,1,0,3:T(4,128)S(1)}) fusion(f32[6,4,128,128]{2,1,0,3:T(4,128)S(1)} %copy-done.5, f32[128,128]{0,1:T(8,128)S(1)} %copy-done.6, f32[6,4,129,128]{2,1,0,3:T(4,128)S(1)} %fusion.3, f32[6,4,128,129]{2,1,0,3:T(4,128)S(1)} %copy-done.3, f32[128,128]{0,1:T(8,128)S(1)} %copy-done.9), kind=kLoop, calls=%fused_computation.33 | loop fusion | flops 2359296 | bytes 11141120 | tf_op jit(solution)/shard_map/add | solution.py:72
  91.7 2.1 %fusion.24 = (f32[24,1,128]{1,2,0:T(8,128)S(1)}, f32[24,128]{1,0:T(8,128)S(1)}, f32[24,1,128]{1,2,0:T(8,128)}) fusion(f32[24,128,128]{1,2,0:T(8,128)S(1)} %fusion.12), kind=kLoop, calls=%fused_computation.66 | loop fusion | bytes 61440 | tf_op jit(solution)/shard_map/slice | solution.py:24
  93.9 1.9 %collective-permute-start.12 = (f32[24,128]{1,0:T(8,128)S(1)}, f32[24,128]{1,0:T(8,128)S(1)}, u32[]{:S(2)}, u32[]{:S(2)}) collective-permute-start(f32[24,128]{1,0:T(8,128)S(1)} %get-tuple-element.16), channel_id=1, source_target_pairs={{0,16},{16,0},{32,48},{48,32},{64,80},{80,64},{96,112},{112,96},{1... | collective-permute-start | bytes 36872 | tf_op jit(solution)/shard_map/ppermute | solution.py:16
  95.8 4.9 %collective-permute-start.10 = (f32[24,128,1]{1,2,0:T(1,128)S(1)}, f32[24,128,1]{1,2,0:T(1,128)S(1)}, u32[]{:S(2)}, u32[]{:S(2)}) collective-permute-start(f32[24,128,1]{1,2,0:T(1,128)S(1)} %get-tuple-element.14), channel_id=1, source_target_pairs={{16,0},{32,16},{48,32},{64,48},{80,64},{96,80},{112,96},{128,112},... | collective-permute-start | bytes 36872 | tf_op jit(solution)/shard_map/ppermute | solution.py:29
  100.7 1.9 %collective-permute-start.9 = (f32[24,128,1]{1,2,0:T(1,128)S(1)}, f32[24,128,1]{1,2,0:T(1,128)S(1)}, u32[]{:S(2)}, u32[]{:S(2)}) collective-permute-start(f32[24,128,1]{1,2,0:T(1,128)S(1)} %get-tuple-element.13), channel_id=1, source_target_pairs={{0,16},{16,32},{32,48},{48,64},{64,80},{80,96},{96,112},{112,128},... | collective-permute-start | bytes 36872 | tf_op jit(solution)/shard_map/ppermute | solution.py:27
  104.5 1.9 %collective-permute-start.17 = (f32[24,1,128]{2,0,1:T(8,128)S(1)}, f32[24,1,128]{2,0,1:T(8,128)S(1)}, u32[]{:S(2)}, u32[]{:S(2)}) collective-permute-start(f32[24,1,128]{2,0,1:T(8,128)S(1)} %copy.248), channel_id=1, source_target_pairs={{1,0},{2,1},{3,2},{4,3},{5,4},{6,5},{7,6},{8,7},{9,8},{10,9},{11,1... | collective-permute-start | bytes 36872 | tf_op jit(solution)/shard_map/ppermute | solution.py:29
  106.9 2.4 %collective-permute-start.11 = (f32[24,1,128]{2,0,1:T(8,128)S(1)}, f32[24,1,128]{2,0,1:T(8,128)S(1)}, u32[]{:S(2)}, u32[]{:S(2)}) collective-permute-start(f32[24,1,128]{2,0,1:T(8,128)S(1)} %copy.246), channel_id=1, source_target_pairs={{0,1},{1,2},{2,3},{3,4},{4,5},{5,6},{6,7},{7,8},{8,9},{9,10},{10,1... | collective-permute-start | bytes 36872 | tf_op jit(solution)/shard_map/ppermute | solution.py:27
  109.4 2.4 %collective-permute-start.13 = (f32[24,128]{1,0:T(8,128)S(1)}, f32[24,128]{1,0:T(8,128)S(1)}, u32[]{:S(2)}, u32[]{:S(2)}) collective-permute-start(f32[24,128]{1,0:T(8,128)S(1)} %collective-permute-done.12), channel_id=1, source_target_pairs={{0,32},{16,48},{32,0},{48,16},{64,96},{80,112},{96,64},{112,80},{1... | collective-permute-start | bytes 36872 | tf_op jit(solution)/shard_map/ppermute | solution.py:16
  111.9 3.9 %collective-permute-done.13 = f32[24,128]{1,0:T(8,128)S(1)} collective-permute-done((f32[24,128]{1,0:T(8,128)S(1)}, f32[24,128]{1,0:T(8,128)S(1)}, u32[]{:S(2)}, u32[]{:S(2)}) %collective-permute-start.13) | collective-permute-done | bytes 12320 | tf_op jit(solution)/shard_map/ppermute | solution.py:16
  115.8 3.5 %collective-permute-start.14 = (f32[24,128]{1,0:T(8,128)S(1)}, f32[24,128]{1,0:T(8,128)S(1)}, u32[]{:S(2)}, u32[]{:S(2)}) collective-permute-start(f32[24,128]{1,0:T(8,128)S(1)} %collective-permute-done.13), channel_id=1, source_target_pairs={{0,64},{16,80},{32,96},{48,112},{64,0},{80,16},{96,32},{112,48},{1... | collective-permute-start | bytes 36872 | tf_op jit(solution)/shard_map/ppermute | solution.py:16
  119.6 5.7 %collective-permute-done.14 = f32[24,128]{1,0:T(8,128)S(1)} collective-permute-done((f32[24,128]{1,0:T(8,128)S(1)}, f32[24,128]{1,0:T(8,128)S(1)}, u32[]{:S(2)}, u32[]{:S(2)}) %collective-permute-start.14) | collective-permute-done | bytes 12320 | tf_op jit(solution)/shard_map/ppermute | solution.py:16
  125.3 7.8 %collective-permute-start.15 = (f32[24,128]{1,0:T(8,128)S(1)}, f32[24,128]{1,0:T(8,128)}, u32[]{:S(2)}, u32[]{:S(2)}) collective-permute-start(f32[24,128]{1,0:T(8,128)S(1)} %collective-permute-done.14), channel_id=1, source_target_pairs={{0,128},{16,144},{32,160},{48,176},{64,192},{80,208},{96,224},{112... | collective-permute-start | bytes 36872 | tf_op jit(solution)/shard_map/ppermute | solution.py:16
  133.3 6.5 %collective-permute-done.15 = f32[24,128]{1,0:T(8,128)} collective-permute-done((f32[24,128]{1,0:T(8,128)S(1)}, f32[24,128]{1,0:T(8,128)}, u32[]{:S(2)}, u32[]{:S(2)}) %collective-permute-start.15) | collective-permute-done | bytes 12320 | tf_op jit(solution)/shard_map/ppermute | solution.py:16
  139.7 3.0 %collective-permute-start.16 = (f32[24,128]{1,0:T(8,128)}, f32[24,128]{1,0:T(8,128)S(1)}, u32[]{:S(2)}, u32[]{:S(2)}) collective-permute-start(f32[24,128]{1,0:T(8,128)} %collective-permute-done.15), channel_id=1, source_target_pairs={{0,256},{16,272},{32,288},{48,304},{64,320},{80,336},{96,352},{112... | collective-permute-start | bytes 36872 | tf_op jit(solution)/shard_map/ppermute | solution.py:16
  142.7 2.1 %subtract_multiply_fusion.1 = f32[6,4,128,129]{2,1,0,3:T(4,128)} fusion(f32[6,4,128,129]{2,3,1,0:T(8,128)S(1)} %get-tuple-element.12, f32[6,4,128,129]{2,3,1,0:T(8,128)S(1)} %get-tuple-element.11, f32[4,128,129]{1,0,2:T(4,128)S(1)} %copy.243, f32[128,129]{0,1:T(8,128)S(1)} %copy-done.8), kind=kLoop, calls=%fused_computation.18 | loop fusion | flops 2377728 | bytes 5085696 | tf_op jit(solution)/shard_map/mul | solution.py:37
  151.9 3.8 %subtract_multiply_fusion = f32[6,4,129,128]{2,1,0,3:T(4,128)S(1)} fusion(f32[6,4,1,128]{2,1,0,3:T(4,128)S(1)} %copy.252, f32[6,4,128,128]{2,1,0,3:T(4,128)S(1)} %copy-done.1, f32[6,4,1,128]{2,1,0,3:T(4,128)} %copy.251, f32[4,129,128]{1,0,2:T(4,128)} %copy.250, f32[129,128]{0,1:T(8,128)S(1)} %maximum_bitcast_fusion), kind=kLoop, calls=%fused_computation.11 | loop fusion | flops 3170304 | bytes 3512832 | tf_op jit(solution)/shard_map/mul | solution.py:37
  (85 shorter events, 32.9 us)
Async XLA Ops:
  0.0 1.9 %copy-start.10 = (f32[2,128,128]{2,1,0:T(8,128)S(1)}, f32[2,128,128]{2,1,0:T(8,128)}, u32[]{:S(2)}) copy-start(f32[2,128,128]{2,1,0:T(8,128)} %param.6) | copy-start | bytes 393220
  5.8 43.4 %collective-permute-start.2 = (f32[26,1,128]{2,1,0:T(1,128)S(1)}, f32[26,1,128]{2,1,0:T(1,128)S(1)}, u32[]{:S(2)}, u32[]{:S(2)}) collective-permute-start(f32[26,1,128]{2,1,0:T(1,128)S(1)} %copy.230), channel_id=1, source_target_pairs={{0,1},{1,2},{2,3},{3,4},{4,5},{5,6},{6,7},{7,8},{8,9},{9,10},{10,1... | collective-permute-start | bytes 39944 | tf_op jit(solution)/shard_map/ppermute | solution.py:27
  8.2 25.5 %copy-start.11 = (s32[128,128]{1,0:T(8,128)S(1)}, s32[128,128]{1,0:T(8,128)}, u32[]{:S(2)}) copy-start(s32[128,128]{1,0:T(8,128)} %param.8) | copy-start | bytes 196612
  8.2 26.1 %copy-start.4 = (f32[6,4,128,128]{3,2,1,0:T(8,128)S(1)}, f32[6,4,128,128]{3,2,1,0:T(8,128)}, u32[]{:S(2)}) copy-start(f32[6,4,128,128]{3,2,1,0:T(8,128)} %param.5) | copy-start | bytes 4718596
  8.3 66.5 %collective-permute-start.8 = (f32[26,1,128]{2,1,0:T(1,128)S(1)}, f32[26,1,128]{2,1,0:T(1,128)}, u32[]{:S(2)}, u32[]{:S(2)}) collective-permute-start(f32[26,1,128]{2,1,0:T(1,128)S(1)} %copy.232), channel_id=1, source_target_pairs={{1,0},{2,1},{3,2},{4,3},{5,4},{6,5},{7,6},{8,7},{9,8},{10,9},{11,1... | collective-permute-start | bytes 39944 | tf_op jit(solution)/shard_map/ppermute | solution.py:29
  16.6 20.8 %collective-permute-start.3 = (f32[24,128]{1,0:T(8,128)S(1)}, f32[24,128]{1,0:T(8,128)S(1)}, u32[]{:S(2)}, u32[]{:S(2)}) collective-permute-start(f32[24,128]{1,0:T(8,128)S(1)} %slice_reduce_fusion), channel_id=1, source_target_pairs={{0,16},{16,0},{32,48},{48,32},{64,80},{80,64},{96,112},{112,96},{1... | collective-permute-start | bytes 36872 | tf_op jit(solution)/shard_map/ppermute | solution.py:16
  20.4 18.9 %collective-permute-start = (f32[26,128,1]{1,2,0:T(1,128)S(1)}, f32[26,128,1]{1,2,0:T(1,128)S(1)}, u32[]{:S(2)}, u32[]{:S(2)}) collective-permute-start(f32[26,128,1]{1,2,0:T(1,128)S(1)} %get-tuple-element.7), channel_id=1, source_target_pairs={{0,16},{16,32},{32,48},{48,64},{64,80},{80,96},{96,112},{112,128},... | collective-permute-start | bytes 39944 | tf_op jit(solution)/shard_map/ppermute | solution.py:27
  22.4 16.9 %collective-permute-start.1 = (f32[26,128,1]{1,2,0:T(1,128)S(1)}, f32[26,128,1]{1,2,0:T(1,128)S(1)}, u32[]{:S(2)}, u32[]{:S(2)}) collective-permute-start(f32[26,128,1]{1,2,0:T(1,128)S(1)} %get-tuple-element.8), channel_id=1, source_target_pairs={{16,0},{32,16},{48,32},{64,48},{80,64},{96,80},{112,96},{128,112},... | collective-permute-start | bytes 39944 | tf_op jit(solution)/shard_map/ppermute | solution.py:29
  34.4 2.3 %copy-start.12 = (f32[128,128]{1,0:T(8,128)S(1)}, f32[128,128]{1,0:T(8,128)}, u32[]{:S(2)}) copy-start(f32[128,128]{1,0:T(8,128)} %param.7) | copy-start | bytes 196612
  37.4 6.5 %collective-permute-start.4 = (f32[24,128]{1,0:T(8,128)S(1)}, f32[24,128]{1,0:T(8,128)S(1)}, u32[]{:S(2)}, u32[]{:S(2)}) collective-permute-start(f32[24,128]{1,0:T(8,128)S(1)} %collective-permute-done.3), channel_id=1, source_target_pairs={{0,32},{16,48},{32,0},{48,16},{64,96},{80,112},{96,64},{112,80},{1... | collective-permute-start | bytes 36872 | tf_op jit(solution)/shard_map/ppermute | solution.py:16
  39.6 7.8 %copy-start.7 = (f32[128,129]{0,1:T(8,128)}, f32[128,129]{0,1:T(8,128)S(1)}, u32[]{:S(2)}) copy-start(f32[128,129]{0,1:T(8,128)S(1)} %maximum_bitcast_fusion.1) | copy-start | bytes 198148
  43.9 9.5 %collective-permute-start.5 = (f32[24,128]{1,0:T(8,128)S(1)}, f32[24,128]{1,0:T(8,128)S(1)}, u32[]{:S(2)}, u32[]{:S(2)}) collective-permute-start(f32[24,128]{1,0:T(8,128)S(1)} %collective-permute-done.4), channel_id=1, source_target_pairs={{0,64},{16,80},{32,96},{48,112},{64,0},{80,16},{96,32},{112,48},{1... | collective-permute-start | bytes 36872 | tf_op jit(solution)/shard_map/ppermute | solution.py:16
  53.4 14.3 %collective-permute-start.6 = (f32[24,128]{1,0:T(8,128)S(1)}, f32[24,128]{1,0:T(8,128)S(1)}, u32[]{:S(2)}, u32[]{:S(2)}) collective-permute-start(f32[24,128]{1,0:T(8,128)S(1)} %collective-permute-done.5), channel_id=1, source_target_pairs={{0,128},{16,144},{32,160},{48,176},{64,192},{80,208},{96,224},{112... | collective-permute-start | bytes 36872 | tf_op jit(solution)/shard_map/ppermute | solution.py:16
  63.4 7.6 %copy-start = (f32[24,129,128]{1,2,0:T(8,128)}, f32[24,129,128]{1,2,0:T(8,128)S(1)}, u32[]{:S(2)}) copy-start(f32[24,129,128]{1,2,0:T(8,128)S(1)} %pad_maximum_fusion.1) | copy-start | bytes 4755460
  67.7 8.4 %collective-permute-start.7 = (f32[24,128]{1,0:T(8,128)S(1)}, f32[24,128]{1,0:T(8,128)}, u32[]{:S(2)}, u32[]{:S(2)}) collective-permute-start(f32[24,128]{1,0:T(8,128)S(1)} %collective-permute-done.6), channel_id=1, source_target_pairs={{0,256},{16,272},{32,288},{48,304},{64,320},{80,336},{96,352},{112... | collective-permute-start | bytes 36872 | tf_op jit(solution)/shard_map/ppermute | solution.py:16
  83.3 5.3 %copy-start.3 = (f32[6,4,128,129]{2,1,0,3:T(4,128)S(1)}, f32[6,4,128,129]{2,1,0,3:T(4,128)}, u32[]{:S(2)}) copy-start(f32[6,4,128,129]{2,1,0,3:T(4,128)} %subtract_multiply_fusion.2) | copy-start | bytes 4755460
  83.3 5.3 %copy-start.5 = (f32[6,4,128,128]{2,1,0,3:T(4,128)S(1)}, f32[6,4,128,128]{2,1,0,3:T(4,128)}, u32[]{:S(2)}) copy-start(f32[6,4,128,128]{2,1,0,3:T(4,128)} %copy.240) | copy-start | bytes 4718596
  83.3 5.3 %copy-start.6 = (f32[128,128]{0,1:T(8,128)S(1)}, f32[128,128]{0,1:T(8,128)}, u32[]{:S(2)}) copy-start(f32[128,128]{0,1:T(8,128)} %copy.224) | copy-start | bytes 196612
  83.3 5.3 %copy-start.9 = (f32[128,128]{0,1:T(8,128)S(1)}, f32[128,128]{0,1:T(8,128)}, u32[]{:S(2)}) copy-start(f32[128,128]{0,1:T(8,128)} %copy.225) | copy-start | bytes 196612
  93.9 15.5 %collective-permute-start.12 = (f32[24,128]{1,0:T(8,128)S(1)}, f32[24,128]{1,0:T(8,128)S(1)}, u32[]{:S(2)}, u32[]{:S(2)}) collective-permute-start(f32[24,128]{1,0:T(8,128)S(1)} %get-tuple-element.16), channel_id=1, source_target_pairs={{0,16},{16,0},{32,48},{48,32},{64,80},{80,64},{96,112},{112,96},{1... | collective-permute-start | bytes 36872 | tf_op jit(solution)/shard_map/ppermute | solution.py:16
  95.8 15.9 %collective-permute-start.10 = (f32[24,128,1]{1,2,0:T(1,128)S(1)}, f32[24,128,1]{1,2,0:T(1,128)S(1)}, u32[]{:S(2)}, u32[]{:S(2)}) collective-permute-start(f32[24,128,1]{1,2,0:T(1,128)S(1)} %get-tuple-element.14), channel_id=1, source_target_pairs={{16,0},{32,16},{48,32},{64,48},{80,64},{96,80},{112,96},{128,112},... | collective-permute-start | bytes 36872 | tf_op jit(solution)/shard_map/ppermute | solution.py:29
  100.7 11.0 %collective-permute-start.9 = (f32[24,128,1]{1,2,0:T(1,128)S(1)}, f32[24,128,1]{1,2,0:T(1,128)S(1)}, u32[]{:S(2)}, u32[]{:S(2)}) collective-permute-start(f32[24,128,1]{1,2,0:T(1,128)S(1)} %get-tuple-element.13), channel_id=1, source_target_pairs={{0,16},{16,32},{32,48},{48,64},{64,80},{80,96},{96,112},{112,128},... | collective-permute-start | bytes 36872 | tf_op jit(solution)/shard_map/ppermute | solution.py:27
  104.5 42.5 %collective-permute-start.17 = (f32[24,1,128]{2,0,1:T(8,128)S(1)}, f32[24,1,128]{2,0,1:T(8,128)S(1)}, u32[]{:S(2)}, u32[]{:S(2)}) collective-permute-start(f32[24,1,128]{2,0,1:T(8,128)S(1)} %copy.248), channel_id=1, source_target_pairs={{1,0},{2,1},{3,2},{4,3},{5,4},{6,5},{7,6},{8,7},{9,8},{10,9},{11,1... | collective-permute-start | bytes 36872 | tf_op jit(solution)/shard_map/ppermute | solution.py:29
  106.9 37.9 %collective-permute-start.11 = (f32[24,1,128]{2,0,1:T(8,128)S(1)}, f32[24,1,128]{2,0,1:T(8,128)S(1)}, u32[]{:S(2)}, u32[]{:S(2)}) collective-permute-start(f32[24,1,128]{2,0,1:T(8,128)S(1)} %copy.246), channel_id=1, source_target_pairs={{0,1},{1,2},{2,3},{3,4},{4,5},{5,6},{6,7},{7,8},{8,9},{9,10},{10,1... | collective-permute-start | bytes 36872 | tf_op jit(solution)/shard_map/ppermute | solution.py:27
  109.4 6.5 %collective-permute-start.13 = (f32[24,128]{1,0:T(8,128)S(1)}, f32[24,128]{1,0:T(8,128)S(1)}, u32[]{:S(2)}, u32[]{:S(2)}) collective-permute-start(f32[24,128]{1,0:T(8,128)S(1)} %collective-permute-done.12), channel_id=1, source_target_pairs={{0,32},{16,48},{32,0},{48,16},{64,96},{80,112},{96,64},{112,80},{1... | collective-permute-start | bytes 36872 | tf_op jit(solution)/shard_map/ppermute | solution.py:16
  115.8 9.5 %collective-permute-start.14 = (f32[24,128]{1,0:T(8,128)S(1)}, f32[24,128]{1,0:T(8,128)S(1)}, u32[]{:S(2)}, u32[]{:S(2)}) collective-permute-start(f32[24,128]{1,0:T(8,128)S(1)} %collective-permute-done.13), channel_id=1, source_target_pairs={{0,64},{16,80},{32,96},{48,112},{64,0},{80,16},{96,32},{112,48},{1... | collective-permute-start | bytes 36872 | tf_op jit(solution)/shard_map/ppermute | solution.py:16
  119.6 23.1 %copy-start.8 = (f32[128,129]{0,1:T(8,128)S(1)}, f32[128,129]{0,1:T(8,128)}, u32[]{:S(2)}) copy-start(f32[128,129]{0,1:T(8,128)} %copy-done.7) | copy-start | bytes 198148
  125.3 14.4 %collective-permute-start.15 = (f32[24,128]{1,0:T(8,128)S(1)}, f32[24,128]{1,0:T(8,128)}, u32[]{:S(2)}, u32[]{:S(2)}) collective-permute-start(f32[24,128]{1,0:T(8,128)S(1)} %collective-permute-done.14), channel_id=1, source_target_pairs={{0,128},{16,144},{32,160},{48,176},{64,192},{80,208},{96,224},{112... | collective-permute-start | bytes 36872 | tf_op jit(solution)/shard_map/ppermute | solution.py:16
  139.7 7.2 %collective-permute-start.16 = (f32[24,128]{1,0:T(8,128)}, f32[24,128]{1,0:T(8,128)S(1)}, u32[]{:S(2)}, u32[]{:S(2)}) collective-permute-start(f32[24,128]{1,0:T(8,128)} %collective-permute-done.15), channel_id=1, source_target_pairs={{0,256},{16,272},{32,288},{48,304},{64,320},{80,336},{96,352},{112... | collective-permute-start | bytes 36872 | tf_op jit(solution)/shard_map/ppermute | solution.py:16
  144.9 2.2 %copy-start.13 = (f32[24]{0:T(128)S(1)}, f32[24]{0:T(128)}, u32[]{:S(2)}) copy-start(f32[24]{0:T(128)} %compare_select_fusion) | copy-start | bytes 292
  150.0 1.9 %copy-start.1 = (f32[6,4,128,128]{2,1,0,3:T(4,128)S(1)}, f32[6,4,128,128]{2,1,0,3:T(4,128)}, u32[]{:S(2)}) copy-start(f32[6,4,128,128]{2,1,0,3:T(4,128)} %get-tuple-element.5) | copy-start | bytes 4718596
  151.9 3.8 %copy-start.2 = (f32[6,4,128,129]{2,1,0,3:T(4,128)S(1)}, f32[6,4,128,129]{2,1,0,3:T(4,128)}, u32[]{:S(2)}) copy-start(f32[6,4,128,129]{2,1,0,3:T(4,128)} %subtract_multiply_fusion.1) | copy-start | bytes 4755460
where the time goes:
time: 160 us; the launch traced here: 159 us
  starting transfers between devices  73.3 us (46%)
  local copies, waits for them, and re-layouts  31.8 us (20%)
  waiting for transfers between devices  27.9 us (17%)
  other arithmetic  24.4 us (15%)
    ppermute x10, starting transfers between devices, swapped(): return lax.ppermute(value, axis, pairs)  40.1 us
    ppermute x10, waiting for transfers between devices, swapped(): return lax.ppermute(value, axis, pairs)  27.8 us
    ppermute x4, starting transfers between devices, with_halo(): lax.ppermute(head, axis, [((i + 1) % count, i) for i in range(ends)])  24.9 us
    mul x6, other arithmetic, face_flux(): face_weight * (ADVECTION * face_speed * (near_side + far_side) * 0.5 - (f...  13.1 us
    ppermute x4, starting transfers between devices, with_halo(): lax.ppermute(tail, axis, [(i, (i + 1) % count) for i in range(ends)])  8.27 us
    concatenate x4, local copies, waits for them, and re-layouts, local(): jnp.concatenate([lat_ext[:plane_count, :-1, :], north_row[:, None, :]], a...  6.71 us
    slice x4, local copies, waits for them, and re-layouts, with_halo(): lax.slice_in_dim(cells, cells.shape[dim] - width, cells.shape[dim], axis=...  4.57 us
    unnamed x32, local copies, waits for them, and re-layouts  4.33 us
  transfers between devices with their start and end apart: 18, of which 6 were waited for; matrix products, arithmetic and copies ran while one was open for 13% of the time, Pallas kernels for 0%

commit v1 on v0

v1 whole, which is shorter than its diff:
```python
import functools

import jax
import jax.numpy as jnp
from jax import lax
from jax.experimental import pallas as pl
from jax.experimental.pallas import tpu as pltpu
from jax.sharding import PartitionSpec as P

F32 = jnp.float32
TIME_STEP = 0.1
NP = 24
GE, GN, GM, GS = 24, 25, 26, 27
ROWS2, ROWS4 = 56, 112
PAD = 8
CHUNK = 32
HIGH = lax.Precision.HIGHEST


def lon_pairs(nlon, nlat, odd):
    def other(i):
        if not odd:
            return i ^ 1
        return (i + 1) % nlon if i % 2 else (i - 1) % nlon

    return [(i * nlat + l, other(i) * nlat + l) for i in range(nlon) for l in range(nlat)]


def lat_pairs(nlon, nlat, odd):
    pairs = []
    for i in range(nlon):
        for l in range(nlat):
            if not odd:
                pairs.append((i * nlat + l, i * nlat + (l ^ 1)))
            elif l == nlat - 1:
                pairs.append((i * nlat + l, (nlon - 1 - i) * nlat + l))
            elif l > 0:
                pairs.append((i * nlat + l, i * nlat + (l + 1 if l % 2 else l - 1)))
    return pairs


def lanes(shape):
    return lax.broadcasted_iota(jnp.int32, shape, 1)


def rows_of(shape):
    return lax.broadcasted_iota(jnp.int32, shape, 0)


def roll(x, shift, axis):
    n = x.shape[axis]
    shift %= n
    return x if shift == 0 else pltpu.roll(x, shift, axis)


def step_factor(area, mask, land):
    sea = mask.astype(F32) * (1 - land).astype(F32)
    return TIME_STEP * sea * area


def coefs(u, ue, uw, v, vn, vs, me, mw, mn, ms, base):
    te = me * (0.125 * (u + ue))
    tw = mw * (0.125 * (u + uw))
    tn = mn * (0.125 * (v + vn))
    ts = ms * (0.125 * (v + vs))
    return me - te, mw + tw, mn - tn, ms + ts, base + ((tw - te) + (ts - tn))


def apply(c, x, xe, xw, xn, xs):
    ce, cw, cn, cs, cc = c
    return cc * x + ((ce * xe + cw * xw) + (cn * xn + cs * xs))


def rows_kernel(f_lo, f_hi, w_lo, w_hi, a_lo, a_hi, k_lo, k_hi, land, to_odd, to_even):
    odd = lax.axis_index("lat") % 2 == 1
    m_lo = step_factor(a_lo[0:2], k_lo[0:2], land[0, 0])
    m_hi = step_factor(a_hi[6:8], k_hi[6:8], land[0, 0])
    zero = jnp.zeros((2, 128), F32)
    for g in range(28):
        if g < NP:
            south, north = f_lo[g, 0:2], f_hi[g, 6:8]
        elif g < GM:
            south, north = w_lo[g - NP, 0:2], w_hi[g - NP, 6:8]
        elif g == GM:
            south, north = m_lo, m_hi
        else:
            south, north = zero, zero
        to_odd[2 * g : 2 * g + 2] = jnp.where(odd, north, south)
        to_even[2 * g : 2 * g + 2] = jnp.where(odd, south, north)


def columns_kernel(f, w, area, mask, land, out):
    for r in range(0, 128, CHUNK):
        rr = slice(r, r + CHUNK)
        group = lanes((CHUNK, 128)) // 4
        acc = jnp.zeros((CHUNK, 128), F32)
        for g in range(GM + 1):
            if g < NP:
                x = f[g, rr]
            elif g < GM:
                x = w[g - NP, rr]
            else:
                x = step_factor(area[rr], mask[rr], land[0, 0])
            acc = jnp.where(group == g, roll(x, 4 * g + 2, 1), acc)
        out[rr] = acc


def strips_kernel(to_odd, to_even, got_odd, got_even, pack, out, north, south, recv):
    odd = lax.axis_index("lat") % 2 == 1
    top = lax.axis_index("lat") == lax.axis_size("lat") - 1
    raw = jnp.where(odd, got_odd[...], got_even[...])
    row = rows_of((ROWS2, 128))
    flip = (rows_of((128, 128)) + lanes((128, 128)) == 127).astype(F32)
    mirrored = jnp.dot(raw, flip, precision=HIGH, preferred_element_type=F32)
    mirrored = jnp.where((row >= 32) & (row < 48), -mirrored, mirrored)
    mirrored = jnp.where(row % 2 == 0, roll(mirrored, -1, 0), roll(mirrored, 1, 0))
    recv[0] = jnp.where(top, mirrored, raw)
    recv[1] = jnp.where(odd, got_even[...], got_odd[...])
    recv[2] = jnp.where(odd, to_odd[...], to_even[...])
    recv[3] = jnp.where(odd, to_even[...], to_odd[...])
    for g in range(28):
        two = slice(2 * g, 2 * g + 2)
        north[4 * g : 4 * g + 2] = recv[2, two]
        north[4 * g + 2 : 4 * g + 4] = recv[0, two]
        south[4 * g : 4 * g + 2] = recv[1, two]
        south[4 * g + 2 : 4 * g + 4] = recv[3, two]
    a, b = recv[0, 2 * GN : 2 * GN + 1], recv[0, 2 * GN + 1 : 2 * GN + 2]
    north[4 * GN + 2 : 4 * GN + 3] = jnp.where(top, b, a)
    north[4 * GS + 2 : 4 * GS + 3] = jnp.where(top, a, recv[2, 2 * GN + 1 : 2 * GN + 2])
    south[4 * GS + 1 : 4 * GS + 2] = recv[1, 2 * GN : 2 * GN + 1]
    lane = lanes((ROWS4, 128))
    acc = jnp.where(lane // 4 == 28, roll(north[...], 114, 1), pack[0:ROWS4])
    out[0:ROWS4] = jnp.where(lane // 4 == 29, roll(south[...], 118, 1), acc)
    out[ROWS4:128] = pack[ROWS4:128]


def repeat_group(x, g):
    y = roll(x, -4 * g, 1)
    y = jnp.where(lanes(y.shape) < 4, y, 0.0)
    for s in (4, 8, 16, 32, 64):
        y = y + roll(y, s, 1)
    return y


def repeat_field(x, f):
    y = jnp.where(lanes(x.shape) // 16 == f, x, 0.0)
    for s in (16, 32, 64):
        y = y + roll(y, s, 1)
    return y


def repeat_half(v, half):
    low = rows_of(v.shape) < 4
    other = roll(v, 4, 0)
    return jnp.where(low, v, other) if half == 0 else jnp.where(low, other, v)


def lat_strip(strip, from_west, from_east, shift_w, shift_e, top):
    lane = lanes((8, 128))
    def tile(t):
        x = strip[8 * t : 8 * t + 8]
        w = roll(from_west[8 * t : 8 * t + 8], shift_w, 1)
        e = roll(from_east[8 * t : 8 * t + 8], shift_e, 1)
        return x, jnp.where(lane == 127, e, roll(x, -1, 1)), jnp.where(lane == 0, w, roll(x, 1, 1))

    x12, e12, w12 = tile(12)
    x13, _, _ = tile(13)
    here, right, left = (repeat_half(a, 0) for a in (x12, e12, w12))
    we = here if top is None else jnp.where(top, right, here)
    ww = left if top is None else jnp.where(top, here, left)
    m = repeat_half(x13, 0)
    me, mw = m * we, m * ww
    mn, ms = m * repeat_half(x12, 1), m * repeat_half(x13, 1)
    base = 1.0 - ((me + mw) + (mn + ms))
    c = []
    for t in range(2):
        u, ue, uw = tile(8 + t)
        v = tile(10 + t)[0]
        c.append(coefs(u, ue, uw, v, roll(v, -1, 0), roll(v, 1, 0), me, mw, mn, ms, base))
    out = []
    for t in range(12):
        x, xe, xw = tile(t)
        out.append(apply(c[t % 2], x, xe, xw, roll(x, -1, 0), roll(x, 1, 0)))
    return out


def step_kernel(f_hbm, w, area, mask, land, pack, got_even, got_odd, north, south, out_hbm,
                buf, mid, res, side, side_v, side_w, edge, edge1, halo1, mw5, sem_in, sem_out):
    odd = lax.axis_index("lon") % 2 == 1
    top = lax.axis_index("lat") == lax.axis_size("lat") - 1
    copies = [
        pltpu.make_async_copy(f_hbm.at[:, k], buf.at[:, k, pl.ds(PAD, 128)], sem_in.at[k])
        for k in range(4)
    ]
    for c in copies:
        c.start()

    west = jnp.where(odd, got_even[...], got_odd[...])
    east = jnp.where(odd, got_odd[...], got_even[...])
    own = pack[...]
    lane = lanes((128, 128))
    j = lane % 4

    both = jnp.where(lane < 120, west, roll(east, 8, 1))
    turned = both.T
    nw, ne = roll(turned[113:114], -1, 1), turned[122:123]
    sw, se = turned[117:118], roll(turned[126:127], 1, 1)

    for s, (strip, above, below) in enumerate(
        (
            (jnp.where(j < 2, west, own), nw, sw),
            (jnp.where(j < 2, own, east), ne, se),
        )
    ):
        side[s, PAD : PAD + 128] = strip
        side[s, PAD - 1 : PAD] = below
        side[s, PAD + 128 : PAD + 129] = above
        for r in range(0, 128 + 2 * PAD, 16):
            x = side[s, r : r + 16]
            side_v[s, r : r + 16] = repeat_field(x, 5)
            side_w[s, r : r + 16] = repeat_group(x, GN)
    edge[...] = jnp.where(j == 1, side[0, PAD : PAD + 128], roll(side[1, PAD : PAD + 128], -2, 1))
    for r in range(0, 128, CHUNK):
        new = []
        for s in range(2):
            at = lambda ref, d: ref[s, PAD + r + d : PAD + r + d + CHUNK]
            x = at(side, 0)
            we, m, u = repeat_group(x, GE), repeat_group(x, GM), repeat_field(x, 4)
            me, mw = m * we, m * roll(we, 1, 1)
            mn, ms = m * at(side_w, 0), m * at(side_w, -1)
            base = 1.0 - ((me + mw) + (mn + ms))
            c = coefs(u, roll(u, -1, 1), roll(u, 1, 1), at(side_v, 0), at(side_v, 1), at(side_v, -1),
                      me, mw, mn, ms, base)
            new.append(apply(c, x, roll(x, -1, 1), roll(x, 1, 1), at(side, 1), at(side, -1)))
        jj = lanes((CHUNK, 128)) % 4
        edge1[r : r + CHUNK] = jnp.where(jj == 1, new[0], roll(new[1], -2, 1))

    for s, tiles in enumerate(
        (
            lat_strip(south, west, east, 11, 9, None),
            lat_strip(north, west, east, 15, 13, top),
        )
    ):
        for t in range(12):
            halo1[s, 8 * t : 8 * t + 8] = tiles[t]

    m = step_factor(area[...], mask[...], land[0, 0])
    we, wn = w[0], w[1]
    ww = jnp.where(lane == 0, roll(edge[...], -(4 * GE + 1), 1), roll(we, 1, 1))
    first = rows_of((128, 128)) == 0
    ws = jnp.where(first, south[4 * GN + 1 : 4 * GN + 2], roll(wn, 1, 0))
    me, mw, mn, ms = m * we, m * ww, m * wn, m * ws
    for n, x in enumerate((me, mw, mn, ms, 1.0 - ((me + mw) + (mn + ms)))):
        mw5[n] = x

    def substep(get, ring, put, k):
        lane = lanes((CHUNK, 128))
        for r in range(0, 128, CHUNK):
            rr = slice(r, r + CHUNK)

            def around(f):
                x = get(f, r)
                col = roll(ring[rr], -(4 * (4 * f + k) + 1), 1)
                xe = jnp.where(lane == 127, col, roll(x, -1, 1))
                xw = jnp.where(lane == 0, col, roll(x, 1, 1))
                return x, xe, xw, get(f, r + 1), get(f, r - 1)

            u, ue, uw, _, _ = around(4)
            v, vn, vs = get(5, r), get(5, r + 1), get(5, r - 1)
            c = coefs(u, ue, uw, v, vn, vs, mw5[0, rr], mw5[1, rr], mw5[2, rr], mw5[3, rr], mw5[4, rr])
            for f in range(6):
                put(f, r, apply(c, *around(f)))

    outs = []
    for k in range(4):
        for f in range(6):
            g = 4 * f + k
            mid[f, PAD - 1 : PAD] = halo1[0, 4 * g + 1 : 4 * g + 2]
            mid[f, PAD + 128 : PAD + 129] = halo1[1, 4 * g + 2 : 4 * g + 3]
        copies[k].wait()
        for f in range(6):
            g = 4 * f + k
            buf[f, k, PAD - 1 : PAD] = south[4 * g + 1 : 4 * g + 2]
            buf[f, k, PAD + 128 : PAD + 129] = north[4 * g + 2 : 4 * g + 3]

        def put_mid(f, r, x):
            mid[f, PAD + r : PAD + r + CHUNK] = x

        def put_res(f, r, x):
            res[f, k, r : r + CHUNK] = x

        substep(lambda f, r: buf[f, k, PAD + r : PAD + r + CHUNK], edge, put_mid, k)
        substep(lambda f, r: mid[f, PAD + r : PAD + r + CHUNK], edge1, put_res, k)
        c = pltpu.make_async_copy(res.at[:, k], out_hbm.at[:, k], sem_out.at[k])
        c.start()
        outs.append(c)
    for c in outs:
        c.wait()


def cost(nbytes, flops):
    return pl.CostEstimate(flops=flops, bytes_accessed=nbytes, transcendentals=0)


def vmem():
    return pl.BlockSpec(memory_space=pltpu.VMEM)


def smem():
    return pl.BlockSpec(memory_space=pltpu.SMEM)


def local(nlon, nlat, fields, weights, area, mask, land):
    shape = jax.ShapeDtypeStruct
    planes = fields.reshape(NP, 128, 128)
    params = pltpu.CompilerParams(vmem_limit_bytes=24 << 20)

    def lo3(n):
        return pl.BlockSpec((n, 8, 128), lambda i: (0, 0, 0))

    def hi3(n):
        return pl.BlockSpec((n, 8, 128), lambda i: (0, 15, 0))

    lo2 = pl.BlockSpec((8, 128), lambda i: (0, 0))
    hi2 = pl.BlockSpec((8, 128), lambda i: (15, 0))
    whole = pl.BlockSpec((ROWS2, 128), lambda i: (0, 0))
    rows = shape((ROWS2, 128), F32)
    to_odd, to_even = pl.pallas_call(
        rows_kernel,
        grid=(1,),
        out_shape=(rows, rows),
        in_specs=[lo3(NP), hi3(NP), lo3(2), hi3(2), lo2, hi2, lo2, hi2, smem()],
        out_specs=(whole, whole),
        compiler_params=params,
        cost_estimate=cost(1 << 18, 1 << 16),
        name="rows",
    )(planes, planes, weights, weights, area, area, mask, mask, land)

    axes = ("lon", "lat")
    with jax.named_scope("lat_odd"):
        got_odd = lax.ppermute(to_odd, axes, lat_pairs(nlon, nlat, True))
    with jax.named_scope("lat_even"):
        got_even = lax.ppermute(to_even, axes, lat_pairs(nlon, nlat, False))

    tile = shape((128, 128), F32)
    pack = pl.pallas_call(
        columns_kernel,
        out_shape=tile,
        in_specs=[vmem()] * 4 + [smem()],
        out_specs=vmem(),
        compiler_params=params,
        cost_estimate=cost(2 << 20, 1 << 20),
        name="columns",
    )(planes, weights, area, mask, land)

    pack, north, south = pl.pallas_call(
        strips_kernel,
        out_shape=(tile, shape((ROWS4, 128), F32), shape((ROWS4, 128), F32)),
        in_specs=[vmem()] * 5,
        out_specs=(vmem(),) * 3,
        scratch_shapes=[pltpu.VMEM((4, ROWS2, 128), F32)],
        compiler_params=params,
        cost_estimate=cost(1 << 18, 1 << 18),
        name="strips",
    )(to_odd, to_even, got_odd, got_even, pack)

    with jax.named_scope("lon_even"):
        col_even = lax.ppermute(pack, axes, lon_pairs(nlon, nlat, False))
    with jax.named_scope("lon_odd"):
        col_odd = lax.ppermute(pack, axes, lon_pairs(nlon, nlat, True))

    padded = 128 + 2 * PAD
    return pl.pallas_call(
        step_kernel,
        out_shape=shape((6, 4, 128, 128), F32),
        in_specs=[pl.BlockSpec(memory_space=pl.ANY)] + [vmem()] * 3 + [smem()] + [vmem()] * 5,
        out_specs=pl.BlockSpec(memory_space=pl.ANY),
        scratch_shapes=[
            pltpu.VMEM((6, 4, padded, 128), F32),
            pltpu.VMEM((6, padded, 128), F32),
            pltpu.VMEM((6, 4, 128, 128), F32),
            pltpu.VMEM((2, padded, 128), F32),
            pltpu.VMEM((2, padded, 128), F32),
            pltpu.VMEM((2, padded, 128), F32),
            pltpu.VMEM((128, 128), F32),
            pltpu.VMEM((128, 128), F32),
            pltpu.VMEM((2, 96, 128), F32),
            pltpu.VMEM((5, 128, 128), F32),
            pltpu.SemaphoreType.DMA((4,)),
            pltpu.SemaphoreType.DMA((4,)),
        ],
        compiler_params=params,
        cost_estimate=cost(4 << 20, 20 << 20),
        name="step",
    )(fields, weights, area, mask, land, pack, col_even, col_odd, north, south)


def solution(mesh):
    in_specs = (
        P(None, None, "lat", "lon"),
        P(None, "lat", "lon"),
        P("lat", "lon"),
        P("lat", "lon"),
        P("lat", "lon"),
    )
    body = functools.partial(local, mesh.shape["lon"], mesh.shape["lat"])
    return jax.shard_map(
        body, mesh=mesh, in_specs=in_specs, out_specs=P(None, None, "lat", "lon"), check_vma=False
    )
```

time: 160 us -> 48.5 us (0.30)
  the two profiles are of different devices: /device:TPU:6 before, /device:TPU:4 now
where the time goes in v1:
time: 48.5 us; the launch traced here: 48.2 us
  starting transfers between devices  20.3 us (42%)
  Pallas kernels  16.9 us (35%)
  waiting for transfers between devices  6.26 us (13%)
  local copies, waits for them, and re-layouts  3.99 us (8%)
  between operations  0.72 us (1%)
    pallas_call x1, Pallas kernels, local(): pl.pallas_call(step_kernel, out_shape=shape((6, 4, 128, 128), F32), in_sp...  16.1 us
    ppermute x1, starting transfers between devices, local(): col_odd = lax.ppermute(pack, axes, lon_pairs(nlon, nlat, True))  12 us
    ppermute x1, starting transfers between devices, local(): got_odd = lax.ppermute(to_odd, axes, lat_pairs(nlon, nlat, True))  4.44 us
    unnamed x10, local copies, waits for them, and re-layouts  3.99 us
    ppermute x1, waiting for transfers between devices, local(): col_even = lax.ppermute(pack, axes, lon_pairs(nlon, nlat, False))  3.93 us
    ppermute x1, waiting for transfers between devices, local(): got_odd = lax.ppermute(to_odd, axes, lat_pairs(nlon, nlat, True))  2.03 us
    ppermute x1, starting transfers between devices, local(): got_even = lax.ppermute(to_even, axes, lat_pairs(nlon, nlat, False))  1.92 us
    ppermute x1, starting transfers between devices, local(): col_even = lax.ppermute(pack, axes, lon_pairs(nlon, nlat, False))  1.92 us
  transfers between devices with their start and end apart: 4, of which 3 were waited for; matrix products, arithmetic and copies ran while one was open for 0% of the time, Pallas kernels for 1%

profile of v1, /device:TPU:4, one launch (start us, length us, event | category | flops | bytes accessed | tf_op | source)
XLA Modules:
  0.0 48.2 jit_solution(9697711947747318543)
XLA Ops:
  0.7 0.0 copy-start
  0.7 1.4 %copy-done = f32[6,4,128,128]{3,2,1,0:T(8,128)S(1)} copy-done((f32[6,4,128,128]{3,2,1,0:T(8,128)S(1)}, f32[6,4,128,128]{3,2,1,0:T(8,128)}, u32[]{:S(2)}) %copy-start) | copy-done | bytes 1572888
  2.1 0.0 copy-start.2
  2.1 0.9 %copy-done.2 = f32[2,128,128]{2,1,0:T(8,128)S(1)} copy-done((f32[2,128,128]{2,1,0:T(8,128)S(1)}, f32[2,128,128]{2,1,0:T(8,128)}, u32[]{:S(2)}) %copy-start.2) | copy-done | bytes 131096
  3.0 0.0 copy-start.3
  3.0 0.8 %copy-done.3 = f32[128,128]{1,0:T(8,128)S(1)} copy-done((f32[128,128]{1,0:T(8,128)S(1)}, f32[128,128]{1,0:T(8,128)}, u32[]{:S(2)}) %copy-start.3) | copy-done | bytes 65560
  3.8 0.0 copy-start.4
  3.8 0.8 %copy-done.4 = s32[128,128]{1,0:T(8,128)S(1)} copy-done((s32[128,128]{1,0:T(8,128)S(1)}, s32[128,128]{1,0:T(8,128)}, u32[]{:S(2)}) %copy-start.4) | copy-done | bytes 65560
  4.7 0.0 copy-start.1
  4.7 4.4 %collective-permute-start = (f32[56,128]{1,0:T(8,128)S(1)}, f32[56,128]{1,0:T(8,128)S(1)}, u32[]{:S(2)}, u32[]{:S(2)}) collective-permute-start(f32[56,128]{1,0:T(8,128)S(1)} %get-tuple-element.10.to_odd), channel_id=1, source_target_pairs={{1,2},{2,1},{3,4},{4,3},{5,6},{6,5},{7,8},{8,7},{9,10},{10,9},{11,... | collective-permute-start | bytes 86024 | tf_op jit(solution)/shard_map/lat_odd/ppermute | solution.py:341
  9.1 1.9 %collective-permute-start.1 = (f32[56,128]{1,0:T(8,128)S(1)}, f32[56,128]{1,0:T(8,128)S(1)}, u32[]{:S(2)}, u32[]{:S(2)}) collective-permute-start(f32[56,128]{1,0:T(8,128)S(1)} %get-tuple-element.11.to_even), channel_id=1, source_target_pairs={{0,1},{1,0},{2,3},{3,2},{4,5},{5,4},{6,7},{7,6},{8,9},{9,8},{10,11... | collective-permute-start | bytes 86024 | tf_op jit(solution)/shard_map/lat_even/ppermute | solution.py:343
  11.1 0.5 %columns.1.pack = f32[128,128]{1,0:T(8,128)S(1)} custom-call(f32[24,128,128]{2,1,0:T(8,128)S(1)} %bitcast.3, f32[2,128,128]{2,1,0:T(8,128)S(1)} %copy-done.2, f32[128,128]{1,0:T(8,128)S(1)} %copy-done.3, s32[128,128]{1,0:T(8,128)S(1)} %copy-done.4, s32[1,1]{1,0:T(1,128)S(6)} %copy.6.land), custom_call_target="tpu_custom_call" | custom-call | flops 1048576 | bytes 2097152 | tf_op jit(solution)/shard_map/columns/pallas_call | solution.py:346
  11.6 2.0 %collective-permute-done.got_odd = f32[56,128]{1,0:T(8,128)S(1)} collective-permute-done((f32[56,128]{1,0:T(8,128)S(1)}, f32[56,128]{1,0:T(8,128)S(1)}, u32[]{:S(2)}, u32[]{:S(2)}) %collective-permute-start) | collective-permute-done | bytes 28704 | tf_op jit(solution)/shard_map/lat_odd/ppermute | solution.py:341
  13.6 0.0 collective-permute-done.1.got_even
  13.6 0.3 strips.1
  14.0 12.0 %collective-permute-start.3 = (f32[128,128]{1,0:T(8,128)S(1)}, f32[128,128]{1,0:T(8,128)S(1)}, u32[]{:S(2)}, u32[]{:S(2)}) collective-permute-start(f32[128,128]{1,0:T(8,128)S(1)} %get-tuple-element.12.pack), channel_id=1, source_target_pairs={{0,496},{1,497},{2,498},{3,499},{4,500},{5,501},{6,502},{7,503},{8... | collective-permute-start | bytes 196616 | tf_op jit(solution)/shard_map/lon_odd/ppermute | solution.py:370
  26.0 1.9 %collective-permute-start.2 = (f32[128,128]{1,0:T(8,128)S(1)}, f32[128,128]{1,0:T(8,128)S(1)}, u32[]{:S(2)}, u32[]{:S(2)}) collective-permute-start(f32[128,128]{1,0:T(8,128)S(1)} %get-tuple-element.12.pack), channel_id=1, source_target_pairs={{0,16},{1,17},{2,18},{3,19},{4,20},{5,21},{6,22},{7,23},{8,24},{9,... | collective-permute-start | bytes 196616 | tf_op jit(solution)/shard_map/lon_even/ppermute | solution.py:368
  27.9 0.3 collective-permute-done.3.got_odd
  28.2 3.9 %collective-permute-done.2.got_even = f32[128,128]{1,0:T(8,128)S(1)} collective-permute-done((f32[128,128]{1,0:T(8,128)S(1)}, f32[128,128]{1,0:T(8,128)S(1)}, u32[]{:S(2)}, u32[]{:S(2)}) %collective-permute-start.2) | collective-permute-done | bytes 65568 | tf_op jit(solution)/shard_map/lon_even/ppermute | solution.py:368
  32.2 0.0 copy-done.1
  32.2 16.1 %step.1 = f32[6,4,128,128]{3,2,1,0:T(8,128)} custom-call(f32[6,4,128,128]{3,2,1,0:T(8,128)S(1)} %copy-done.1, f32[2,128,128]{2,1,0:T(8,128)S(1)} %copy-done.2, f32[128,128]{1,0:T(8,128)S(1)} %copy-done.3, s32[128,128]{1,0:T(8,128)S(1)} %copy-done.4, s32[1,1]{1,0:T(1,128)S(6)} %copy.6.land, f32[128,128]{1,0:T(8,128)S(1)} %get-tuple-element.12.pack, ...), custom_call_target="tpu_custom_call" | custom-call | flops 20971520 | bytes 4194304 | tf_op jit(solution)/shard_map/step/pallas_call | solution.py:373
  (1 shorter events, 0.0 us)
Async XLA Ops:
  0.7 1.4 %copy-start = (f32[6,4,128,128]{3,2,1,0:T(8,128)S(1)}, f32[6,4,128,128]{3,2,1,0:T(8,128)}, u32[]{:S(2)}) copy-start(f32[6,4,128,128]{3,2,1,0:T(8,128)} %f_hbm.1) | copy-start | bytes 4718596
  2.1 0.9 %copy-start.2 = (f32[2,128,128]{2,1,0:T(8,128)S(1)}, f32[2,128,128]{2,1,0:T(8,128)}, u32[]{:S(2)}) copy-start(f32[2,128,128]{2,1,0:T(8,128)} %w.3) | copy-start | bytes 393220
  3.0 0.8 %copy-start.3 = (f32[128,128]{1,0:T(8,128)S(1)}, f32[128,128]{1,0:T(8,128)}, u32[]{:S(2)}) copy-start(f32[128,128]{1,0:T(8,128)} %area.3) | copy-start | bytes 196612
  3.8 0.8 %copy-start.4 = (s32[128,128]{1,0:T(8,128)S(1)}, s32[128,128]{1,0:T(8,128)}, u32[]{:S(2)}) copy-start(s32[128,128]{1,0:T(8,128)} %mask.3) | copy-start | bytes 196612
  4.7 27.5 %copy-start.1 = (f32[6,4,128,128]{3,2,1,0:T(8,128)S(1)}, f32[6,4,128,128]{3,2,1,0:T(8,128)}, u32[]{:S(2)}) copy-start(f32[6,4,128,128]{3,2,1,0:T(8,128)} %f_hbm.1) | copy-start | bytes 4718596
  4.7 8.9 %collective-permute-start = (f32[56,128]{1,0:T(8,128)S(1)}, f32[56,128]{1,0:T(8,128)S(1)}, u32[]{:S(2)}, u32[]{:S(2)}) collective-permute-start(f32[56,128]{1,0:T(8,128)S(1)} %get-tuple-element.10.to_odd), channel_id=1, source_target_pairs={{1,2},{2,1},{3,4},{4,3},{5,6},{6,5},{7,8},{8,7},{9,10},{10,9},{11,... | collective-permute-start | bytes 86024 | tf_op jit(solution)/shard_map/lat_odd/ppermute | solution.py:341
  9.1 4.5 %collective-permute-start.1 = (f32[56,128]{1,0:T(8,128)S(1)}, f32[56,128]{1,0:T(8,128)S(1)}, u32[]{:S(2)}, u32[]{:S(2)}) collective-permute-start(f32[56,128]{1,0:T(8,128)S(1)} %get-tuple-element.11.to_even), channel_id=1, source_target_pairs={{0,1},{1,0},{2,3},{3,2},{4,5},{5,4},{6,7},{7,6},{8,9},{9,8},{10,11... | collective-permute-start | bytes 86024 | tf_op jit(solution)/shard_map/lat_even/ppermute | solution.py:343
  14.0 14.3 %collective-permute-start.3 = (f32[128,128]{1,0:T(8,128)S(1)}, f32[128,128]{1,0:T(8,128)S(1)}, u32[]{:S(2)}, u32[]{:S(2)}) collective-permute-start(f32[128,128]{1,0:T(8,128)S(1)} %get-tuple-element.12.pack), channel_id=1, source_target_pairs={{0,496},{1,497},{2,498},{3,499},{4,500},{5,501},{6,502},{7,503},{8... | collective-permute-start | bytes 196616 | tf_op jit(solution)/shard_map/lon_odd/ppermute | solution.py:370
  26.0 6.2 %collective-permute-start.2 = (f32[128,128]{1,0:T(8,128)S(1)}, f32[128,128]{1,0:T(8,128)S(1)}, u32[]{:S(2)}, u32[]{:S(2)}) collective-permute-start(f32[128,128]{1,0:T(8,128)S(1)} %get-tuple-element.12.pack), channel_id=1, source_target_pairs={{0,16},{1,17},{2,18},{3,19},{4,20},{5,21},{6,22},{7,23},{8,24},{9,... | collective-permute-start | bytes 196616 | tf_op jit(solution)/shard_map/lon_even/ppermute | solution.py:368

commit v2 on v1

v2 whole, which is shorter than its diff:
```python
import functools

import jax
import jax.numpy as jnp
import numpy as np
from jax import lax
from jax.experimental import pallas as pl
from jax.experimental.pallas import tpu as pltpu
from jax.sharding import PartitionSpec as P

F32 = jnp.float32
TIME_STEP = 0.1
NP = 24
GE, GN, GM, GS = 24, 25, 26, 27
ROWS2, ROWS4 = 56, 112
PAD = 8
CHUNK = 32
HIGH = lax.Precision.HIGHEST


def lon_pairs(nlon, nlat, odd):
    def other(i):
        if not odd:
            return i ^ 1
        return (i + 1) % nlon if i % 2 else (i - 1) % nlon

    return [(i * nlat + l, other(i) * nlat + l) for i in range(nlon) for l in range(nlat)]


def lat_pairs(nlon, nlat, odd):
    pairs = []
    for i in range(nlon):
        for l in range(nlat):
            if not odd:
                pairs.append((i * nlat + l, i * nlat + (l ^ 1)))
            elif l == nlat - 1:
                pairs.append((i * nlat + l, (nlon - 1 - i) * nlat + l))
            elif l > 0:
                pairs.append((i * nlat + l, i * nlat + (l + 1 if l % 2 else l - 1)))
    return pairs


def lanes(shape):
    return lax.broadcasted_iota(jnp.int32, shape, 1)


def rows_of(shape):
    return lax.broadcasted_iota(jnp.int32, shape, 0)


def roll(x, shift, axis):
    n = x.shape[axis]
    shift %= n
    return x if shift == 0 else pltpu.roll(x, shift, axis)


def step_factor(area, mask, land):
    sea = mask.astype(F32) * (1 - land).astype(F32)
    return TIME_STEP * sea * area


def coefs(se, sw, sn, ss, me, mw, mn, ms, base):
    te, tw, tn, ts = me * (0.125 * se), mw * (0.125 * sw), mn * (0.125 * sn), ms * (0.125 * ss)
    return me - te, mw + tw, mn - tn, ms + ts, base + ((tw - te) + (ts - tn))


def apply(c, x, xe, xw, xn, xs):
    ce, cw, cn, cs, cc = c
    return cc * x + ((ce * xe + cw * xw) + (cn * xn + cs * xs))


def rows_kernel(f, w, area, mask, land, to_odd, to_even, fb, wb, ab, kb, sem):
    copies = []
    for n, (src, dst) in enumerate(((f, fb), (w, wb), (area, ab), (mask, kb))):
        for h in range(2):
            rows = pl.ds(120 * h, 8)
            part = src.at[:, rows] if len(src.shape) == 3 else src.at[rows]
            copies.append(pltpu.make_async_copy(part, dst.at[h], sem.at[2 * n + h]))
    for c in copies:
        c.start()
    odd = lax.axis_index("lat") % 2 == 1
    for c in copies:
        c.wait()
    m_lo = step_factor(ab[0, 0:2], kb[0, 0:2], land[0, 0])
    m_hi = step_factor(ab[1, 6:8], kb[1, 6:8], land[0, 0])
    zero = jnp.zeros((2, 128), F32)
    for g in range(28):
        if g < NP:
            south, north = fb[0, g, 0:2], fb[1, g, 6:8]
        elif g < GM:
            south, north = wb[0, g - NP, 0:2], wb[1, g - NP, 6:8]
        elif g == GM:
            south, north = m_lo, m_hi
        else:
            south, north = zero, zero
        to_odd[2 * g : 2 * g + 2] = jnp.where(odd, north, south)
        to_even[2 * g : 2 * g + 2] = jnp.where(odd, south, north)


def columns_kernel(f, w, area, mask, land, out):
    for r in range(0, 128, CHUNK):
        rr = slice(r, r + CHUNK)
        group = lanes((CHUNK, 128)) // 4
        acc = jnp.zeros((CHUNK, 128), F32)
        for g in range(28):
            if g < NP:
                x = f[g, rr]
            elif g < GM:
                x = w[g - NP, rr]
            elif g == GM:
                x = step_factor(area[rr], mask[rr], land[0, 0])
            else:
                x = w[0, rr]
            acc = jnp.where(group == g, roll(x, 4 * g + 2 + (g == GS), 1), acc)
        out[rr] = acc


def strips_kernel(to_odd, to_even, got_odd, got_even, pack, out, north, south, recv):
    odd = lax.axis_index("lat") % 2 == 1
    top = lax.axis_index("lat") == lax.axis_size("lat") - 1
    raw = jnp.where(odd, got_odd[...], got_even[...])
    row = rows_of((ROWS2, 128))
    flip = (rows_of((128, 128)) + lanes((128, 128)) == 127).astype(F32)
    mirrored = jnp.dot(raw, flip, precision=HIGH, preferred_element_type=F32)
    mirrored = jnp.where((row >= 32) & (row < 48), -mirrored, mirrored)
    mirrored = jnp.where(row % 2 == 0, roll(mirrored, -1, 0), roll(mirrored, 1, 0))
    recv[0] = jnp.where(top, mirrored, raw)
    recv[1] = jnp.where(odd, got_even[...], got_odd[...])
    recv[2] = jnp.where(odd, to_odd[...], to_even[...])
    recv[3] = jnp.where(odd, to_even[...], to_odd[...])
    for g in range(28):
        two = slice(2 * g, 2 * g + 2)
        north[4 * g : 4 * g + 2] = recv[2, two]
        north[4 * g + 2 : 4 * g + 4] = recv[0, two]
        south[4 * g : 4 * g + 2] = recv[1, two]
        south[4 * g + 2 : 4 * g + 4] = recv[3, two]
    a, b = recv[0, 2 * GN : 2 * GN + 1], recv[0, 2 * GN + 1 : 2 * GN + 2]
    north[4 * GN + 2 : 4 * GN + 3] = jnp.where(top, b, a)
    north[4 * GS + 2 : 4 * GS + 3] = jnp.where(top, a, recv[2, 2 * GN + 1 : 2 * GN + 2])
    south[4 * GS + 1 : 4 * GS + 2] = recv[1, 2 * GN : 2 * GN + 1]
    lane = lanes((ROWS4, 128))
    acc = jnp.where(lane // 4 == 28, roll(north[...], 114, 1), pack[0:ROWS4])
    out[0:ROWS4] = jnp.where(lane // 4 == 29, roll(south[...], 118, 1), acc)
    out[ROWS4:128] = pack[ROWS4:128]


def repeat_half(v, half):
    low = rows_of(v.shape) < 4
    other = roll(v, 4, 0)
    return jnp.where(low, v, other) if half == 0 else jnp.where(low, other, v)


def lat_strip(strip, ends, shift_w, shift_e, top):
    lane = lanes((8, 128))

    def tile(t):
        x = strip[8 * t : 8 * t + 8]
        xe, xw = roll(x, -1, 1), roll(x, 1, 1)
        if ends is not None:
            w = roll(ends[0][8 * t : 8 * t + 8], shift_w, 1)
            e = roll(ends[1][8 * t : 8 * t + 8], shift_e, 1)
            xe, xw = jnp.where(lane == 127, e, xe), jnp.where(lane == 0, w, xw)
        return x, xe, xw

    x12, e12, w12 = tile(12)
    x13 = strip[104:112]
    here, right, left = (repeat_half(a, 0) for a in (x12, e12, w12))
    we = here if top is None else jnp.where(top, right, here)
    ww = left if top is None else jnp.where(top, here, left)
    m = repeat_half(x13, 0)
    me, mw = m * we, m * ww
    mn, ms = m * repeat_half(x12, 1), m * repeat_half(x13, 1)
    base = 1.0 - ((me + mw) + (mn + ms))
    c = []
    for t in range(2):
        u, ue, uw = tile(8 + t)
        v = strip[8 * (10 + t) : 8 * (10 + t) + 8]
        c.append(coefs(u + ue, u + uw, v + roll(v, -1, 0), v + roll(v, 1, 0), me, mw, mn, ms, base))
    out = []
    for t in range(12):
        x, xe, xw = tile(t)
        out.append(apply(c[t % 2], x, xe, xw, roll(x, -1, 0), roll(x, 1, 0)))
    return out


def inner_kernel(fields, w, area, mask, land, north, south, res, ends, mid, halo, mw5):
    top = lax.axis_index("lat") == lax.axis_size("lat") - 1
    for s, tiles in enumerate(
        (lat_strip(south, None, 0, 0, None), lat_strip(north, None, 0, 0, top))
    ):
        for t in range(12):
            halo[s, 8 * t : 8 * t + 8] = tiles[t]

    m = step_factor(area[...], mask[...], land[0, 0])
    we, wn = w[0], w[1]
    first = rows_of((128, 128)) == 0
    ws = jnp.where(first, south[4 * GN + 1 : 4 * GN + 2], roll(wn, 1, 0))
    me, mw, mn, ms = m * we, m * roll(we, 1, 1), m * wn, m * ws
    for n, x in enumerate((me, mw, mn, ms, 1.0 - ((me + mw) + (mn + ms)))):
        mw5[n] = x
    ends[...] = jnp.zeros((128, 128), F32)

    lane = lanes((CHUNK, 128))
    row = rows_of((CHUNK, 128))
    for k in range(4):

        def first_get(f, r):
            g = 4 * f + k
            x = fields[f, k, r : r + CHUNK]
            if r == 0:
                s = jnp.where(row == 0, south[4 * g + 1 : 4 * g + 2], roll(x, 1, 0))
            else:
                s = fields[f, k, r - 1 : r - 1 + CHUNK]
            if r == 128 - CHUNK:
                n = jnp.where(row == CHUNK - 1, north[4 * g + 2 : 4 * g + 3], roll(x, -1, 0))
            else:
                n = fields[f, k, r + 1 : r + 1 + CHUNK]
            return x, n, s

        def second_get(f, r):
            return tuple(mid[f, PAD + r + d : PAD + r + d + CHUNK] for d in (0, 1, -1))

        for f in range(6):
            g = 4 * f + k
            mid[f, PAD - 1 : PAD] = halo[0, 4 * g + 1 : 4 * g + 2]
            mid[f, PAD + 128 : PAD + 129] = halo[1, 4 * g + 2 : 4 * g + 3]
        for substep, get in enumerate((first_get, second_get)):
            for r in range(0, 128, CHUNK):
                rr = slice(r, r + CHUNK)
                u = get(4, r)[0]
                v, vn, vs = get(5, r)
                c = coefs(u + roll(u, -1, 1), u + roll(u, 1, 1), v + vn, v + vs,
                          *(mw5[n, rr] for n in range(5)))
                acc = ends[rr]
                for f in range(6):
                    g = 4 * f + k
                    x, xn, xs = get(f, r)
                    xe, xw = roll(x, -1, 1), roll(x, 1, 1)
                    y = apply(c, x, xe, xw, xn, xs)
                    if substep == 0:
                        mid[f, PAD + r : PAD + r + CHUNK] = y
                    else:
                        res[f, k, rr] = y
                        beside = jnp.where(lane < 64, xe, xw)
                        acc = jnp.where(lane // 4 == g, roll(beside, 4 * g + 2, 1), acc)
                if substep == 1:
                    ends[rr] = acc


def spread_matrix():
    out = np.zeros((7, 128, 128), np.float32)
    for l in range(128):
        k, j = l // 4 % 4, l % 4
        u, v = 64 + 4 * k + j, 80 + 4 * k + j
        for n, src in enumerate((
            (u, u + 1), (u, u - 1), (v,), (4 * GE + j,),
            (4 * GS if j == 0 else 4 * GE + j - 1,), (4 * GN + j,), (4 * GM + j,),
        )):
            for i in src:
                out[n, i, l] = 1.0
    return np.concatenate(list(out), axis=1)


def spread(x, matrix):
    hi = x.astype(jnp.bfloat16)
    rest = x - hi.astype(F32)
    mid = rest.astype(jnp.bfloat16)
    lo = (rest - mid.astype(F32)).astype(jnp.bfloat16)
    dot = functools.partial(jnp.dot, preferred_element_type=F32)
    return dot(lo, matrix) + dot(mid, matrix) + dot(hi, matrix)


def outer_kernel(pack, got_even, got_odd, north, south, inner, ends, matrix, out_hbm,
                 side, wide, halo, z, res, sem):
    odd = lax.axis_index("lon") % 2 == 1
    top = lax.axis_index("lat") == lax.axis_size("lat") - 1
    west = jnp.where(odd, got_even[...], got_odd[...])
    east = jnp.where(odd, got_odd[...], got_even[...])
    own = pack[...]
    lane = lanes((128, 128))
    j = lane % 4
    span = 128 + 2 * PAD

    def fill(s, strip, above, below):
        side[s, PAD : PAD + 128] = strip
        side[s, 0:PAD] = jnp.broadcast_to(below, (PAD, 128))
        side[s, PAD + 128 : span] = jnp.broadcast_to(above, (PAD, 128))

    def widen(n):
        for s in range(2):
            wide[s, :, 0 : 128 * n] = spread(side[s], matrix[:, 0 : 128 * n])

    def update(s, r):
        def rep(n, d=0):
            return wide[s, PAD + r + d : PAD + r + d + CHUNK, 128 * n : 128 * n + 128]

        def at(d):
            return side[s, PAD + r + d : PAD + r + d + CHUNK]

        m, v, x = rep(6), rep(2), at(0)
        me, mw, mn, ms = m * rep(3), m * rep(4), m * rep(5), m * rep(5, -1)
        base = 1.0 - ((me + mw) + (mn + ms))
        c = coefs(rep(0), rep(1), v + rep(2, 1), v + rep(2, -1), me, mw, mn, ms, base)
        return apply(c, x, roll(x, -1, 1), roll(x, 1, 1), at(1), at(-1))

    j1 = lanes((1, 128)) % 4

    def as_row(turned, columns, shift):
        parts = [roll(turned[c : c + 1], shift + d, 1) for c, d in zip(columns, (-2, -1, 0, 1))]
        low = jnp.where(j1 == 0, parts[0], parts[1])
        return jnp.where(j1 < 2, low, jnp.where(j1 == 2, parts[2], parts[3]))

    three = jnp.where(lane < 112, roll(own, -8, 1), jnp.where(lane < 120, west, roll(east, 8, 1)))
    turned = three.T
    above, below = as_row(turned, range(104, 108), 0), as_row(turned, range(108, 112), 1)
    fill(0, jnp.where(j < 2, west, own),
         jnp.where(j1 == 1, roll(turned[113:114], -1, 1), above),
         jnp.where(j1 == 1, turned[117:118], below))
    fill(1, jnp.where(j < 2, own, east),
         jnp.where(j1 == 2, turned[122:123], above),
         jnp.where(j1 == 2, roll(turned[126:127], 1, 1), below))
    widen(7)

    packs = (west, east)
    low = lat_strip(south, packs, 11, 9, None)
    high = lat_strip(north, packs, 15, 13, top)
    ring = rows_of((8, 128)) % 4 == 2
    for t in range(12):
        halo[8 * t : 8 * t + 8] = jnp.where(ring, high[t], low[t])
    halo[96:128] = jnp.zeros((32, 128), F32)
    turned = halo[...].T
    outer = (126, 127, 0, 1)
    above, below = as_row(turned, outer, 0), as_row(turned, outer, 1)

    new = [[update(s, r) for r in range(0, 128, CHUNK)] for s in range(2)]
    edge = (j == 0) | (j == 3)
    for s in range(2):
        strip = jnp.where(edge, roll(ends[...], 1 - 2 * s, 1), jnp.concatenate(new[s], axis=0))
        fill(s, strip, above, below)
    widen(3)
    jj = lanes((CHUNK, 128)) % 4
    for r in range(0, 128, CHUNK):
        z[r : r + CHUNK] = jnp.where(jj < 2, update(1, r), update(0, r))

    outs = []
    outer = (lanes((CHUNK, 128)) < 2) | (lanes((CHUNK, 128)) >= 126)
    for k in range(4):
        for r in range(0, 128, CHUNK):
            rr = slice(r, r + CHUNK)
            zr = z[rr]
            for f in range(6):
                res[f, k, rr] = jnp.where(outer, roll(zr, -(4 * (4 * f + k) + 2), 1), inner[f, k, rr])
        c = pltpu.make_async_copy(res.at[:, k], out_hbm.at[:, k], sem.at[k])
        c.start()
        outs.append(c)
    for c in outs:
        c.wait()


def cost(nbytes, flops):
    return pl.CostEstimate(flops=flops, bytes_accessed=nbytes, transcendentals=0)


def vmem():
    return pl.BlockSpec(memory_space=pltpu.VMEM)


def smem():
    return pl.BlockSpec(memory_space=pltpu.SMEM)


def local(nlon, nlat, fields, weights, area, mask, land):
    shape = jax.ShapeDtypeStruct
    planes = fields.reshape(NP, 128, 128)
    params = pltpu.CompilerParams(vmem_limit_bytes=24 << 20)

    rows = shape((ROWS2, 128), F32)
    to_odd, to_even = pl.pallas_call(
        rows_kernel,
        out_shape=(rows, rows),
        in_specs=[pl.BlockSpec(memory_space=pltpu.HBM)] * 4 + [smem()],
        out_specs=(vmem(), vmem()),
        scratch_shapes=[
            pltpu.VMEM((2, NP, 8, 128), F32),
            pltpu.VMEM((2, 2, 8, 128), F32),
            pltpu.VMEM((2, 8, 128), F32),
            pltpu.VMEM((2, 8, 128), jnp.int32),
            pltpu.SemaphoreType.DMA((8,)),
        ],
        cost_estimate=cost(1 << 18, 1 << 16),
        name="rows",
    )(planes, weights, area, mask, land)

    axes = ("lon", "lat")
    with jax.named_scope("lat_odd"):
        got_odd = lax.ppermute(to_odd, axes, lat_pairs(nlon, nlat, True))
    with jax.named_scope("lat_even"):
        got_even = lax.ppermute(to_even, axes, lat_pairs(nlon, nlat, False))

    tile = shape((128, 128), F32)
    pack = pl.pallas_call(
        columns_kernel,
        out_shape=tile,
        in_specs=[vmem()] * 4 + [smem()],
        out_specs=vmem(),
        compiler_params=params,
        cost_estimate=cost(2 << 20, 1 << 20),
        name="columns",
    )(planes, weights, area, mask, land)

    pack, north, south = pl.pallas_call(
        strips_kernel,
        out_shape=(tile, shape((ROWS4, 128), F32), shape((ROWS4, 128), F32)),
        in_specs=[vmem()] * 5,
        out_specs=(vmem(),) * 3,
        scratch_shapes=[pltpu.VMEM((4, ROWS2, 128), F32)],
        compiler_params=params,
        cost_estimate=cost(1 << 18, 1 << 18),
        name="strips",
    )(to_odd, to_even, got_odd, got_even, pack)

    with jax.named_scope("lon_even"):
        col_even = lax.ppermute(pack, axes, lon_pairs(nlon, nlat, False))
    with jax.named_scope("lon_odd"):
        col_odd = lax.ppermute(pack, axes, lon_pairs(nlon, nlat, True))

    padded = 128 + 2 * PAD
    state = shape((6, 4, 128, 128), F32)
    inner, ends = pl.pallas_call(
        inner_kernel,
        out_shape=(state, tile),
        in_specs=[vmem()] * 4 + [smem()] + [vmem()] * 2,
        out_specs=(vmem(), vmem()),
        scratch_shapes=[
            pltpu.VMEM((6, padded, 128), F32),
            pltpu.VMEM((2, 96, 128), F32),
            pltpu.VMEM((5, 128, 128), F32),
        ],
        compiler_params=params,
        cost_estimate=cost(4 << 20, 20 << 20),
        name="inner",
    )(fields, weights, area, mask, land, north, south)

    return pl.pallas_call(
        outer_kernel,
        out_shape=state,
        in_specs=[vmem()] * 8,
        out_specs=pl.BlockSpec(memory_space=pltpu.HBM),
        scratch_shapes=[
            pltpu.VMEM((2, padded, 128), F32),
            pltpu.VMEM((2, padded, 7 * 128), F32),
            pltpu.VMEM((128, 128), F32),
            pltpu.VMEM((128, 128), F32),
            pltpu.VMEM((6, 4, 128, 128), F32),
            pltpu.SemaphoreType.DMA((4,)),
        ],
        compiler_params=params,
        cost_estimate=cost(4 << 20, 1 << 20),
        name="outer",
    )(pack, col_even, col_odd, north, south, inner, ends, jnp.asarray(spread_matrix(), jnp.bfloat16))


def solution(mesh):
    in_specs = (
        P(None, None, "lat", "lon"),
        P(None, "lat", "lon"),
        P("lat", "lon"),
        P("lat", "lon"),
        P("lat", "lon"),
    )
    body = functools.partial(local, mesh.shape["lon"], mesh.shape["lat"])
    return jax.shard_map(
        body, mesh=mesh, in_specs=in_specs, out_specs=P(None, None, "lat", "lon"), check_vma=False
    )
```

time: 48.5 us -> 37.5 us (0.77)
  the two profiles are of different devices: /device:TPU:4 before, /device:TPU:36 now
where the time goes in v2:
time: 37.5 us; the launch traced here: 37.2 us
  starting transfers between devices  20.5 us (55%)
  Pallas kernels  13.7 us (37%)
  waiting for transfers between devices  2.05 us (5%)
  between operations  0.93 us (2%)
    ppermute x1, starting transfers between devices, local(): col_even = lax.ppermute(pack, axes, lon_pairs(nlon, nlat, False))  10.2 us
    pallas_call x1, Pallas kernels, local(): pl.pallas_call(inner_kernel, out_shape=(state, tile), in_specs=[vmem()] *...  8.32 us
    ppermute x1, starting transfers between devices, local(): got_odd = lax.ppermute(to_odd, axes, lat_pairs(nlon, nlat, True))  4.44 us
    ppermute x1, starting transfers between devices, local(): col_odd = lax.ppermute(pack, axes, lon_pairs(nlon, nlat, True))  3.83 us
    pallas_call x1, Pallas kernels, local(): pl.pallas_call(outer_kernel, out_shape=state, in_specs=[vmem()] * 8, out_...  2.81 us
    ppermute x1, starting transfers between devices, local(): got_even = lax.ppermute(to_even, axes, lat_pairs(nlon, nlat, False))  2.05 us
    ppermute x1, waiting for transfers between devices, local(): got_odd = lax.ppermute(to_odd, axes, lat_pairs(nlon, nlat, True))  2.04 us
    pallas_call x1, Pallas kernels, local(): pl.pallas_call(rows_kernel, out_shape=(rows, rows), in_specs=[pl.BlockSpe...  1.66 us
  transfers between devices with their start and end apart: 4, of which 1 were waited for; matrix products, arithmetic and copies ran while one was open for 0% of the time, Pallas kernels for 24%

profile of v2, /device:TPU:36, one launch (start us, length us, event | category | flops | bytes accessed | tf_op | source)
XLA Modules:
  0.0 37.2 jit_solution(8379421859604265504)
XLA Ops:
  0.0 0.0 copy-start.3
  0.0 0.0 copy-start.2
  0.0 0.0 copy-start.1
  0.0 0.0 copy-start
  0.8 1.7 %rows.1 = (f32[56,128]{1,0:T(8,128)}, f32[56,128]{1,0:T(8,128)}) custom-call(f32[24,128,128]{2,1,0:T(8,128)} %bitcast.1, f32[2,128,128]{2,1,0:T(8,128)} %w.5, f32[128,128]{1,0:T(8,128)} %area.5, s32[128,128]{1,0:T(8,128)} %mask.5, s32[1,1]{1,0:T(1,128)S(6)} %copy.7.land), custom_call_target="tpu_custom_call" | custom-call | flops 65536 | bytes 262144 | tf_op jit(solution)/shard_map/rows/pallas_call | solution.py:378
  2.5 0.0 copy-start.5
  2.5 0.0 copy-start.6
  2.5 4.4 %collective-permute-start = (f32[56,128]{1,0:T(8,128)}, f32[56,128]{1,0:T(8,128)S(1)}, u32[]{:S(2)}, u32[]{:S(2)}) collective-permute-start(f32[56,128]{1,0:T(8,128)} %get-tuple-element.12.to_odd), channel_id=1, source_target_pairs={{1,2},{2,1},{3,4},{4,3},{5,6},{6,5},{7,8},{8,7},{9,10},{10,9},{11,... | collective-permute-start | bytes 86024 | tf_op jit(solution)/shard_map/lat_odd/ppermute | solution.py:396
  6.9 0.0 copy-start.4
  6.9 2.1 %collective-permute-start.1 = (f32[56,128]{1,0:T(8,128)}, f32[56,128]{1,0:T(8,128)S(1)}, u32[]{:S(2)}, u32[]{:S(2)}) collective-permute-start(f32[56,128]{1,0:T(8,128)} %get-tuple-element.13.to_even), channel_id=1, source_target_pairs={{0,1},{1,0},{2,3},{3,2},{4,5},{5,4},{6,7},{7,6},{8,9},{9,8},{10,11... | collective-permute-start | bytes 86024 | tf_op jit(solution)/shard_map/lat_even/ppermute | solution.py:398
  9.0 0.0 copy-done.3
  9.0 0.0 copy-done.2
  9.0 0.0 copy-done.1
  9.0 0.0 copy-done
  9.0 0.5 %columns.1.pack = f32[128,128]{1,0:T(8,128)S(1)} custom-call(f32[24,128,128]{2,1,0:T(8,128)S(1)} %bitcast.2, f32[2,128,128]{2,1,0:T(8,128)S(1)} %copy-done.1, f32[128,128]{1,0:T(8,128)S(1)} %copy-done.2, s32[128,128]{1,0:T(8,128)S(1)} %copy-done.3, s32[1,1]{1,0:T(1,128)S(6)} %copy.7.land), custom_call_target="tpu_custom_call" | custom-call | flops 1048576 | bytes 2097152 | tf_op jit(solution)/shard_map/columns/pallas_call | solution.py:401
  9.6 2.0 %collective-permute-done.got_odd = f32[56,128]{1,0:T(8,128)S(1)} collective-permute-done((f32[56,128]{1,0:T(8,128)}, f32[56,128]{1,0:T(8,128)S(1)}, u32[]{:S(2)}, u32[]{:S(2)}) %collective-permute-start) | collective-permute-done | bytes 28704 | tf_op jit(solution)/shard_map/lat_odd/ppermute | solution.py:396
  11.6 0.0 collective-permute-done.1.got_even
  11.6 0.0 copy-done.5
  11.6 0.0 copy-done.6
  11.6 0.3 strips.1
  12.0 3.8 %collective-permute-start.3 = (f32[128,128]{1,0:T(8,128)S(1)}, f32[128,128]{1,0:T(8,128)S(1)}, u32[]{:S(2)}, u32[]{:S(2)}) collective-permute-start(f32[128,128]{1,0:T(8,128)S(1)} %get-tuple-element.14.pack), channel_id=1, source_target_pairs={{0,496},{1,497},{2,498},{3,499},{4,500},{5,501},{6,502},{7,503},{8... | collective-permute-start | bytes 196616 | tf_op jit(solution)/shard_map/lon_odd/ppermute | solution.py:425
  15.8 10.2 %collective-permute-start.2 = (f32[128,128]{1,0:T(8,128)S(1)}, f32[128,128]{1,0:T(8,128)S(1)}, u32[]{:S(2)}, u32[]{:S(2)}) collective-permute-start(f32[128,128]{1,0:T(8,128)S(1)} %get-tuple-element.14.pack), channel_id=1, source_target_pairs={{0,16},{1,17},{2,18},{3,19},{4,20},{5,21},{6,22},{7,23},{8,24},{9,... | collective-permute-start | bytes 196616 | tf_op jit(solution)/shard_map/lon_even/ppermute | solution.py:423
  26.0 8.3 %inner.1 = (f32[6,4,128,128]{3,2,1,0:T(8,128)S(1)}, f32[128,128]{1,0:T(8,128)S(1)}) custom-call(f32[6,4,128,128]{3,2,1,0:T(8,128)S(1)} %copy-done, f32[2,128,128]{2,1,0:T(8,128)S(1)} %copy-done.1, f32[128,128]{1,0:T(8,128)S(1)} %copy-done.2, s32[128,128]{1,0:T(8,128)S(1)} %copy-done.3, s32[1,1]{1,0:T(1,128)S(6)} %copy.7.land, ...), custom_call_target="tpu_custom_call" | custom-call | flops 20971520 | bytes 4194304 | tf_op jit(solution)/shard_map/inner/pallas_call | solution.py:429
  34.4 0.0 collective-permute-done.3.got_odd
  34.4 0.0 collective-permute-done.2.got_even
  34.4 0.0 copy-done.4
  34.4 2.8 %outer.1 = f32[6,4,128,128]{3,2,1,0:T(8,128)} custom-call(f32[128,128]{1,0:T(8,128)S(1)} %get-tuple-element.14.pack, f32[128,128]{1,0:T(8,128)S(1)} %collective-permute-done.2.got_even, f32[128,128]{1,0:T(8,128)S(1)} %collective-permute-done.3.got_odd, f32[112,128]{1,0:T(8,128)S(1)} %get-tuple-element.15.north, f32[112,128]{1,0:T(8,128)S(1)} %get-tuple-element.16.south, ...), custom_call_target="tpu_custom_call" | custom-call | flops 1048576 | bytes 4194304 | tf_op jit(solution)/shard_map/outer/pallas_call | solution.py:444
Async XLA Ops:
  0.0 9.0 %copy-start.3 = (s32[128,128]{1,0:T(8,128)S(1)}, s32[128,128]{1,0:T(8,128)}, u32[]{:S(2)}) copy-start(s32[128,128]{1,0:T(8,128)} %mask.5) | copy-start | bytes 196612
  0.0 9.0 %copy-start.2 = (f32[128,128]{1,0:T(8,128)S(1)}, f32[128,128]{1,0:T(8,128)}, u32[]{:S(2)}) copy-start(f32[128,128]{1,0:T(8,128)} %area.5) | copy-start | bytes 196612
  0.0 9.0 %copy-start.1 = (f32[2,128,128]{2,1,0:T(8,128)S(1)}, f32[2,128,128]{2,1,0:T(8,128)}, u32[]{:S(2)}) copy-start(f32[2,128,128]{2,1,0:T(8,128)} %w.5) | copy-start | bytes 393220
  0.0 9.0 %copy-start = (f32[6,4,128,128]{3,2,1,0:T(8,128)S(1)}, f32[6,4,128,128]{3,2,1,0:T(8,128)}, u32[]{:S(2)}) copy-start(f32[6,4,128,128]{3,2,1,0:T(8,128)} %fields.1) | copy-start | bytes 4718596
  2.5 9.2 %copy-start.5 = (f32[56,128]{1,0:T(8,128)S(1)}, f32[56,128]{1,0:T(8,128)}, u32[]{:S(2)}) copy-start(f32[56,128]{1,0:T(8,128)} %get-tuple-element.12.to_odd) | copy-start | bytes 86020
  2.5 9.2 %copy-start.6 = (f32[56,128]{1,0:T(8,128)S(1)}, f32[56,128]{1,0:T(8,128)}, u32[]{:S(2)}) copy-start(f32[56,128]{1,0:T(8,128)} %get-tuple-element.13.to_even) | copy-start | bytes 86020
  2.5 9.1 %collective-permute-start = (f32[56,128]{1,0:T(8,128)}, f32[56,128]{1,0:T(8,128)S(1)}, u32[]{:S(2)}, u32[]{:S(2)}) collective-permute-start(f32[56,128]{1,0:T(8,128)} %get-tuple-element.12.to_odd), channel_id=1, source_target_pairs={{1,2},{2,1},{3,4},{4,3},{5,6},{6,5},{7,8},{8,7},{9,10},{10,9},{11,... | collective-permute-start | bytes 86024 | tf_op jit(solution)/shard_map/lat_odd/ppermute | solution.py:396
  6.9 27.4 %copy-start.4 = (bf16[128,896]{1,0:T(8,128)(2,1)S(1)}, bf16[128,896]{1,0:T(8,128)(2,1)}, u32[]{:S(2)}) copy-start(bf16[128,896]{1,0:T(8,128)(2,1)} %constant.2.clone.matrix) | copy-start | bytes 688132
  6.9 4.7 %collective-permute-start.1 = (f32[56,128]{1,0:T(8,128)}, f32[56,128]{1,0:T(8,128)S(1)}, u32[]{:S(2)}, u32[]{:S(2)}) collective-permute-start(f32[56,128]{1,0:T(8,128)} %get-tuple-element.13.to_even), channel_id=1, source_target_pairs={{0,1},{1,0},{2,3},{3,2},{4,5},{5,4},{6,7},{7,6},{8,9},{9,8},{10,11... | collective-permute-start | bytes 86024 | tf_op jit(solution)/shard_map/lat_even/ppermute | solution.py:398
  12.0 22.4 %collective-permute-start.3 = (f32[128,128]{1,0:T(8,128)S(1)}, f32[128,128]{1,0:T(8,128)S(1)}, u32[]{:S(2)}, u32[]{:S(2)}) collective-permute-start(f32[128,128]{1,0:T(8,128)S(1)} %get-tuple-element.14.pack), channel_id=1, source_target_pairs={{0,496},{1,497},{2,498},{3,499},{4,500},{5,501},{6,502},{7,503},{8... | collective-permute-start | bytes 196616 | tf_op jit(solution)/shard_map/lon_odd/ppermute | solution.py:425
  15.8 18.6 %collective-permute-start.2 = (f32[128,128]{1,0:T(8,128)S(1)}, f32[128,128]{1,0:T(8,128)S(1)}, u32[]{:S(2)}, u32[]{:S(2)}) collective-permute-start(f32[128,128]{1,0:T(8,128)S(1)} %get-tuple-element.14.pack), channel_id=1, source_target_pairs={{0,16},{1,17},{2,18},{3,19},{4,20},{5,21},{6,22},{7,23},{8,24},{9,... | collective-permute-start | bytes 196616 | tf_op jit(solution)/shard_map/lon_even/ppermute | solution.py:423

commit v3 on v2

--- a/solution.py
+++ b/solution.py
@@ -54,9 +54,8 @@
     return x if shift == 0 else pltpu.roll(x, shift, axis)
 
 
-def step_factor(area, mask, land):
-    sea = mask.astype(F32) * (1 - land).astype(F32)
-    return TIME_STEP * sea * area
+def step_factor(area, mask, sea):
+    return TIME_STEP * (mask.astype(F32) * sea) * area
 
 
 def coefs(se, sw, sn, ss, me, mw, mn, ms, base):
@@ -69,7 +68,7 @@
     return cc * x + ((ce * xe + cw * xw) + (cn * xn + cs * xs))
 
 
-def rows_kernel(f, w, area, mask, land, to_odd, to_even, fb, wb, ab, kb, sem):
+def rows_kernel(f, w, area, mask, land, to_odd, to_even, sea, fb, wb, ab, kb, sem):
     copies = []
     for n, (src, dst) in enumerate(((f, fb), (w, wb), (area, ab), (mask, kb))):
         for h in range(2):
@@ -81,8 +80,10 @@
     odd = lax.axis_index("lat") % 2 == 1
     for c in copies:
         c.wait()
-    m_lo = step_factor(ab[0, 0:2], kb[0, 0:2], land[0, 0])
-    m_hi = step_factor(ab[1, 6:8], kb[1, 6:8], land[0, 0])
+    is_sea = (1 - land[0, 0]).astype(F32)
+    sea[...] = jnp.full((8, 128), is_sea, F32)
+    m_lo = step_factor(ab[0, 0:2], kb[0, 0:2], is_sea)
+    m_hi = step_factor(ab[1, 6:8], kb[1, 6:8], is_sea)
     zero = jnp.zeros((2, 128), F32)
     for g in range(28):
         if g < NP:
@@ -97,7 +98,7 @@
         to_even[2 * g : 2 * g + 2] = jnp.where(odd, south, north)
 
 
-def columns_kernel(f, w, area, mask, land, out):
+def columns_kernel(f, w, area, mask, sea, out):
     for r in range(0, 128, CHUNK):
         rr = slice(r, r + CHUNK)
         group = lanes((CHUNK, 128)) // 4
@@ -108,14 +109,14 @@
             elif g < GM:
                 x = w[g - NP, rr]
             elif g == GM:
-                x = step_factor(area[rr], mask[rr], land[0, 0])
+                x = step_factor(area[rr], mask[rr], sea[0:1])
             else:
                 x = w[0, rr]
             acc = jnp.where(group == g, roll(x, 4 * g + 2 + (g == GS), 1), acc)
         out[rr] = acc
 
 
-def strips_kernel(to_odd, to_even, got_odd, got_even, pack, out, north, south, recv):
+def strips_kernel(to_odd, to_even, got_odd, got_even, pack, out, lon_odd, lon_even, north, south, recv):
     odd = lax.axis_index("lat") % 2 == 1
     top = lax.axis_index("lat") == lax.axis_size("lat") - 1
     raw = jnp.where(odd, got_odd[...], got_even[...])
@@ -142,6 +143,13 @@
     acc = jnp.where(lane // 4 == 28, roll(north[...], 114, 1), pack[0:ROWS4])
     out[0:ROWS4] = jnp.where(lane // 4 == 29, roll(south[...], 118, 1), acc)
     out[ROWS4:128] = pack[ROWS4:128]
+    j = lanes((64, 128)) % 4
+    a, b = out[0:64], out[64:128]
+    to_east = jnp.where(j < 2, a, roll(b, 2, 1))
+    to_west = jnp.where(j < 2, roll(b, -2, 1), a)
+    lon_is_odd = lax.axis_index("lon") % 2 == 1
+    lon_odd[...] = jnp.where(lon_is_odd, to_east, to_west)
+    lon_even[...] = jnp.where(lon_is_odd, to_west, to_east)
 
 
 def repeat_half(v, half):
@@ -152,14 +160,16 @@
 
 def lat_strip(strip, ends, shift_w, shift_e, top):
     lane = lanes((8, 128))
+    if ends is not None:
+        west = roll(ends[0][0:ROWS4], shift_w, 1)
+        east = roll(ends[1][0:ROWS4], shift_e, 1)
 
     def tile(t):
         x = strip[8 * t : 8 * t + 8]
         xe, xw = roll(x, -1, 1), roll(x, 1, 1)
         if ends is not None:
-            w = roll(ends[0][8 * t : 8 * t + 8], shift_w, 1)
-            e = roll(ends[1][8 * t : 8 * t + 8], shift_e, 1)
-            xe, xw = jnp.where(lane == 127, e, xe), jnp.where(lane == 0, w, xw)
+            xe = jnp.where(lane == 127, east[8 * t : 8 * t + 8], xe)
+            xw = jnp.where(lane == 0, west[8 * t : 8 * t + 8], xw)
         return x, xe, xw
 
     x12, e12, w12 = tile(12)
@@ -183,7 +193,7 @@
     return out
 
 
-def inner_kernel(fields, w, area, mask, land, north, south, res, ends, mid, halo, mw5):
+def inner_kernel(fields, w, area, mask, sea, north, south, res, ends, mid, halo, mw5, beside):
     top = lax.axis_index("lat") == lax.axis_size("lat") - 1
     for s, tiles in enumerate(
         (lat_strip(south, None, 0, 0, None), lat_strip(north, None, 0, 0, top))
@@ -191,28 +201,26 @@
         for t in range(12):
             halo[s, 8 * t : 8 * t + 8] = tiles[t]
 
-    m = step_factor(area[...], mask[...], land[0, 0])
+    m = step_factor(area[...], mask[...], sea[0:1])
     we, wn = w[0], w[1]
     first = rows_of((128, 128)) == 0
     ws = jnp.where(first, south[4 * GN + 1 : 4 * GN + 2], roll(wn, 1, 0))
     me, mw, mn, ms = m * we, m * roll(we, 1, 1), m * wn, m * ws
     for n, x in enumerate((me, mw, mn, ms, 1.0 - ((me + mw) + (mn + ms)))):
         mw5[n] = x
-    ends[...] = jnp.zeros((128, 128), F32)
-
     lane = lanes((CHUNK, 128))
     row = rows_of((CHUNK, 128))
-    for k in range(4):
-
+
+    def level(k, _):
         def first_get(f, r):
-            g = 4 * f + k
+            g = 4 * (4 * f + k)
             x = fields[f, k, r : r + CHUNK]
             if r == 0:
-                s = jnp.where(row == 0, south[4 * g + 1 : 4 * g + 2], roll(x, 1, 0))
+                s = jnp.where(row == 0, south[pl.ds(g + 1, 1)], roll(x, 1, 0))
             else:
                 s = fields[f, k, r - 1 : r - 1 + CHUNK]
             if r == 128 - CHUNK:
-                n = jnp.where(row == CHUNK - 1, north[4 * g + 2 : 4 * g + 3], roll(x, -1, 0))
+                n = jnp.where(row == CHUNK - 1, north[pl.ds(g + 2, 1)], roll(x, -1, 0))
             else:
                 n = fields[f, k, r + 1 : r + 1 + CHUNK]
             return x, n, s
@@ -221,9 +229,9 @@
             return tuple(mid[f, PAD + r + d : PAD + r + d + CHUNK] for d in (0, 1, -1))
 
         for f in range(6):
-            g = 4 * f + k
-            mid[f, PAD - 1 : PAD] = halo[0, 4 * g + 1 : 4 * g + 2]
-            mid[f, PAD + 128 : PAD + 129] = halo[1, 4 * g + 2 : 4 * g + 3]
+            g = 4 * (4 * f + k)
+            mid[f, PAD - 1 : PAD] = halo[0, pl.ds(g + 1, 1)]
+            mid[f, PAD + 128 : PAD + 129] = halo[1, pl.ds(g + 2, 1)]
         for substep, get in enumerate((first_get, second_get)):
             for r in range(0, 128, CHUNK):
                 rr = slice(r, r + CHUNK)
@@ -231,9 +239,7 @@
                 v, vn, vs = get(5, r)
                 c = coefs(u + roll(u, -1, 1), u + roll(u, 1, 1), v + vn, v + vs,
                           *(mw5[n, rr] for n in range(5)))
-                acc = ends[rr]
                 for f in range(6):
-                    g = 4 * f + k
                     x, xn, xs = get(f, r)
                     xe, xw = roll(x, -1, 1), roll(x, 1, 1)
                     y = apply(c, x, xe, xw, xn, xs)
@@ -241,10 +247,16 @@
                         mid[f, PAD + r : PAD + r + CHUNK] = y
                     else:
                         res[f, k, rr] = y
-                        beside = jnp.where(lane < 64, xe, xw)
-                        acc = jnp.where(lane // 4 == g, roll(beside, 4 * g + 2, 1), acc)
-                if substep == 1:
-                    ends[rr] = acc
+                        beside[f, k, rr] = jnp.where(lane < 64, xe, xw)
+        return 0
+
+    lax.fori_loop(0, 4, level, 0)
+    for r in range(0, 128, CHUNK):
+        acc = jnp.zeros((CHUNK, 128), F32)
+        for g in range(NP):
+            x = roll(beside[g // 4, g % 4, r : r + CHUNK], 4 * g + 2, 1)
+            acc = jnp.where(lane // 4 == g, x, acc)
+        ends[r : r + CHUNK] = acc
 
 
 def spread_matrix():
@@ -276,6 +288,8 @@
     top = lax.axis_index("lat") == lax.axis_size("lat") - 1
     west = jnp.where(odd, got_even[...], got_odd[...])
     east = jnp.where(odd, got_odd[...], got_even[...])
+    west = jnp.concatenate([west, roll(west, -2, 1)], axis=0)
+    east = jnp.concatenate([east, roll(east, 2, 1)], axis=0)
     own = pack[...]
     lane = lanes((128, 128))
     j = lane % 4
@@ -365,21 +379,17 @@
     return pl.BlockSpec(memory_space=pltpu.VMEM)
 
 
-def smem():
-    return pl.BlockSpec(memory_space=pltpu.SMEM)
-
-
 def local(nlon, nlat, fields, weights, area, mask, land):
     shape = jax.ShapeDtypeStruct
     planes = fields.reshape(NP, 128, 128)
     params = pltpu.CompilerParams(vmem_limit_bytes=24 << 20)
 
     rows = shape((ROWS2, 128), F32)
-    to_odd, to_even = pl.pallas_call(
+    to_odd, to_even, sea = pl.pallas_call(
         rows_kernel,
-        out_shape=(rows, rows),
-        in_specs=[pl.BlockSpec(memory_space=pltpu.HBM)] * 4 + [smem()],
-        out_specs=(vmem(), vmem()),
+        out_shape=(rows, rows, shape((8, 128), F32)),
+        in_specs=[pl.BlockSpec(memory_space=pltpu.HBM)] * 4 + [pl.BlockSpec(memory_space=pltpu.SMEM)],
+        out_specs=(vmem(),) * 3,
         scratch_shapes=[
             pltpu.VMEM((2, NP, 8, 128), F32),
             pltpu.VMEM((2, 2, 8, 128), F32),
@@ -397,22 +407,22 @@
     with jax.named_scope("lat_even"):
         got_even = lax.ppermute(to_even, axes, lat_pairs(nlon, nlat, False))
 
-    tile = shape((128, 128), F32)
+    tile, half = shape((128, 128), F32), shape((64, 128), F32)
     pack = pl.pallas_call(
         columns_kernel,
         out_shape=tile,
-        in_specs=[vmem()] * 4 + [smem()],
+        in_specs=[vmem()] * 5,
         out_specs=vmem(),
         compiler_params=params,
         cost_estimate=cost(2 << 20, 1 << 20),
         name="columns",
-    )(planes, weights, area, mask, land)
-
-    pack, north, south = pl.pallas_call(
+    )(planes, weights, area, mask, sea)
+
+    pack, lon_odd, lon_even, north, south = pl.pallas_call(
         strips_kernel,
-        out_shape=(tile, shape((ROWS4, 128), F32), shape((ROWS4, 128), F32)),
+        out_shape=(tile, half, half, shape((ROWS4, 128), F32), shape((ROWS4, 128), F32)),
         in_specs=[vmem()] * 5,
-        out_specs=(vmem(),) * 3,
+        out_specs=(vmem(),) * 5,
         scratch_shapes=[pltpu.VMEM((4, ROWS2, 128), F32)],
         compiler_params=params,
         cost_estimate=cost(1 << 18, 1 << 18),
@@ -420,26 +430,27 @@
     )(to_odd, to_even, got_odd, got_even, pack)
 
     with jax.named_scope("lon_even"):
-        col_even = lax.ppermute(pack, axes, lon_pairs(nlon, nlat, False))
+        col_even = lax.ppermute(lon_even, axes, lon_pairs(nlon, nlat, False))
     with jax.named_scope("lon_odd"):
-        col_odd = lax.ppermute(pack, axes, lon_pairs(nlon, nlat, True))
+        col_odd = lax.ppermute(lon_odd, axes, lon_pairs(nlon, nlat, True))
 
     padded = 128 + 2 * PAD
     state = shape((6, 4, 128, 128), F32)
     inner, ends = pl.pallas_call(
         inner_kernel,
         out_shape=(state, tile),
-        in_specs=[vmem()] * 4 + [smem()] + [vmem()] * 2,
+        in_specs=[vmem()] * 7,
         out_specs=(vmem(), vmem()),
         scratch_shapes=[
             pltpu.VMEM((6, padded, 128), F32),
             pltpu.VMEM((2, 96, 128), F32),
             pltpu.VMEM((5, 128, 128), F32),
+            pltpu.VMEM((6, 4, 128, 128), F32),
         ],
         compiler_params=params,
         cost_estimate=cost(4 << 20, 20 << 20),
         name="inner",
-    )(fields, weights, area, mask, land, north, south)
+    )(fields, weights, area, mask, sea, north, south)
 
     return pl.pallas_call(
         outer_kernel,

time: 37.5 us -> 33.1 us (0.88)
  the two profiles are of different devices: /device:TPU:36 before, /device:TPU:4 now
where the time goes in v3:
time: 33.1 us; the launch traced here: 32.8 us
  starting transfers between devices  21.3 us (64%)
  Pallas kernels  8.31 us (25%)
  waiting for transfers between devices  1.5 us (5%)
  between operations  0.93 us (3%)
  local copies, waits for them, and re-layouts  0.71 us (2%)
    ppermute x1, starting transfers between devices, local(): col_odd = lax.ppermute(lon_odd, axes, lon_pairs(nlon, nlat, True))  11.1 us
    ppermute x1, starting transfers between devices, local(): got_odd = lax.ppermute(to_odd, axes, lat_pairs(nlon, nlat, True))  4.44 us
    ppermute x1, starting transfers between devices, local(): col_even = lax.ppermute(lon_even, axes, lon_pairs(nlon, nlat, False))  3.83 us
    pallas_call x1, Pallas kernels, local(): pl.pallas_call(outer_kernel, out_shape=state, in_specs=[vmem()] * 8, out_...  2.89 us
    pallas_call x1, Pallas kernels, local(): pl.pallas_call(inner_kernel, out_shape=(state, tile), in_specs=[vmem()] *...  2.83 us
    ppermute x1, starting transfers between devices, local(): got_even = lax.ppermute(to_even, axes, lat_pairs(nlon, nlat, False))  1.92 us
    pallas_call x1, Pallas kernels, local(): pl.pallas_call(rows_kernel, out_shape=(rows, rows, shape((8, 128), F32)),...  1.67 us
    ppermute x1, waiting for transfers between devices, local(): got_odd = lax.ppermute(to_odd, axes, lat_pairs(nlon, nlat, True))  1.5 us
  transfers between devices with their start and end apart: 4, of which 1 were waited for; matrix products, arithmetic and copies ran while one was open for 0% of the time, Pallas kernels for 10%

profile of v3, /device:TPU:4, one launch (start us, length us, event | category | flops | bytes accessed | tf_op | source)
XLA Modules:
  0.0 32.8 jit_solution(6488693851087016930)
XLA Ops:
  0.0 0.0 copy-start.3
  0.0 0.0 copy-start.2
  0.0 0.0 copy-start.1
  0.0 0.0 copy-start
  0.8 1.7 %rows.1 = (f32[56,128]{1,0:T(8,128)}, f32[56,128]{1,0:T(8,128)}, f32[8,128]{1,0:T(8,128)}) custom-call(f32[24,128,128]{2,1,0:T(8,128)} %bitcast.1, f32[2,128,128]{2,1,0:T(8,128)} %w.5, f32[128,128]{1,0:T(8,128)} %area.5, s32[128,128]{1,0:T(8,128)} %mask.5, s32[1,1]{1,0:T(1,128)S(6)} %copy.7.land), custom_call_target="tpu_custom_call" | custom-call | flops 65536 | bytes 262144 | tf_op jit(solution)/shard_map/rows/pallas_call | solution.py:388
  2.5 0.0 copy-start.5
  2.5 0.0 copy-start.6
  2.5 4.4 %collective-permute-start = (f32[56,128]{1,0:T(8,128)}, f32[56,128]{1,0:T(8,128)S(1)}, u32[]{:S(2)}, u32[]{:S(2)}) collective-permute-start(f32[56,128]{1,0:T(8,128)} %get-tuple-element.15.to_odd), channel_id=1, source_target_pairs={{1,2},{2,1},{3,4},{4,3},{5,6},{6,5},{7,8},{8,7},{9,10},{10,9},{11,... | collective-permute-start | bytes 86024 | tf_op jit(solution)/shard_map/lat_odd/ppermute | solution.py:406
  6.9 1.9 %collective-permute-start.1 = (f32[56,128]{1,0:T(8,128)}, f32[56,128]{1,0:T(8,128)S(1)}, u32[]{:S(2)}, u32[]{:S(2)}) collective-permute-start(f32[56,128]{1,0:T(8,128)} %get-tuple-element.16.to_even), channel_id=1, source_target_pairs={{0,1},{1,0},{2,3},{3,2},{4,5},{5,4},{6,7},{7,6},{8,9},{9,8},{10,11... | collective-permute-start | bytes 86024 | tf_op jit(solution)/shard_map/lat_even/ppermute | solution.py:408
  8.9 0.0 copy-done.3
  8.9 0.0 copy-done.2
  8.9 0.0 copy-done.1
  8.9 0.0 copy-done
  8.9 0.0 copy-start.7
  8.9 0.7 %copy-done.7 = f32[8,128]{1,0:T(8,128)S(1)} copy-done((f32[8,128]{1,0:T(8,128)S(1)}, f32[8,128]{1,0:T(8,128)}, u32[]{:S(2)}) %copy-start.7) | copy-done | bytes 4120
  9.6 0.0 copy-start.4
  9.6 0.5 %columns.1.pack = f32[128,128]{1,0:T(8,128)S(1)} custom-call(f32[24,128,128]{2,1,0:T(8,128)S(1)} %bitcast.2, f32[2,128,128]{2,1,0:T(8,128)S(1)} %copy-done.1, f32[128,128]{1,0:T(8,128)S(1)} %copy-done.2, s32[128,128]{1,0:T(8,128)S(1)} %copy-done.3, f32[8,128]{1,0:T(8,128)S(1)} %copy-done.7), custom_call_target="tpu_custom_call" | custom-call | flops 1048576 | bytes 2097152 | tf_op jit(solution)/shard_map/columns/pallas_call | solution.py:411
  10.1 1.5 %collective-permute-done.got_odd = f32[56,128]{1,0:T(8,128)S(1)} collective-permute-done((f32[56,128]{1,0:T(8,128)}, f32[56,128]{1,0:T(8,128)S(1)}, u32[]{:S(2)}, u32[]{:S(2)}) %collective-permute-start) | collective-permute-done | bytes 28704 | tf_op jit(solution)/shard_map/lat_odd/ppermute | solution.py:406
  11.6 0.0 collective-permute-done.1.got_even
  11.6 0.0 copy-done.5
  11.6 0.0 copy-done.6
  11.7 0.4 %strips.1 = (f32[128,128]{1,0:T(8,128)S(1)}, f32[64,128]{1,0:T(8,128)S(1)}, f32[64,128]{1,0:T(8,128)S(1)}, f32[112,128]{1,0:T(8,128)S(1)}, f32[112,128]{1,0:T(8,128)S(1)}) custom-call(f32[56,128]{1,0:T(8,128)S(1)} %copy-done.5, f32[56,128]{1,0:T(8,128)S(1)} %copy-done.6, f32[56,128]{1,0:T(8,128)S(1)} %collective-permute-done.got_odd, ...), custom_call_target="tpu_custom_call" | custom-call | flops 262144 | bytes 262144 | tf_op jit(solution)/shard_map/strips/pallas_call | solution.py:421
  12.0 3.8 %collective-permute-start.2 = (f32[64,128]{1,0:T(8,128)S(1)}, f32[64,128]{1,0:T(8,128)S(1)}, u32[]{:S(2)}, u32[]{:S(2)}) collective-permute-start(f32[64,128]{1,0:T(8,128)S(1)} %get-tuple-element.19), channel_id=1, source_target_pairs={{0,16},{1,17},{2,18},{3,19},{4,20},{5,21},{6,22},{7,23},{8,24},{9,... | collective-permute-start | bytes 98312 | tf_op jit(solution)/shard_map/lon_even/ppermute | solution.py:433
  15.9 11.1 %collective-permute-start.3 = (f32[64,128]{1,0:T(8,128)S(1)}, f32[64,128]{1,0:T(8,128)S(1)}, u32[]{:S(2)}, u32[]{:S(2)}) collective-permute-start(f32[64,128]{1,0:T(8,128)S(1)} %get-tuple-element.20), channel_id=1, source_target_pairs={{0,496},{1,497},{2,498},{3,499},{4,500},{5,501},{6,502},{7,503},{8... | collective-permute-start | bytes 98312 | tf_op jit(solution)/shard_map/lon_odd/ppermute | solution.py:435
  27.0 2.8 %inner.1 = (f32[6,4,128,128]{3,2,1,0:T(8,128)S(1)}, f32[128,128]{1,0:T(8,128)S(1)}) custom-call(f32[6,4,128,128]{3,2,1,0:T(8,128)S(1)} %copy-done, f32[2,128,128]{2,1,0:T(8,128)S(1)} %copy-done.1, f32[128,128]{1,0:T(8,128)S(1)} %copy-done.2, s32[128,128]{1,0:T(8,128)S(1)} %copy-done.3, f32[8,128]{1,0:T(8,128)S(1)} %copy-done.7, ...), custom_call_target="tpu_custom_call" | custom-call | flops 20971520 | bytes 4194304 | tf_op jit(solution)/shard_map/inner/pallas_call | solution.py:439
  29.8 0.0 collective-permute-done.2.got_even
  29.9 0.0 collective-permute-done.3.got_odd
  29.9 0.0 copy-done.4
  29.9 2.9 %outer.1 = f32[6,4,128,128]{3,2,1,0:T(8,128)} custom-call(f32[128,128]{1,0:T(8,128)S(1)} %get-tuple-element.18.pack, f32[64,128]{1,0:T(8,128)S(1)} %collective-permute-done.2.got_even, f32[64,128]{1,0:T(8,128)S(1)} %collective-permute-done.3.got_odd, f32[112,128]{1,0:T(8,128)S(1)} %get-tuple-element.21.north, f32[112,128]{1,0:T(8,128)S(1)} %get-tuple-element.22.south, ...), custom_call_target="tpu_custom_call" | custom-call | flops 1048576 | bytes 4194304 | tf_op jit(solution)/shard_map/outer/pallas_call | solution.py:455
Async XLA Ops:
  0.0 8.9 %copy-start.3 = (s32[128,128]{1,0:T(8,128)S(1)}, s32[128,128]{1,0:T(8,128)}, u32[]{:S(2)}) copy-start(s32[128,128]{1,0:T(8,128)} %mask.5) | copy-start | bytes 196612
  0.0 8.9 %copy-start.2 = (f32[128,128]{1,0:T(8,128)S(1)}, f32[128,128]{1,0:T(8,128)}, u32[]{:S(2)}) copy-start(f32[128,128]{1,0:T(8,128)} %area.5) | copy-start | bytes 196612
  0.0 8.9 %copy-start.1 = (f32[2,128,128]{2,1,0:T(8,128)S(1)}, f32[2,128,128]{2,1,0:T(8,128)}, u32[]{:S(2)}) copy-start(f32[2,128,128]{2,1,0:T(8,128)} %w.5) | copy-start | bytes 393220
  0.0 8.9 %copy-start = (f32[6,4,128,128]{3,2,1,0:T(8,128)S(1)}, f32[6,4,128,128]{3,2,1,0:T(8,128)}, u32[]{:S(2)}) copy-start(f32[6,4,128,128]{3,2,1,0:T(8,128)} %fields.1) | copy-start | bytes 4718596
  2.5 9.2 %copy-start.5 = (f32[56,128]{1,0:T(8,128)S(1)}, f32[56,128]{1,0:T(8,128)}, u32[]{:S(2)}) copy-start(f32[56,128]{1,0:T(8,128)} %get-tuple-element.15.to_odd) | copy-start | bytes 86020
  2.5 9.2 %copy-start.6 = (f32[56,128]{1,0:T(8,128)S(1)}, f32[56,128]{1,0:T(8,128)}, u32[]{:S(2)}) copy-start(f32[56,128]{1,0:T(8,128)} %get-tuple-element.16.to_even) | copy-start | bytes 86020
  2.5 9.1 %collective-permute-start = (f32[56,128]{1,0:T(8,128)}, f32[56,128]{1,0:T(8,128)S(1)}, u32[]{:S(2)}, u32[]{:S(2)}) collective-permute-start(f32[56,128]{1,0:T(8,128)} %get-tuple-element.15.to_odd), channel_id=1, source_target_pairs={{1,2},{2,1},{3,4},{4,3},{5,6},{6,5},{7,8},{8,7},{9,10},{10,9},{11,... | collective-permute-start | bytes 86024 | tf_op jit(solution)/shard_map/lat_odd/ppermute | solution.py:406
  6.9 4.7 %collective-permute-start.1 = (f32[56,128]{1,0:T(8,128)}, f32[56,128]{1,0:T(8,128)S(1)}, u32[]{:S(2)}, u32[]{:S(2)}) collective-permute-start(f32[56,128]{1,0:T(8,128)} %get-tuple-element.16.to_even), channel_id=1, source_target_pairs={{0,1},{1,0},{2,3},{3,2},{4,5},{5,4},{6,7},{7,6},{8,9},{9,8},{10,11... | collective-permute-start | bytes 86024 | tf_op jit(solution)/shard_map/lat_even/ppermute | solution.py:408
  8.9 0.7 %copy-start.7 = (f32[8,128]{1,0:T(8,128)S(1)}, f32[8,128]{1,0:T(8,128)}, u32[]{:S(2)}) copy-start(f32[8,128]{1,0:T(8,128)} %get-tuple-element.17.sea) | copy-start | bytes 12292
  9.6 20.3 %copy-start.4 = (bf16[128,896]{1,0:T(8,128)(2,1)S(1)}, bf16[128,896]{1,0:T(8,128)(2,1)}, u32[]{:S(2)}) copy-start(bf16[128,896]{1,0:T(8,128)(2,1)} %constant.2.clone.matrix) | copy-start | bytes 688132
  12.0 17.8 %collective-permute-start.2 = (f32[64,128]{1,0:T(8,128)S(1)}, f32[64,128]{1,0:T(8,128)S(1)}, u32[]{:S(2)}, u32[]{:S(2)}) collective-permute-start(f32[64,128]{1,0:T(8,128)S(1)} %get-tuple-element.19), channel_id=1, source_target_pairs={{0,16},{1,17},{2,18},{3,19},{4,20},{5,21},{6,22},{7,23},{8,24},{9,... | collective-permute-start | bytes 98312 | tf_op jit(solution)/shard_map/lon_even/ppermute | solution.py:433
  15.9 14.0 %collective-permute-start.3 = (f32[64,128]{1,0:T(8,128)S(1)}, f32[64,128]{1,0:T(8,128)S(1)}, u32[]{:S(2)}, u32[]{:S(2)}) collective-permute-start(f32[64,128]{1,0:T(8,128)S(1)} %get-tuple-element.20), channel_id=1, source_target_pairs={{0,496},{1,497},{2,498},{3,499},{4,500},{5,501},{6,502},{7,503},{8... | collective-permute-start | bytes 98312 | tf_op jit(solution)/shard_map/lon_odd/ppermute | solution.py:435

commit v4 on v3

--- a/solution.py
+++ b/solution.py
@@ -18,13 +18,8 @@
 HIGH = lax.Precision.HIGHEST
 
 
-def lon_pairs(nlon, nlat, odd):
-    def other(i):
-        if not odd:
-            return i ^ 1
-        return (i + 1) % nlon if i % 2 else (i - 1) % nlon
-
-    return [(i * nlat + l, other(i) * nlat + l) for i in range(nlon) for l in range(nlat)]
+def lon_pairs(nlon, nlat, step):
+    return [(i * nlat + l, (i + step) % nlon * nlat + l) for i in range(nlon) for l in range(nlat)]
 
 
 def lat_pairs(nlon, nlat, odd):
@@ -68,7 +63,7 @@
     return cc * x + ((ce * xe + cw * xw) + (cn * xn + cs * xs))
 
 
-def rows_kernel(f, w, area, mask, land, to_odd, to_even, sea, fb, wb, ab, kb, sem):
+def rows_kernel(f, w, area, mask, land, to_odd, to_even, fb, wb, ab, kb, sem):
     copies = []
     for n, (src, dst) in enumerate(((f, fb), (w, wb), (area, ab), (mask, kb))):
         for h in range(2):
@@ -81,7 +76,6 @@
     for c in copies:
         c.wait()
     is_sea = (1 - land[0, 0]).astype(F32)
-    sea[...] = jnp.full((8, 128), is_sea, F32)
     m_lo = step_factor(ab[0, 0:2], kb[0, 0:2], is_sea)
     m_hi = step_factor(ab[1, 6:8], kb[1, 6:8], is_sea)
     zero = jnp.zeros((2, 128), F32)
@@ -98,7 +92,8 @@
         to_even[2 * g : 2 * g + 2] = jnp.where(odd, south, north)
 
 
-def columns_kernel(f, w, area, mask, sea, out):
+def columns_kernel(f, w, area, mask, land, out):
+    sea = (1 - land[0, 0]).astype(F32)
     for r in range(0, 128, CHUNK):
         rr = slice(r, r + CHUNK)
         group = lanes((CHUNK, 128)) // 4
@@ -109,14 +104,14 @@
             elif g < GM:
                 x = w[g - NP, rr]
             elif g == GM:
-                x = step_factor(area[rr], mask[rr], sea[0:1])
+                x = step_factor(area[rr], mask[rr], sea)
             else:
                 x = w[0, rr]
             acc = jnp.where(group == g, roll(x, 4 * g + 2 + (g == GS), 1), acc)
         out[rr] = acc
 
 
-def strips_kernel(to_odd, to_even, got_odd, got_even, pack, out, lon_odd, lon_even, north, south, recv):
+def strips_kernel(to_odd, to_even, got_odd, got_even, pack, out, to_east, to_west, north, south, recv):
     odd = lax.axis_index("lat") % 2 == 1
     top = lax.axis_index("lat") == lax.axis_size("lat") - 1
     raw = jnp.where(odd, got_odd[...], got_even[...])
@@ -145,11 +140,8 @@
     out[ROWS4:128] = pack[ROWS4:128]
     j = lanes((64, 128)) % 4
     a, b = out[0:64], out[64:128]
-    to_east = jnp.where(j < 2, a, roll(b, 2, 1))
-    to_west = jnp.where(j < 2, roll(b, -2, 1), a)
-    lon_is_odd = lax.axis_index("lon") % 2 == 1
-    lon_odd[...] = jnp.where(lon_is_odd, to_east, to_west)
-    lon_even[...] = jnp.where(lon_is_odd, to_west, to_east)
+    to_east[...] = jnp.where(j < 2, a, roll(b, 2, 1))
+    to_west[...] = jnp.where(j < 2, roll(b, -2, 1), a)
 
 
 def repeat_half(v, half):
@@ -193,7 +185,16 @@
     return out
 
 
-def inner_kernel(fields, w, area, mask, sea, north, south, res, ends, mid, halo, mw5, beside):
+def inner_kernel(early, fields, w, area, mask, land, north, south, *refs):
+    blocks = lax.axis_size("lon") // 2
+    soon = lax.axis_index("lon") % blocks < max(1, blocks // 4)
+
+    @pl.when(soon if early else jnp.logical_not(soon))
+    def _():
+        inner_steps(fields, w, area, mask, land, north, south, *refs[-6:])
+
+
+def inner_steps(fields, w, area, mask, land, north, south, res, ends, mid, halo, mw5, beside):
     top = lax.axis_index("lat") == lax.axis_size("lat") - 1
     for s, tiles in enumerate(
         (lat_strip(south, None, 0, 0, None), lat_strip(north, None, 0, 0, top))
@@ -201,7 +202,7 @@
         for t in range(12):
             halo[s, 8 * t : 8 * t + 8] = tiles[t]
 
-    m = step_factor(area[...], mask[...], sea[0:1])
+    m = step_factor(area[...], mask[...], (1 - land[0, 0]).astype(F32))
     we, wn = w[0], w[1]
     first = rows_of((128, 128)) == 0
     ws = jnp.where(first, south[4 * GN + 1 : 4 * GN + 2], roll(wn, 1, 0))
@@ -282,12 +283,10 @@
     return dot(lo, matrix) + dot(mid, matrix) + dot(hi, matrix)
 
 
-def outer_kernel(pack, got_even, got_odd, north, south, inner, ends, matrix, out_hbm,
+def outer_kernel(pack, got_west, got_east, north, south, inner, ends, matrix, out_hbm,
                  side, wide, halo, z, res, sem):
-    odd = lax.axis_index("lon") % 2 == 1
     top = lax.axis_index("lat") == lax.axis_size("lat") - 1
-    west = jnp.where(odd, got_even[...], got_odd[...])
-    east = jnp.where(odd, got_odd[...], got_even[...])
+    west, east = got_west[...], got_east[...]
     west = jnp.concatenate([west, roll(west, -2, 1)], axis=0)
     east = jnp.concatenate([east, roll(east, 2, 1)], axis=0)
     own = pack[...]
@@ -375,6 +374,10 @@
     return pl.CostEstimate(flops=flops, bytes_accessed=nbytes, transcendentals=0)
 
 
+def smem():
+    return pl.BlockSpec(memory_space=pltpu.SMEM)
+
+
 def vmem():
     return pl.BlockSpec(memory_space=pltpu.VMEM)
 
@@ -385,11 +388,11 @@
     params = pltpu.CompilerParams(vmem_limit_bytes=24 << 20)
 
     rows = shape((ROWS2, 128), F32)
-    to_odd, to_even, sea = pl.pallas_call(
+    to_odd, to_even = pl.pallas_call(
         rows_kernel,
-        out_shape=(rows, rows, shape((8, 128), F32)),
-        in_specs=[pl.BlockSpec(memory_space=pltpu.HBM)] * 4 + [pl.BlockSpec(memory_space=pltpu.SMEM)],
-        out_specs=(vmem(),) * 3,
+        out_shape=(rows, rows),
+        in_specs=[pl.BlockSpec(memory_space=pltpu.HBM)] * 4 + [smem()],
+        out_specs=(vmem(),) * 2,
         scratch_shapes=[
             pltpu.VMEM((2, NP, 8, 128), F32),
             pltpu.VMEM((2, 2, 8, 128), F32),
@@ -411,14 +414,14 @@
     pack = pl.pallas_call(
         columns_kernel,
         out_shape=tile,
-        in_specs=[vmem()] * 5,
+        in_specs=[vmem()] * 4 + [smem()],
         out_specs=vmem(),
         compiler_params=params,
         cost_estimate=cost(2 << 20, 1 << 20),
         name="columns",
-    )(planes, weights, area, mask, sea)
-
-    pack, lon_odd, lon_even, north, south = pl.pallas_call(
+    )(planes, weights, area, mask, land)
+
+    pack, to_east, to_west, north, south = pl.pallas_call(
         strips_kernel,
         out_shape=(tile, half, half, shape((ROWS4, 128), F32), shape((ROWS4, 128), F32)),
         in_specs=[vmem()] * 5,
@@ -429,28 +432,36 @@
         name="strips",
     )(to_odd, to_even, got_odd, got_even, pack)
 
-    with jax.named_scope("lon_even"):
-        col_even = lax.ppermute(lon_even, axes, lon_pairs(nlon, nlat, False))
-    with jax.named_scope("lon_odd"):
-        col_odd = lax.ppermute(lon_odd, axes, lon_pairs(nlon, nlat, True))
+    with jax.named_scope("lon_east"):
+        got_west = lax.ppermute(to_east, axes, lon_pairs(nlon, nlat, 1))
 
     padded = 128 + 2 * PAD
     state = shape((6, 4, 128, 128), F32)
-    inner, ends = pl.pallas_call(
-        inner_kernel,
-        out_shape=(state, tile),
-        in_specs=[vmem()] * 7,
-        out_specs=(vmem(), vmem()),
-        scratch_shapes=[
-            pltpu.VMEM((6, padded, 128), F32),
-            pltpu.VMEM((2, 96, 128), F32),
-            pltpu.VMEM((5, 128, 128), F32),
-            pltpu.VMEM((6, 4, 128, 128), F32),
-        ],
-        compiler_params=params,
-        cost_estimate=cost(4 << 20, 20 << 20),
-        name="inner",
-    )(fields, weights, area, mask, sea, north, south)
+    inputs = (fields, weights, area, mask, land, north, south)
+
+    def inner_call(early, before):
+        return pl.pallas_call(
+            functools.partial(inner_kernel, early),
+            out_shape=(state, tile),
+            in_specs=[vmem()] * 4 + [smem()] + [vmem()] * (2 + len(before)),
+            out_specs=(vmem(), vmem()),
+            scratch_shapes=[
+                pltpu.VMEM((6, padded, 128), F32),
+                pltpu.VMEM((2, 96, 128), F32),
+                pltpu.VMEM((5, 128, 128), F32),
+                pltpu.VMEM((6, 4, 128, 128), F32),
+            ],
+            input_output_aliases={7: 0, 8: 1} if before else {},
+            compiler_params=params,
+            cost_estimate=cost(4 << 20, 20 << 20),
+            name="inner_early" if early else "inner_late",
+        )(*inputs, *before)
+
+    inner, ends = inner_call(True, ())
+    to_west, inner, ends = lax.optimization_barrier((to_west, inner, ends))
+    with jax.named_scope("lon_west"):
+        got_east = lax.ppermute(to_west, axes, lon_pairs(nlon, nlat, -1))
+    inner, ends = inner_call(False, (inner, ends))
 
     return pl.pallas_call(
         outer_kernel,
@@ -468,7 +479,7 @@
         compiler_params=params,
         cost_estimate=cost(4 << 20, 1 << 20),
         name="outer",
-    )(pack, col_even, col_odd, north, south, inner, ends, jnp.asarray(spread_matrix(), jnp.bfloat16))
+    )(pack, got_west, got_east, north, south, inner, ends, jnp.asarray(spread_matrix(), jnp.bfloat16))
 
 
 def solution(mesh):

time: 33.1 us -> 34.8 us (1.051)
  the two profiles are of different devices: /device:TPU:4 before, /device:TPU:124 now
where the time goes in v4:
time: 34.8 us; the launch traced here: 34.6 us
  starting transfers between devices  19.8 us (57%)
  Pallas kernels  8.33 us (24%)
  waiting for transfers between devices  5.5 us (16%)
  between operations  0.93 us (3%)
    ppermute x1, starting transfers between devices, local(): got_even = lax.ppermute(to_even, axes, lat_pairs(nlon, nlat, False))  11.4 us
    ppermute x1, waiting for transfers between devices, local(): got_east = lax.ppermute(to_west, axes, lon_pairs(nlon, nlat, -1))  5.05 us
    ppermute x1, starting transfers between devices, local(): got_west = lax.ppermute(to_east, axes, lon_pairs(nlon, nlat, 1))  4.13 us
    pallas_call x2, Pallas kernels, inner_call(): pl.pallas_call(functools.partial(inner_kernel, early), out_shape=(state,...  2.87 us
    pallas_call x1, Pallas kernels, local(): pl.pallas_call(outer_kernel, out_shape=state, in_specs=[vmem()] * 8, out_...  2.87 us
    ppermute x1, starting transfers between devices, local(): got_odd = lax.ppermute(to_odd, axes, lat_pairs(nlon, nlat, True))  2.22 us
    ppermute x1, starting transfers between devices, local(): got_east = lax.ppermute(to_west, axes, lon_pairs(nlon, nlat, -1))  2.05 us
    pallas_call x1, Pallas kernels, local(): pl.pallas_call(rows_kernel, out_shape=(rows, rows), in_specs=[pl.BlockSpe...  1.67 us
  transfers between devices with their start and end apart: 4, of which 2 were waited for; matrix products, arithmetic and copies ran while one was open for 0% of the time, Pallas kernels for 10%

profile of v4, /device:TPU:124, one launch (start us, length us, event | category | flops | bytes accessed | tf_op | source)
XLA Modules:
  0.0 34.6 jit_solution(8946312122399889517)
XLA Ops:
  0.0 0.0 copy-start.3
  0.0 0.0 copy-start.2
  0.0 0.0 copy-start.1
  0.0 0.0 copy-start
  0.8 1.7 %rows.1 = (f32[56,128]{1,0:T(8,128)}, f32[56,128]{1,0:T(8,128)}) custom-call(f32[24,128,128]{2,1,0:T(8,128)} %bitcast.1, f32[2,128,128]{2,1,0:T(8,128)} %w.7, f32[128,128]{1,0:T(8,128)} %area.7, s32[128,128]{1,0:T(8,128)} %mask.7, s32[1,1]{1,0:T(1,128)S(6)} %copy.11.land), custom_call_target="tpu_custom_call" | custom-call | flops 65536 | bytes 262144 | tf_op jit(solution)/shard_map/rows/pallas_call | solution.py:391
  2.5 0.0 copy-start.5
  2.5 0.0 copy-start.6
  2.5 2.2 %collective-permute-start = (f32[56,128]{1,0:T(8,128)}, f32[56,128]{1,0:T(8,128)S(1)}, u32[]{:S(2)}, u32[]{:S(2)}) collective-permute-start(f32[56,128]{1,0:T(8,128)} %get-tuple-element.19.to_odd), channel_id=1, source_target_pairs={{1,2},{2,1},{3,4},{4,3},{5,6},{6,5},{7,8},{8,7},{9,10},{10,9},{11,... | collective-permute-start | bytes 86024 | tf_op jit(solution)/shard_map/lat_odd/ppermute | solution.py:409
  4.7 11.4 %collective-permute-start.1 = (f32[56,128]{1,0:T(8,128)}, f32[56,128]{1,0:T(8,128)S(1)}, u32[]{:S(2)}, u32[]{:S(2)}) collective-permute-start(f32[56,128]{1,0:T(8,128)} %get-tuple-element.20.to_even), channel_id=1, source_target_pairs={{0,1},{1,0},{2,3},{3,2},{4,5},{5,4},{6,7},{7,6},{8,9},{9,8},{10,11... | collective-permute-start | bytes 86024 | tf_op jit(solution)/shard_map/lat_even/ppermute | solution.py:411
  16.1 0.0 copy-done.3
  16.1 0.0 copy-done.2
  16.1 0.0 copy-done.1
  16.1 0.0 copy-done
  16.1 0.5 %columns.1.pack = f32[128,128]{1,0:T(8,128)S(1)} custom-call(f32[24,128,128]{2,1,0:T(8,128)S(1)} %bitcast.2, f32[2,128,128]{2,1,0:T(8,128)S(1)} %copy-done.1, f32[128,128]{1,0:T(8,128)S(1)} %copy-done.2, s32[128,128]{1,0:T(8,128)S(1)} %copy-done.3, s32[1,1]{1,0:T(1,128)S(6)} %copy.11.land), custom_call_target="tpu_custom_call" | custom-call | flops 1048576 | bytes 2097152 | tf_op jit(solution)/shard_map/columns/pallas_call | solution.py:414
  16.7 0.0 collective-permute-done.got_odd
  16.7 0.4 %collective-permute-done.1.got_even = f32[56,128]{1,0:T(8,128)S(1)} collective-permute-done((f32[56,128]{1,0:T(8,128)}, f32[56,128]{1,0:T(8,128)S(1)}, u32[]{:S(2)}, u32[]{:S(2)}) %collective-permute-start.1) | collective-permute-done | bytes 28704 | tf_op jit(solution)/shard_map/lat_even/ppermute | solution.py:411
  17.2 0.0 copy-done.5
  17.2 0.0 copy-done.6
  17.2 0.4 %strips.1 = (f32[128,128]{1,0:T(8,128)S(1)}, f32[64,128]{1,0:T(8,128)S(1)}, f32[64,128]{1,0:T(8,128)S(1)}, f32[112,128]{1,0:T(8,128)S(1)}, f32[112,128]{1,0:T(8,128)S(1)}) custom-call(f32[56,128]{1,0:T(8,128)S(1)} %copy-done.5, f32[56,128]{1,0:T(8,128)S(1)} %copy-done.6, f32[56,128]{1,0:T(8,128)S(1)} %collective-permute-done.got_odd, ...), custom_call_target="tpu_custom_call" | custom-call | flops 262144 | bytes 262144 | tf_op jit(solution)/shard_map/strips/pallas_call | solution.py:424
  17.5 4.1 %collective-permute-start.2 = (f32[64,128]{1,0:T(8,128)S(1)}, f32[64,128]{1,0:T(8,128)S(1)}, u32[]{:S(2)}, u32[]{:S(2)}) collective-permute-start(f32[64,128]{1,0:T(8,128)S(1)} %get-tuple-element.22), channel_id=1, source_target_pairs={{0,16},{1,17},{2,18},{3,19},{4,20},{5,21},{6,22},{7,23},{8,24},{9,... | collective-permute-start | bytes 98312 | tf_op jit(solution)/shard_map/lon_east/ppermute | solution.py:436
  21.7 2.9 %inner_early.1 = (f32[6,4,128,128]{3,2,1,0:T(8,128)S(1)}, f32[128,128]{1,0:T(8,128)S(1)}) custom-call(f32[6,4,128,128]{3,2,1,0:T(8,128)S(1)} %copy-done, f32[2,128,128]{2,1,0:T(8,128)S(1)} %copy-done.1, f32[128,128]{1,0:T(8,128)S(1)} %copy-done.2, s32[128,128]{1,0:T(8,128)S(1)} %copy-done.3, s32[1,1]{1,0:T(1,128)S(6)} %copy.11.land, ...), custom_call_target="tpu_custom_call" | custom-call | flops 20971520 | bytes 4194304 | tf_op jit(solution)/shard_map/inner_early/pallas_call | solution.py:443
  24.5 0.0 copy-start.4
  24.5 2.1 %collective-permute-start.3 = (f32[64,128]{1,0:T(8,128)S(1)}, f32[64,128]{1,0:T(8,128)S(1)}, u32[]{:S(2)}, u32[]{:S(2)}) collective-permute-start(f32[64,128]{1,0:T(8,128)S(1)} %get-tuple-element.28), channel_id=1, source_target_pairs={{0,496},{1,497},{2,498},{3,499},{4,500},{5,501},{6,502},{7,503},{8... | collective-permute-start | bytes 98312 | tf_op jit(solution)/shard_map/lon_west/ppermute | solution.py:463
  26.6 0.0 collective-permute-done.2.got_west
  26.6 5.0 %collective-permute-done.3.got_east = f32[64,128]{1,0:T(8,128)S(1)} collective-permute-done((f32[64,128]{1,0:T(8,128)S(1)}, f32[64,128]{1,0:T(8,128)S(1)}, u32[]{:S(2)}, u32[]{:S(2)}) %collective-permute-start.3) | collective-permute-done | bytes 32800 | tf_op jit(solution)/shard_map/lon_west/ppermute | solution.py:463
  31.7 0.0 copy-done.4
  31.7 2.9 %outer.1 = f32[6,4,128,128]{3,2,1,0:T(8,128)} custom-call(f32[128,128]{1,0:T(8,128)S(1)} %get-tuple-element.21.pack, f32[64,128]{1,0:T(8,128)S(1)} %collective-permute-done.2.got_west, f32[64,128]{1,0:T(8,128)S(1)} %collective-permute-done.3.got_east, f32[112,128]{1,0:T(8,128)S(1)} %get-tuple-element.24.north, f32[112,128]{1,0:T(8,128)S(1)} %get-tuple-element.25.south, ...), custom_call_target="tpu_custom_call" | custom-call | flops 1048576 | bytes 4194304 | tf_op jit(solution)/shard_map/outer/pallas_call | solution.py:466
  (1 shorter events, 0.0 us)
Async XLA Ops:
  0.0 16.1 %copy-start.3 = (s32[128,128]{1,0:T(8,128)S(1)}, s32[128,128]{1,0:T(8,128)}, u32[]{:S(2)}) copy-start(s32[128,128]{1,0:T(8,128)} %mask.7) | copy-start | bytes 196612
  0.0 16.1 %copy-start.2 = (f32[128,128]{1,0:T(8,128)S(1)}, f32[128,128]{1,0:T(8,128)}, u32[]{:S(2)}) copy-start(f32[128,128]{1,0:T(8,128)} %area.7) | copy-start | bytes 196612
  0.0 16.1 %copy-start.1 = (f32[2,128,128]{2,1,0:T(8,128)S(1)}, f32[2,128,128]{2,1,0:T(8,128)}, u32[]{:S(2)}) copy-start(f32[2,128,128]{2,1,0:T(8,128)} %w.7) | copy-start | bytes 393220
  0.0 16.1 %copy-start = (f32[6,4,128,128]{3,2,1,0:T(8,128)S(1)}, f32[6,4,128,128]{3,2,1,0:T(8,128)}, u32[]{:S(2)}) copy-start(f32[6,4,128,128]{3,2,1,0:T(8,128)} %fields.3) | copy-start | bytes 4718596
  2.5 14.7 %copy-start.5 = (f32[56,128]{1,0:T(8,128)S(1)}, f32[56,128]{1,0:T(8,128)}, u32[]{:S(2)}) copy-start(f32[56,128]{1,0:T(8,128)} %get-tuple-element.19.to_odd) | copy-start | bytes 86020
  2.5 14.7 %copy-start.6 = (f32[56,128]{1,0:T(8,128)S(1)}, f32[56,128]{1,0:T(8,128)}, u32[]{:S(2)}) copy-start(f32[56,128]{1,0:T(8,128)} %get-tuple-element.20.to_even) | copy-start | bytes 86020
  2.5 14.2 %collective-permute-start = (f32[56,128]{1,0:T(8,128)}, f32[56,128]{1,0:T(8,128)S(1)}, u32[]{:S(2)}, u32[]{:S(2)}) collective-permute-start(f32[56,128]{1,0:T(8,128)} %get-tuple-element.19.to_odd), channel_id=1, source_target_pairs={{1,2},{2,1},{3,4},{4,3},{5,6},{6,5},{7,8},{8,7},{9,10},{10,9},{11,... | collective-permute-start | bytes 86024 | tf_op jit(solution)/shard_map/lat_odd/ppermute | solution.py:409
  4.7 12.4 %collective-permute-start.1 = (f32[56,128]{1,0:T(8,128)}, f32[56,128]{1,0:T(8,128)S(1)}, u32[]{:S(2)}, u32[]{:S(2)}) collective-permute-start(f32[56,128]{1,0:T(8,128)} %get-tuple-element.20.to_even), channel_id=1, source_target_pairs={{0,1},{1,0},{2,3},{3,2},{4,5},{5,4},{6,7},{7,6},{8,9},{9,8},{10,11... | collective-permute-start | bytes 86024 | tf_op jit(solution)/shard_map/lat_even/ppermute | solution.py:411
  17.5 9.1 %collective-permute-start.2 = (f32[64,128]{1,0:T(8,128)S(1)}, f32[64,128]{1,0:T(8,128)S(1)}, u32[]{:S(2)}, u32[]{:S(2)}) collective-permute-start(f32[64,128]{1,0:T(8,128)S(1)} %get-tuple-element.22), channel_id=1, source_target_pairs={{0,16},{1,17},{2,18},{3,19},{4,20},{5,21},{6,22},{7,23},{8,24},{9,... | collective-permute-start | bytes 98312 | tf_op jit(solution)/shard_map/lon_east/ppermute | solution.py:436
  24.5 7.2 %copy-start.4 = (bf16[128,896]{1,0:T(8,128)(2,1)S(1)}, bf16[128,896]{1,0:T(8,128)(2,1)}, u32[]{:S(2)}) copy-start(bf16[128,896]{1,0:T(8,128)(2,1)} %constant.2.clone.matrix) | copy-start | bytes 688132
  24.5 7.2 %collective-permute-start.3 = (f32[64,128]{1,0:T(8,128)S(1)}, f32[64,128]{1,0:T(8,128)S(1)}, u32[]{:S(2)}, u32[]{:S(2)}) collective-permute-start(f32[64,128]{1,0:T(8,128)S(1)} %get-tuple-element.28), channel_id=1, source_target_pairs={{0,496},{1,497},{2,498},{3,499},{4,500},{5,501},{6,502},{7,503},{8... | collective-permute-start | bytes 98312 | tf_op jit(solution)/shard_map/lon_west/ppermute | solution.py:463

commit v5 on v4

--- a/solution.py
+++ b/solution.py
@@ -185,13 +185,15 @@
     return out
 
 
+def runs_early():
+    first = lax.axis_index("lon") % (lax.axis_size("lon") // 2) == 0
+    return first & (lax.axis_index("lat") < lax.axis_size("lat") - 2)
+
+
 def inner_kernel(early, fields, w, area, mask, land, north, south, *refs):
-    blocks = lax.axis_size("lon") // 2
-    soon = lax.axis_index("lon") % blocks < max(1, blocks // 4)
-
-    @pl.when(soon if early else jnp.logical_not(soon))
+    @pl.when(runs_early() if early else jnp.logical_not(runs_early()))
     def _():
-        inner_steps(fields, w, area, mask, land, north, south, *refs[-6:])
+        inner_steps(fields, w, area, mask, land, north, south, *refs)
 
 
 def inner_steps(fields, w, area, mask, land, north, south, res, ends, mid, halo, mw5, beside):
@@ -283,13 +285,15 @@
     return dot(lo, matrix) + dot(mid, matrix) + dot(hi, matrix)
 
 
-def outer_kernel(pack, got_west, got_east, north, south, inner, ends, matrix, out_hbm,
+def outer_kernel(pack, got_west, got_east, north, south, inner_a, inner_b, ends_a, ends_b, matrix, out_hbm,
                  side, wide, halo, z, res, sem):
     top = lax.axis_index("lat") == lax.axis_size("lat") - 1
     west, east = got_west[...], got_east[...]
     west = jnp.concatenate([west, roll(west, -2, 1)], axis=0)
     east = jnp.concatenate([east, roll(east, 2, 1)], axis=0)
     own = pack[...]
+    early = runs_early()
+    ends = jnp.where(early, ends_a[...], ends_b[...])
     lane = lanes((128, 128))
     j = lane % 4
     span = 128 + 2 * PAD
@@ -348,7 +352,7 @@
     new = [[update(s, r) for r in range(0, 128, CHUNK)] for s in range(2)]
     edge = (j == 0) | (j == 3)
     for s in range(2):
-        strip = jnp.where(edge, roll(ends[...], 1 - 2 * s, 1), jnp.concatenate(new[s], axis=0))
+        strip = jnp.where(edge, roll(ends, 1 - 2 * s, 1), jnp.concatenate(new[s], axis=0))
         fill(s, strip, above, below)
     widen(3)
     jj = lanes((CHUNK, 128)) % 4
@@ -362,7 +366,8 @@
             rr = slice(r, r + CHUNK)
             zr = z[rr]
             for f in range(6):
-                res[f, k, rr] = jnp.where(outer, roll(zr, -(4 * (4 * f + k) + 2), 1), inner[f, k, rr])
+                x = jnp.where(early, inner_a[f, k, rr], inner_b[f, k, rr])
+                res[f, k, rr] = jnp.where(outer, roll(zr, -(4 * (4 * f + k) + 2), 1), x)
         c = pltpu.make_async_copy(res.at[:, k], out_hbm.at[:, k], sem.at[k])
         c.start()
         outs.append(c)
@@ -439,11 +444,11 @@
     state = shape((6, 4, 128, 128), F32)
     inputs = (fields, weights, area, mask, land, north, south)
 
-    def inner_call(early, before):
+    def inner_call(early):
         return pl.pallas_call(
             functools.partial(inner_kernel, early),
             out_shape=(state, tile),
-            in_specs=[vmem()] * 4 + [smem()] + [vmem()] * (2 + len(before)),
+            in_specs=[vmem()] * 4 + [smem()] + [vmem()] * 2,
             out_specs=(vmem(), vmem()),
             scratch_shapes=[
                 pltpu.VMEM((6, padded, 128), F32),
@@ -451,22 +456,21 @@
                 pltpu.VMEM((5, 128, 128), F32),
                 pltpu.VMEM((6, 4, 128, 128), F32),
             ],
-            input_output_aliases={7: 0, 8: 1} if before else {},
             compiler_params=params,
             cost_estimate=cost(4 << 20, 20 << 20),
             name="inner_early" if early else "inner_late",
-        )(*inputs, *before)
-
-    inner, ends = inner_call(True, ())
-    to_west, inner, ends = lax.optimization_barrier((to_west, inner, ends))
+        )(*inputs)
+
+    inner_a, ends_a = inner_call(True)
+    to_west, inner_a, ends_a = lax.optimization_barrier((to_west, inner_a, ends_a))
     with jax.named_scope("lon_west"):
         got_east = lax.ppermute(to_west, axes, lon_pairs(nlon, nlat, -1))
-    inner, ends = inner_call(False, (inner, ends))
+    inner_b, ends_b = inner_call(False)
 
     return pl.pallas_call(
         outer_kernel,
         out_shape=state,
-        in_specs=[vmem()] * 8,
+        in_specs=[vmem()] * 10,
         out_specs=pl.BlockSpec(memory_space=pltpu.HBM),
         scratch_shapes=[
             pltpu.VMEM((2, padded, 128), F32),
@@ -479,7 +483,7 @@
         compiler_params=params,
         cost_estimate=cost(4 << 20, 1 << 20),
         name="outer",
-    )(pack, got_west, got_east, north, south, inner, ends, jnp.asarray(spread_matrix(), jnp.bfloat16))
+    )(pack, got_west, got_east, north, south, inner_a, inner_b, ends_a, ends_b, jnp.asarray(spread_matrix(), jnp.bfloat16))
 
 
 def solution(mesh):

time: 34.8 us -> 32 us (0.920)
  the two profiles are of different devices: /device:TPU:124 before, /device:TPU:28 now
where the time goes in v5:
time: 32 us; the launch traced here: 31.5 us
  starting transfers between devices  21.7 us (68%)
  Pallas kernels  8.35 us (26%)
  between operations  0.95 us (3%)
  waiting for transfers between devices  0.45 us (1%)
    ppermute x1, starting transfers between devices, local(): got_even = lax.ppermute(to_even, axes, lat_pairs(nlon, nlat, False))  11.4 us
    ppermute x1, starting transfers between devices, local(): got_east = lax.ppermute(to_west, axes, lon_pairs(nlon, nlat, -1))  4.27 us
    ppermute x1, starting transfers between devices, local(): got_west = lax.ppermute(to_east, axes, lon_pairs(nlon, nlat, 1))  3.82 us
    pallas_call x1, Pallas kernels, local(): pl.pallas_call(outer_kernel, out_shape=state, in_specs=[vmem()] * 10, out...  2.89 us
    pallas_call x2, Pallas kernels, inner_call(): pl.pallas_call(functools.partial(inner_kernel, early), out_shape=(state,...  2.87 us
    ppermute x1, starting transfers between devices, local(): got_odd = lax.ppermute(to_odd, axes, lat_pairs(nlon, nlat, True))  2.22 us
    pallas_call x1, Pallas kernels, local(): pl.pallas_call(rows_kernel, out_shape=(rows, rows), in_specs=[pl.BlockSpe...  1.67 us
  transfers between devices with their start and end apart: 4, of which 1 were waited for; matrix products, arithmetic and copies ran while one was open for 0% of the time, Pallas kernels for 11%

profile of v5, /device:TPU:28, one launch (start us, length us, event | category | flops | bytes accessed | tf_op | source)
XLA Modules:
  0.0 31.5 jit_solution(11920334265232014684)
XLA Ops:
  0.0 0.0 copy-start.3
  0.0 0.0 copy-start.2
  0.0 0.0 copy-start.1
  0.0 0.0 copy-start
  0.8 1.7 %rows.1 = (f32[56,128]{1,0:T(8,128)}, f32[56,128]{1,0:T(8,128)}) custom-call(f32[24,128,128]{2,1,0:T(8,128)} %bitcast.1, f32[2,128,128]{2,1,0:T(8,128)} %w.7, f32[128,128]{1,0:T(8,128)} %area.7, s32[128,128]{1,0:T(8,128)} %mask.7, s32[1,1]{1,0:T(1,128)S(6)} %copy.7.land), custom_call_target="tpu_custom_call" | custom-call | flops 65536 | bytes 262144 | tf_op jit(solution)/shard_map/rows/pallas_call | solution.py:396
  2.5 0.0 copy-start.5
  2.5 0.0 copy-start.6
  2.5 2.2 %collective-permute-start = (f32[56,128]{1,0:T(8,128)}, f32[56,128]{1,0:T(8,128)S(1)}, u32[]{:S(2)}, u32[]{:S(2)}) collective-permute-start(f32[56,128]{1,0:T(8,128)} %get-tuple-element.19.to_odd), channel_id=1, source_target_pairs={{1,2},{2,1},{3,4},{4,3},{5,6},{6,5},{7,8},{8,7},{9,10},{10,9},{11,... | collective-permute-start | bytes 86024 | tf_op jit(solution)/shard_map/lat_odd/ppermute | solution.py:414
  4.7 11.4 %collective-permute-start.1 = (f32[56,128]{1,0:T(8,128)}, f32[56,128]{1,0:T(8,128)S(1)}, u32[]{:S(2)}, u32[]{:S(2)}) collective-permute-start(f32[56,128]{1,0:T(8,128)} %get-tuple-element.20.to_even), channel_id=1, source_target_pairs={{0,1},{1,0},{2,3},{3,2},{4,5},{5,4},{6,7},{7,6},{8,9},{9,8},{10,11... | collective-permute-start | bytes 86024 | tf_op jit(solution)/shard_map/lat_even/ppermute | solution.py:416
  16.1 0.0 copy-done.3
  16.2 0.0 copy-done.2
  16.2 0.0 copy-done.1
  16.2 0.0 copy-done
  16.2 0.5 %columns.1.pack = f32[128,128]{1,0:T(8,128)S(1)} custom-call(f32[24,128,128]{2,1,0:T(8,128)S(1)} %bitcast.2, f32[2,128,128]{2,1,0:T(8,128)S(1)} %copy-done.1, f32[128,128]{1,0:T(8,128)S(1)} %copy-done.2, s32[128,128]{1,0:T(8,128)S(1)} %copy-done.3, s32[1,1]{1,0:T(1,128)S(6)} %copy.7.land), custom_call_target="tpu_custom_call" | custom-call | flops 1048576 | bytes 2097152 | tf_op jit(solution)/shard_map/columns/pallas_call | solution.py:419
  16.7 0.0 collective-permute-done.got_odd
  16.7 0.4 %collective-permute-done.1.got_even = f32[56,128]{1,0:T(8,128)S(1)} collective-permute-done((f32[56,128]{1,0:T(8,128)}, f32[56,128]{1,0:T(8,128)S(1)}, u32[]{:S(2)}, u32[]{:S(2)}) %collective-permute-start.1) | collective-permute-done | bytes 28704 | tf_op jit(solution)/shard_map/lat_even/ppermute | solution.py:416
  17.2 0.0 copy-done.5
  17.2 0.0 copy-done.6
  17.2 0.4 %strips.1 = (f32[128,128]{1,0:T(8,128)S(1)}, f32[64,128]{1,0:T(8,128)S(1)}, f32[64,128]{1,0:T(8,128)S(1)}, f32[112,128]{1,0:T(8,128)S(1)}, f32[112,128]{1,0:T(8,128)S(1)}) custom-call(f32[56,128]{1,0:T(8,128)S(1)} %copy-done.5, f32[56,128]{1,0:T(8,128)S(1)} %copy-done.6, f32[56,128]{1,0:T(8,128)S(1)} %collective-permute-done.got_odd, ...), custom_call_target="tpu_custom_call" | custom-call | flops 262144 | bytes 262144 | tf_op jit(solution)/shard_map/strips/pallas_call | solution.py:429
  17.6 3.8 %collective-permute-start.2 = (f32[64,128]{1,0:T(8,128)S(1)}, f32[64,128]{1,0:T(8,128)S(1)}, u32[]{:S(2)}, u32[]{:S(2)}) collective-permute-start(f32[64,128]{1,0:T(8,128)S(1)} %get-tuple-element.22), channel_id=1, source_target_pairs={{0,16},{1,17},{2,18},{3,19},{4,20},{5,21},{6,22},{7,23},{8,24},{9,... | collective-permute-start | bytes 98312 | tf_op jit(solution)/shard_map/lon_east/ppermute | solution.py:441
  21.4 0.0 copy-start.4
  21.4 4.3 %collective-permute-start.3 = (f32[64,128]{1,0:T(8,128)S(1)}, f32[64,128]{1,0:T(8,128)S(1)}, u32[]{:S(2)}, u32[]{:S(2)}) collective-permute-start(f32[64,128]{1,0:T(8,128)S(1)} %get-tuple-element.28), channel_id=1, source_target_pairs={{0,496},{1,497},{2,498},{3,499},{4,500},{5,501},{6,502},{7,503},{8... | collective-permute-start | bytes 98312 | tf_op jit(solution)/shard_map/lon_west/ppermute | solution.py:467
  25.7 2.8 %inner_late.1 = (f32[6,4,128,128]{3,2,1,0:T(8,128)S(1)}, f32[128,128]{1,0:T(8,128)S(1)}) custom-call(f32[6,4,128,128]{3,2,1,0:T(8,128)S(1)} %copy-done, f32[2,128,128]{2,1,0:T(8,128)S(1)} %copy-done.1, f32[128,128]{1,0:T(8,128)S(1)} %copy-done.2, s32[128,128]{1,0:T(8,128)S(1)} %copy-done.3, s32[1,1]{1,0:T(1,128)S(6)} %copy.7.land, ...), custom_call_target="tpu_custom_call" | custom-call | flops 20971520 | bytes 4194304 | tf_op jit(solution)/shard_map/inner_late/pallas_call | solution.py:448
  28.6 0.0 collective-permute-done.2.got_west
  28.6 0.0 collective-permute-done.3.got_east
  28.6 0.0 copy-done.4
  28.6 2.9 %outer.1 = f32[6,4,128,128]{3,2,1,0:T(8,128)} custom-call(f32[128,128]{1,0:T(8,128)S(1)} %get-tuple-element.21.pack, f32[64,128]{1,0:T(8,128)S(1)} %collective-permute-done.2.got_west, f32[64,128]{1,0:T(8,128)S(1)} %collective-permute-done.3.got_east, f32[112,128]{1,0:T(8,128)S(1)} %get-tuple-element.24.north, f32[112,128]{1,0:T(8,128)S(1)} %get-tuple-element.25.south, ...), custom_call_target="tpu_custom_call" | custom-call | flops 1048576 | bytes 4194304 | tf_op jit(solution)/shard_map/outer/pallas_call | solution.py:470
  (1 shorter events, 0.0 us)
Async XLA Ops:
  0.0 16.1 %copy-start.3 = (s32[128,128]{1,0:T(8,128)S(1)}, s32[128,128]{1,0:T(8,128)}, u32[]{:S(2)}) copy-start(s32[128,128]{1,0:T(8,128)} %mask.7) | copy-start | bytes 196612
  0.0 16.1 %copy-start.2 = (f32[128,128]{1,0:T(8,128)S(1)}, f32[128,128]{1,0:T(8,128)}, u32[]{:S(2)}) copy-start(f32[128,128]{1,0:T(8,128)} %area.7) | copy-start | bytes 196612
  0.0 16.2 %copy-start.1 = (f32[2,128,128]{2,1,0:T(8,128)S(1)}, f32[2,128,128]{2,1,0:T(8,128)}, u32[]{:S(2)}) copy-start(f32[2,128,128]{2,1,0:T(8,128)} %w.7) | copy-start | bytes 393220
  0.0 16.2 %copy-start = (f32[6,4,128,128]{3,2,1,0:T(8,128)S(1)}, f32[6,4,128,128]{3,2,1,0:T(8,128)}, u32[]{:S(2)}) copy-start(f32[6,4,128,128]{3,2,1,0:T(8,128)} %fields.3) | copy-start | bytes 4718596
  2.5 14.7 %copy-start.5 = (f32[56,128]{1,0:T(8,128)S(1)}, f32[56,128]{1,0:T(8,128)}, u32[]{:S(2)}) copy-start(f32[56,128]{1,0:T(8,128)} %get-tuple-element.19.to_odd) | copy-start | bytes 86020
  2.5 14.7 %copy-start.6 = (f32[56,128]{1,0:T(8,128)S(1)}, f32[56,128]{1,0:T(8,128)}, u32[]{:S(2)}) copy-start(f32[56,128]{1,0:T(8,128)} %get-tuple-element.20.to_even) | copy-start | bytes 86020
  2.5 14.2 %collective-permute-start = (f32[56,128]{1,0:T(8,128)}, f32[56,128]{1,0:T(8,128)S(1)}, u32[]{:S(2)}, u32[]{:S(2)}) collective-permute-start(f32[56,128]{1,0:T(8,128)} %get-tuple-element.19.to_odd), channel_id=1, source_target_pairs={{1,2},{2,1},{3,4},{4,3},{5,6},{6,5},{7,8},{8,7},{9,10},{10,9},{11,... | collective-permute-start | bytes 86024 | tf_op jit(solution)/shard_map/lat_odd/ppermute | solution.py:414
  4.7 12.5 %collective-permute-start.1 = (f32[56,128]{1,0:T(8,128)}, f32[56,128]{1,0:T(8,128)S(1)}, u32[]{:S(2)}, u32[]{:S(2)}) collective-permute-start(f32[56,128]{1,0:T(8,128)} %get-tuple-element.20.to_even), channel_id=1, source_target_pairs={{0,1},{1,0},{2,3},{3,2},{4,5},{5,4},{6,7},{7,6},{8,9},{9,8},{10,11... | collective-permute-start | bytes 86024 | tf_op jit(solution)/shard_map/lat_even/ppermute | solution.py:416
  17.6 11.0 %collective-permute-start.2 = (f32[64,128]{1,0:T(8,128)S(1)}, f32[64,128]{1,0:T(8,128)S(1)}, u32[]{:S(2)}, u32[]{:S(2)}) collective-permute-start(f32[64,128]{1,0:T(8,128)S(1)} %get-tuple-element.22), channel_id=1, source_target_pairs={{0,16},{1,17},{2,18},{3,19},{4,20},{5,21},{6,22},{7,23},{8,24},{9,... | collective-permute-start | bytes 98312 | tf_op jit(solution)/shard_map/lon_east/ppermute | solution.py:441
  21.4 7.2 %copy-start.4 = (bf16[128,896]{1,0:T(8,128)(2,1)S(1)}, bf16[128,896]{1,0:T(8,128)(2,1)}, u32[]{:S(2)}) copy-start(bf16[128,896]{1,0:T(8,128)(2,1)} %constant.2.clone.matrix) | copy-start | bytes 688132
  21.4 7.1 %collective-permute-start.3 = (f32[64,128]{1,0:T(8,128)S(1)}, f32[64,128]{1,0:T(8,128)S(1)}, u32[]{:S(2)}, u32[]{:S(2)}) collective-permute-start(f32[64,128]{1,0:T(8,128)S(1)} %get-tuple-element.28), channel_id=1, source_target_pairs={{0,496},{1,497},{2,498},{3,499},{4,500},{5,501},{6,502},{7,503},{8... | collective-permute-start | bytes 98312 | tf_op jit(solution)/shard_map/lon_west/ppermute | solution.py:467

commit v6 on v5

--- a/solution.py
+++ b/solution.py
@@ -186,8 +186,7 @@
 
 
 def runs_early():
-    first = lax.axis_index("lon") % (lax.axis_size("lon") // 2) == 0
-    return first & (lax.axis_index("lat") < lax.axis_size("lat") - 2)
+    return lax.axis_index("lon") % (lax.axis_size("lon") // 2) == 0
 
 
 def inner_kernel(early, fields, w, area, mask, land, north, south, *refs):
@@ -273,7 +272,7 @@
         )):
             for i in src:
                 out[n, i, l] = 1.0
-    return np.concatenate(list(out), axis=1)
+    return np.tile(np.concatenate(list(out), axis=1), (2, 1))
 
 
 def spread(x, matrix):
@@ -282,7 +281,7 @@
     mid = rest.astype(jnp.bfloat16)
     lo = (rest - mid.astype(F32)).astype(jnp.bfloat16)
     dot = functools.partial(jnp.dot, preferred_element_type=F32)
-    return dot(lo, matrix) + dot(mid, matrix) + dot(hi, matrix)
+    return dot(lo, matrix[0:128]) + dot(jnp.concatenate([hi, mid], axis=1), matrix)
 
 
 def outer_kernel(pack, got_west, got_east, north, south, inner_a, inner_b, ends_a, ends_b, matrix, out_hbm,
@@ -405,9 +404,10 @@
             pltpu.VMEM((2, 8, 128), jnp.int32),
             pltpu.SemaphoreType.DMA((8,)),
         ],
+        compiler_params=params,
         cost_estimate=cost(1 << 18, 1 << 16),
         name="rows",
-    )(planes, weights, area, mask, land)
+    )(*(pltpu.with_memory_space_constraint(x, pltpu.HBM) for x in (planes, weights, area, mask)), land)
 
     axes = ("lon", "lat")
     with jax.named_scope("lat_odd"):

time: 32 us -> 32.2 us (level)
  waiting for transfers between devices: 0.45 us -> 4.08 us
  starting transfers between devices: 21.7 us -> 19.2 us
  Pallas kernels: 8.35 us -> 7.69 us
    ppermute x1, waiting for transfers between devices: 0.01 us -> 3.84 us  [local(): got_east = lax.ppermute(to_west, axes, lon_pairs(nlon, nlat, -1))]
    ppermute x1, starting transfers between devices: 4.27 us -> 1.92 us  [local(): got_east = lax.ppermute(to_west, axes, lon_pairs(nlon, nlat, -1))]
    pallas_call x1, Pallas kernels: 1.67 us -> 1.05 us  [local(): pl.pallas_call(rows_kernel, out_shape=(rows, rows), in_specs=[pl.BlockSpe...]
  transfers between devices with their start and end apart: 4 -> 4, of which waited for: 1 -> 2; matrix products, arithmetic and copies ran while one was open for 0% -> 0% of each run, Pallas kernels for 11% -> 11%
where the time goes in v6:
time: 32.2 us; the launch traced here: 31.9 us
  starting transfers between devices  19.2 us (60%)
  Pallas kernels  7.69 us (24%)
  waiting for transfers between devices  4.08 us (13%)
  between operations  0.91 us (3%)
    ppermute x1, starting transfers between devices, local(): got_even = lax.ppermute(to_even, axes, lat_pairs(nlon, nlat, False))  11.4 us
    ppermute x1, waiting for transfers between devices, local(): got_east = lax.ppermute(to_west, axes, lon_pairs(nlon, nlat, -1))  3.84 us
    ppermute x1, starting transfers between devices, local(): got_west = lax.ppermute(to_east, axes, lon_pairs(nlon, nlat, 1))  3.82 us
    pallas_call x2, Pallas kernels, inner_call(): pl.pallas_call(functools.partial(inner_kernel, early), out_shape=(state,...  2.87 us
    pallas_call x1, Pallas kernels, local(): pl.pallas_call(outer_kernel, out_shape=state, in_specs=[vmem()] * 10, out...  2.86 us
    ppermute x1, starting transfers between devices, local(): got_odd = lax.ppermute(to_odd, axes, lat_pairs(nlon, nlat, True))  2.09 us
    ppermute x1, starting transfers between devices, local(): got_east = lax.ppermute(to_west, axes, lon_pairs(nlon, nlat, -1))  1.92 us
    pallas_call x1, Pallas kernels, local(): pl.pallas_call(rows_kernel, out_shape=(rows, rows), in_specs=[pl.BlockSpe...  1.05 us
  transfers between devices with their start and end apart: 4, of which 2 were waited for; matrix products, arithmetic and copies ran while one was open for 0% of the time, Pallas kernels for 11%

profile of v6, /device:TPU:28, one launch (start us, length us, event | category | flops | bytes accessed | tf_op | source)
XLA Modules:
  0.0 31.9 jit_solution(16301902161753988375)
XLA Ops:
  0.0 0.0 copy-start.3
  0.0 0.0 copy-start.2
  0.0 0.0 copy-start.1
  0.0 0.0 copy-start
  0.8 1.0 %rows.1 = (f32[56,128]{1,0:T(8,128)S(1)}, f32[56,128]{1,0:T(8,128)S(1)}) custom-call(f32[24,128,128]{2,1,0:T(8,128)} %bitcast.1, f32[2,128,128]{2,1,0:T(8,128)} %w.7, f32[128,128]{1,0:T(8,128)} %area.7, s32[128,128]{1,0:T(8,128)} %mask.7, s32[1,1]{1,0:T(1,128)S(6)} %copy.7.land), custom_call_target="tpu_custom_call" | custom-call | flops 65536 | bytes 262144 | tf_op jit(solution)/shard_map/rows/pallas_call | solution.py:395
  1.9 2.1 %collective-permute-start = (f32[56,128]{1,0:T(8,128)S(1)}, f32[56,128]{1,0:T(8,128)S(1)}, u32[]{:S(2)}, u32[]{:S(2)}) collective-permute-start(f32[56,128]{1,0:T(8,128)S(1)} %get-tuple-element.19.to_odd), channel_id=1, source_target_pairs={{1,2},{2,1},{3,4},{4,3},{5,6},{6,5},{7,8},{8,7},{9,10},{10,9},{11,... | collective-permute-start | bytes 86024 | tf_op jit(solution)/shard_map/lat_odd/ppermute | solution.py:414
  4.0 11.4 %collective-permute-start.1 = (f32[56,128]{1,0:T(8,128)S(1)}, f32[56,128]{1,0:T(8,128)S(1)}, u32[]{:S(2)}, u32[]{:S(2)}) collective-permute-start(f32[56,128]{1,0:T(8,128)S(1)} %get-tuple-element.20.to_even), channel_id=1, source_target_pairs={{0,1},{1,0},{2,3},{3,2},{4,5},{5,4},{6,7},{7,6},{8,9},{9,8},{10,11... | collective-permute-start | bytes 86024 | tf_op jit(solution)/shard_map/lat_even/ppermute | solution.py:416
  15.4 0.0 copy-done.3
  15.4 0.0 copy-done.2
  15.4 0.0 copy-done.1
  15.4 0.0 copy-done
  15.4 0.5 %columns.1.pack = f32[128,128]{1,0:T(8,128)S(1)} custom-call(f32[24,128,128]{2,1,0:T(8,128)S(1)} %bitcast.2, f32[2,128,128]{2,1,0:T(8,128)S(1)} %copy-done.1, f32[128,128]{1,0:T(8,128)S(1)} %copy-done.2, s32[128,128]{1,0:T(8,128)S(1)} %copy-done.3, s32[1,1]{1,0:T(1,128)S(6)} %copy.7.land), custom_call_target="tpu_custom_call" | custom-call | flops 1048576 | bytes 2097152 | tf_op jit(solution)/shard_map/columns/pallas_call | solution.py:419
  16.0 0.0 collective-permute-done.got_odd
  16.0 0.2 collective-permute-done.1.got_even
  16.2 0.4 %strips.1 = (f32[128,128]{1,0:T(8,128)S(1)}, f32[64,128]{1,0:T(8,128)S(1)}, f32[64,128]{1,0:T(8,128)S(1)}, f32[112,128]{1,0:T(8,128)S(1)}, f32[112,128]{1,0:T(8,128)S(1)}) custom-call(f32[56,128]{1,0:T(8,128)S(1)} %get-tuple-element.19.to_odd, f32[56,128]{1,0:T(8,128)S(1)} %get-tuple-element.20.to_even, f32[56,128]{1,0:T(8,128)S(1)} %collective-permute-done.got_odd, ...), custom_call_target="tpu_custom_call" | custom-call | flops 262144 | bytes 262144 | tf_op jit(solution)/shard_map/strips/pallas_call | solution.py:429
  16.6 3.8 %collective-permute-start.2 = (f32[64,128]{1,0:T(8,128)S(1)}, f32[64,128]{1,0:T(8,128)S(1)}, u32[]{:S(2)}, u32[]{:S(2)}) collective-permute-start(f32[64,128]{1,0:T(8,128)S(1)} %get-tuple-element.22), channel_id=1, source_target_pairs={{0,16},{1,17},{2,18},{3,19},{4,20},{5,21},{6,22},{7,23},{8,24},{9,... | collective-permute-start | bytes 98312 | tf_op jit(solution)/shard_map/lon_east/ppermute | solution.py:441
  20.4 0.0 copy-start.4
  20.4 2.9 %inner_early.1 = (f32[6,4,128,128]{3,2,1,0:T(8,128)S(1)}, f32[128,128]{1,0:T(8,128)S(1)}) custom-call(f32[6,4,128,128]{3,2,1,0:T(8,128)S(1)} %copy-done, f32[2,128,128]{2,1,0:T(8,128)S(1)} %copy-done.1, f32[128,128]{1,0:T(8,128)S(1)} %copy-done.2, s32[128,128]{1,0:T(8,128)S(1)} %copy-done.3, s32[1,1]{1,0:T(1,128)S(6)} %copy.7.land, ...), custom_call_target="tpu_custom_call" | custom-call | flops 20971520 | bytes 4194304 | tf_op jit(solution)/shard_map/inner_early/pallas_call | solution.py:448
  23.3 1.9 %collective-permute-start.3 = (f32[64,128]{1,0:T(8,128)S(1)}, f32[64,128]{1,0:T(8,128)S(1)}, u32[]{:S(2)}, u32[]{:S(2)}) collective-permute-start(f32[64,128]{1,0:T(8,128)S(1)} %get-tuple-element.28), channel_id=1, source_target_pairs={{0,496},{1,497},{2,498},{3,499},{4,500},{5,501},{6,502},{7,503},{8... | collective-permute-start | bytes 98312 | tf_op jit(solution)/shard_map/lon_west/ppermute | solution.py:467
  25.2 0.0 collective-permute-done.2.got_west
  25.2 3.8 %collective-permute-done.3.got_east = f32[64,128]{1,0:T(8,128)S(1)} collective-permute-done((f32[64,128]{1,0:T(8,128)S(1)}, f32[64,128]{1,0:T(8,128)S(1)}, u32[]{:S(2)}, u32[]{:S(2)}) %collective-permute-start.3) | collective-permute-done | bytes 32800 | tf_op jit(solution)/shard_map/lon_west/ppermute | solution.py:467
  29.1 0.0 copy-done.4
  29.1 2.9 %outer.1 = f32[6,4,128,128]{3,2,1,0:T(8,128)} custom-call(f32[128,128]{1,0:T(8,128)S(1)} %get-tuple-element.21.pack, f32[64,128]{1,0:T(8,128)S(1)} %collective-permute-done.2.got_west, f32[64,128]{1,0:T(8,128)S(1)} %collective-permute-done.3.got_east, f32[112,128]{1,0:T(8,128)S(1)} %get-tuple-element.24.north, f32[112,128]{1,0:T(8,128)S(1)} %get-tuple-element.25.south, ...), custom_call_target="tpu_custom_call" | custom-call | flops 1048576 | bytes 4194304 | tf_op jit(solution)/shard_map/outer/pallas_call | solution.py:470
  (1 shorter events, 0.0 us)
Async XLA Ops:
  0.0 15.4 %copy-start.3 = (s32[128,128]{1,0:T(8,128)S(1)}, s32[128,128]{1,0:T(8,128)}, u32[]{:S(2)}) copy-start(s32[128,128]{1,0:T(8,128)} %mask.7) | copy-start | bytes 196612
  0.0 15.4 %copy-start.2 = (f32[128,128]{1,0:T(8,128)S(1)}, f32[128,128]{1,0:T(8,128)}, u32[]{:S(2)}) copy-start(f32[128,128]{1,0:T(8,128)} %area.7) | copy-start | bytes 196612
  0.0 15.4 %copy-start.1 = (f32[2,128,128]{2,1,0:T(8,128)S(1)}, f32[2,128,128]{2,1,0:T(8,128)}, u32[]{:S(2)}) copy-start(f32[2,128,128]{2,1,0:T(8,128)} %w.7) | copy-start | bytes 393220
  0.0 15.4 %copy-start = (f32[6,4,128,128]{3,2,1,0:T(8,128)S(1)}, f32[6,4,128,128]{3,2,1,0:T(8,128)}, u32[]{:S(2)}) copy-start(f32[6,4,128,128]{3,2,1,0:T(8,128)} %fields.3) | copy-start | bytes 4718596
  1.9 14.1 %collective-permute-start = (f32[56,128]{1,0:T(8,128)S(1)}, f32[56,128]{1,0:T(8,128)S(1)}, u32[]{:S(2)}, u32[]{:S(2)}) collective-permute-start(f32[56,128]{1,0:T(8,128)S(1)} %get-tuple-element.19.to_odd), channel_id=1, source_target_pairs={{1,2},{2,1},{3,4},{4,3},{5,6},{6,5},{7,8},{8,7},{9,10},{10,9},{11,... | collective-permute-start | bytes 86024 | tf_op jit(solution)/shard_map/lat_odd/ppermute | solution.py:414
  4.0 12.2 %collective-permute-start.1 = (f32[56,128]{1,0:T(8,128)S(1)}, f32[56,128]{1,0:T(8,128)S(1)}, u32[]{:S(2)}, u32[]{:S(2)}) collective-permute-start(f32[56,128]{1,0:T(8,128)S(1)} %get-tuple-element.20.to_even), channel_id=1, source_target_pairs={{0,1},{1,0},{2,3},{3,2},{4,5},{5,4},{6,7},{7,6},{8,9},{9,8},{10,11... | collective-permute-start | bytes 86024 | tf_op jit(solution)/shard_map/lat_even/ppermute | solution.py:416
  16.6 8.7 %collective-permute-start.2 = (f32[64,128]{1,0:T(8,128)S(1)}, f32[64,128]{1,0:T(8,128)S(1)}, u32[]{:S(2)}, u32[]{:S(2)}) collective-permute-start(f32[64,128]{1,0:T(8,128)S(1)} %get-tuple-element.22), channel_id=1, source_target_pairs={{0,16},{1,17},{2,18},{3,19},{4,20},{5,21},{6,22},{7,23},{8,24},{9,... | collective-permute-start | bytes 98312 | tf_op jit(solution)/shard_map/lon_east/ppermute | solution.py:441
  20.4 8.7 %copy-start.4 = (bf16[256,896]{1,0:T(8,128)(2,1)S(1)}, bf16[256,896]{1,0:T(8,128)(2,1)}, u32[]{:S(2)}) copy-start(bf16[256,896]{1,0:T(8,128)(2,1)} %constant.2.clone.matrix) | copy-start | bytes 1376260
  23.3 5.8 %collective-permute-start.3 = (f32[64,128]{1,0:T(8,128)S(1)}, f32[64,128]{1,0:T(8,128)S(1)}, u32[]{:S(2)}, u32[]{:S(2)}) collective-permute-start(f32[64,128]{1,0:T(8,128)S(1)} %get-tuple-element.28), channel_id=1, source_target_pairs={{0,496},{1,497},{2,498},{3,499},{4,500},{5,501},{6,502},{7,503},{8... | collective-permute-start | bytes 98312 | tf_op jit(solution)/shard_map/lon_west/ppermute | solution.py:467

commit v7 on v6

--- a/solution.py
+++ b/solution.py
@@ -186,7 +186,8 @@
 
 
 def runs_early():
-    return lax.axis_index("lon") % (lax.axis_size("lon") // 2) == 0
+    first = lax.axis_index("lon") % (lax.axis_size("lon") // 2) == 0
+    return first & (lax.axis_index("lat") < lax.axis_size("lat") - 2)
 
 
 def inner_kernel(early, fields, w, area, mask, land, north, south, *refs):

time: 32.2 us -> 30.9 us (0.960)
  the two profiles are of different devices: /device:TPU:28 before, /device:TPU:124 now
where the time goes in v7:
time: 30.9 us; the launch traced here: 30.7 us
  starting transfers between devices  19.6 us (63%)
  Pallas kernels  7.64 us (25%)
  waiting for transfers between devices  2.46 us (8%)
  between operations  0.91 us (3%)
    ppermute x1, starting transfers between devices, local(): got_even = lax.ppermute(to_even, axes, lat_pairs(nlon, nlat, False))  11.4 us
    ppermute x1, starting transfers between devices, local(): got_west = lax.ppermute(to_east, axes, lon_pairs(nlon, nlat, 1))  4.13 us
    pallas_call x2, Pallas kernels, inner_call(): pl.pallas_call(functools.partial(inner_kernel, early), out_shape=(state,...  2.88 us
    pallas_call x1, Pallas kernels, local(): pl.pallas_call(outer_kernel, out_shape=state, in_specs=[vmem()] * 10, out...  2.8 us
    ppermute x1, waiting for transfers between devices, local(): got_east = lax.ppermute(to_west, axes, lon_pairs(nlon, nlat, -1))  2.22 us
    ppermute x1, starting transfers between devices, local(): got_odd = lax.ppermute(to_odd, axes, lat_pairs(nlon, nlat, True))  2.09 us
    ppermute x1, starting transfers between devices, local(): got_east = lax.ppermute(to_west, axes, lon_pairs(nlon, nlat, -1))  2.05 us
    pallas_call x1, Pallas kernels, local(): pl.pallas_call(rows_kernel, out_shape=(rows, rows), in_specs=[pl.BlockSpe...  1.05 us
  transfers between devices with their start and end apart: 4, of which 2 were waited for; matrix products, arithmetic and copies ran while one was open for 0% of the time, Pallas kernels for 11%

profile of v7, /device:TPU:124, one launch (start us, length us, event | category | flops | bytes accessed | tf_op | source)
XLA Modules:
  0.0 30.7 jit_solution(12180209574005261117)
XLA Ops:
  0.0 0.0 copy-start.3
  0.0 0.0 copy-start.2
  0.0 0.0 copy-start.1
  0.0 0.0 copy-start
  0.8 1.0 %rows.1 = (f32[56,128]{1,0:T(8,128)S(1)}, f32[56,128]{1,0:T(8,128)S(1)}) custom-call(f32[24,128,128]{2,1,0:T(8,128)} %bitcast.1, f32[2,128,128]{2,1,0:T(8,128)} %w.7, f32[128,128]{1,0:T(8,128)} %area.7, s32[128,128]{1,0:T(8,128)} %mask.7, s32[1,1]{1,0:T(1,128)S(6)} %copy.7.land), custom_call_target="tpu_custom_call" | custom-call | flops 65536 | bytes 262144 | tf_op jit(solution)/shard_map/rows/pallas_call | solution.py:396
  1.9 2.1 %collective-permute-start = (f32[56,128]{1,0:T(8,128)S(1)}, f32[56,128]{1,0:T(8,128)S(1)}, u32[]{:S(2)}, u32[]{:S(2)}) collective-permute-start(f32[56,128]{1,0:T(8,128)S(1)} %get-tuple-element.19.to_odd), channel_id=1, source_target_pairs={{1,2},{2,1},{3,4},{4,3},{5,6},{6,5},{7,8},{8,7},{9,10},{10,9},{11,... | collective-permute-start | bytes 86024 | tf_op jit(solution)/shard_map/lat_odd/ppermute | solution.py:415
  4.0 11.4 %collective-permute-start.1 = (f32[56,128]{1,0:T(8,128)S(1)}, f32[56,128]{1,0:T(8,128)S(1)}, u32[]{:S(2)}, u32[]{:S(2)}) collective-permute-start(f32[56,128]{1,0:T(8,128)S(1)} %get-tuple-element.20.to_even), channel_id=1, source_target_pairs={{0,1},{1,0},{2,3},{3,2},{4,5},{5,4},{6,7},{7,6},{8,9},{9,8},{10,11... | collective-permute-start | bytes 86024 | tf_op jit(solution)/shard_map/lat_even/ppermute | solution.py:417
  15.3 0.0 copy-done.3
  15.3 0.0 copy-done.2
  15.4 0.0 copy-done.1
  15.4 0.0 copy-done
  15.4 0.5 %columns.1.pack = f32[128,128]{1,0:T(8,128)S(1)} custom-call(f32[24,128,128]{2,1,0:T(8,128)S(1)} %bitcast.2, f32[2,128,128]{2,1,0:T(8,128)S(1)} %copy-done.1, f32[128,128]{1,0:T(8,128)S(1)} %copy-done.2, s32[128,128]{1,0:T(8,128)S(1)} %copy-done.3, s32[1,1]{1,0:T(1,128)S(6)} %copy.7.land), custom_call_target="tpu_custom_call" | custom-call | flops 1048576 | bytes 2097152 | tf_op jit(solution)/shard_map/columns/pallas_call | solution.py:420
  15.9 0.0 collective-permute-done.got_odd
  15.9 0.2 collective-permute-done.1.got_even
  16.2 0.4 %strips.1 = (f32[128,128]{1,0:T(8,128)S(1)}, f32[64,128]{1,0:T(8,128)S(1)}, f32[64,128]{1,0:T(8,128)S(1)}, f32[112,128]{1,0:T(8,128)S(1)}, f32[112,128]{1,0:T(8,128)S(1)}) custom-call(f32[56,128]{1,0:T(8,128)S(1)} %get-tuple-element.19.to_odd, f32[56,128]{1,0:T(8,128)S(1)} %get-tuple-element.20.to_even, f32[56,128]{1,0:T(8,128)S(1)} %collective-permute-done.got_odd, ...), custom_call_target="tpu_custom_call" | custom-call | flops 262144 | bytes 262144 | tf_op jit(solution)/shard_map/strips/pallas_call | solution.py:430
  16.5 4.1 %collective-permute-start.2 = (f32[64,128]{1,0:T(8,128)S(1)}, f32[64,128]{1,0:T(8,128)S(1)}, u32[]{:S(2)}, u32[]{:S(2)}) collective-permute-start(f32[64,128]{1,0:T(8,128)S(1)} %get-tuple-element.22), channel_id=1, source_target_pairs={{0,16},{1,17},{2,18},{3,19},{4,20},{5,21},{6,22},{7,23},{8,24},{9,... | collective-permute-start | bytes 98312 | tf_op jit(solution)/shard_map/lon_east/ppermute | solution.py:442
  20.7 0.0 copy-start.4
  20.7 2.1 %collective-permute-start.3 = (f32[64,128]{1,0:T(8,128)S(1)}, f32[64,128]{1,0:T(8,128)S(1)}, u32[]{:S(2)}, u32[]{:S(2)}) collective-permute-start(f32[64,128]{1,0:T(8,128)S(1)} %get-tuple-element.28), channel_id=1, source_target_pairs={{0,496},{1,497},{2,498},{3,499},{4,500},{5,501},{6,502},{7,503},{8... | collective-permute-start | bytes 98312 | tf_op jit(solution)/shard_map/lon_west/ppermute | solution.py:468
  22.8 2.9 %inner_late.1 = (f32[6,4,128,128]{3,2,1,0:T(8,128)S(1)}, f32[128,128]{1,0:T(8,128)S(1)}) custom-call(f32[6,4,128,128]{3,2,1,0:T(8,128)S(1)} %copy-done, f32[2,128,128]{2,1,0:T(8,128)S(1)} %copy-done.1, f32[128,128]{1,0:T(8,128)S(1)} %copy-done.2, s32[128,128]{1,0:T(8,128)S(1)} %copy-done.3, s32[1,1]{1,0:T(1,128)S(6)} %copy.7.land, ...), custom_call_target="tpu_custom_call" | custom-call | flops 20971520 | bytes 4194304 | tf_op jit(solution)/shard_map/inner_late/pallas_call | solution.py:449
  25.6 0.0 collective-permute-done.2.got_west
  25.7 2.2 %collective-permute-done.3.got_east = f32[64,128]{1,0:T(8,128)S(1)} collective-permute-done((f32[64,128]{1,0:T(8,128)S(1)}, f32[64,128]{1,0:T(8,128)S(1)}, u32[]{:S(2)}, u32[]{:S(2)}) %collective-permute-start.3) | collective-permute-done | bytes 32800 | tf_op jit(solution)/shard_map/lon_west/ppermute | solution.py:468
  27.9 0.0 copy-done.4
  27.9 2.8 %outer.1 = f32[6,4,128,128]{3,2,1,0:T(8,128)} custom-call(f32[128,128]{1,0:T(8,128)S(1)} %get-tuple-element.21.pack, f32[64,128]{1,0:T(8,128)S(1)} %collective-permute-done.2.got_west, f32[64,128]{1,0:T(8,128)S(1)} %collective-permute-done.3.got_east, f32[112,128]{1,0:T(8,128)S(1)} %get-tuple-element.24.north, f32[112,128]{1,0:T(8,128)S(1)} %get-tuple-element.25.south, ...), custom_call_target="tpu_custom_call" | custom-call | flops 1048576 | bytes 4194304 | tf_op jit(solution)/shard_map/outer/pallas_call | solution.py:471
  (1 shorter events, 0.0 us)
Async XLA Ops:
  0.0 15.3 %copy-start.3 = (s32[128,128]{1,0:T(8,128)S(1)}, s32[128,128]{1,0:T(8,128)}, u32[]{:S(2)}) copy-start(s32[128,128]{1,0:T(8,128)} %mask.7) | copy-start | bytes 196612
  0.0 15.3 %copy-start.2 = (f32[128,128]{1,0:T(8,128)S(1)}, f32[128,128]{1,0:T(8,128)}, u32[]{:S(2)}) copy-start(f32[128,128]{1,0:T(8,128)} %area.7) | copy-start | bytes 196612
  0.0 15.4 %copy-start.1 = (f32[2,128,128]{2,1,0:T(8,128)S(1)}, f32[2,128,128]{2,1,0:T(8,128)}, u32[]{:S(2)}) copy-start(f32[2,128,128]{2,1,0:T(8,128)} %w.7) | copy-start | bytes 393220
  0.0 15.4 %copy-start = (f32[6,4,128,128]{3,2,1,0:T(8,128)S(1)}, f32[6,4,128,128]{3,2,1,0:T(8,128)}, u32[]{:S(2)}) copy-start(f32[6,4,128,128]{3,2,1,0:T(8,128)} %fields.3) | copy-start | bytes 4718596
  1.9 14.1 %collective-permute-start = (f32[56,128]{1,0:T(8,128)S(1)}, f32[56,128]{1,0:T(8,128)S(1)}, u32[]{:S(2)}, u32[]{:S(2)}) collective-permute-start(f32[56,128]{1,0:T(8,128)S(1)} %get-tuple-element.19.to_odd), channel_id=1, source_target_pairs={{1,2},{2,1},{3,4},{4,3},{5,6},{6,5},{7,8},{8,7},{9,10},{10,9},{11,... | collective-permute-start | bytes 86024 | tf_op jit(solution)/shard_map/lat_odd/ppermute | solution.py:415
  4.0 12.2 %collective-permute-start.1 = (f32[56,128]{1,0:T(8,128)S(1)}, f32[56,128]{1,0:T(8,128)S(1)}, u32[]{:S(2)}, u32[]{:S(2)}) collective-permute-start(f32[56,128]{1,0:T(8,128)S(1)} %get-tuple-element.20.to_even), channel_id=1, source_target_pairs={{0,1},{1,0},{2,3},{3,2},{4,5},{5,4},{6,7},{7,6},{8,9},{9,8},{10,11... | collective-permute-start | bytes 86024 | tf_op jit(solution)/shard_map/lat_even/ppermute | solution.py:417
  16.5 9.1 %collective-permute-start.2 = (f32[64,128]{1,0:T(8,128)S(1)}, f32[64,128]{1,0:T(8,128)S(1)}, u32[]{:S(2)}, u32[]{:S(2)}) collective-permute-start(f32[64,128]{1,0:T(8,128)S(1)} %get-tuple-element.22), channel_id=1, source_target_pairs={{0,16},{1,17},{2,18},{3,19},{4,20},{5,21},{6,22},{7,23},{8,24},{9,... | collective-permute-start | bytes 98312 | tf_op jit(solution)/shard_map/lon_east/ppermute | solution.py:442
  20.7 7.2 %copy-start.4 = (bf16[256,896]{1,0:T(8,128)(2,1)S(1)}, bf16[256,896]{1,0:T(8,128)(2,1)}, u32[]{:S(2)}) copy-start(bf16[256,896]{1,0:T(8,128)(2,1)} %constant.2.clone.matrix) | copy-start | bytes 1376260
  20.7 7.2 %collective-permute-start.3 = (f32[64,128]{1,0:T(8,128)S(1)}, f32[64,128]{1,0:T(8,128)S(1)}, u32[]{:S(2)}, u32[]{:S(2)}) collective-permute-start(f32[64,128]{1,0:T(8,128)S(1)} %get-tuple-element.28), channel_id=1, source_target_pairs={{0,496},{1,497},{2,498},{3,499},{4,500},{5,501},{6,502},{7,503},{8... | collective-permute-start | bytes 98312 | tf_op jit(solution)/shard_map/lon_west/ppermute | solution.py:468

commit v8 on v7

--- a/solution.py
+++ b/solution.py
@@ -150,18 +150,18 @@
     return jnp.where(low, v, other) if half == 0 else jnp.where(low, other, v)
 
 
-def lat_strip(strip, ends, shift_w, shift_e, top):
+def lat_strip(strip, top, side=None, beside=None, shift=0):
     lane = lanes((8, 128))
-    if ends is not None:
-        west = roll(ends[0][0:ROWS4], shift_w, 1)
-        east = roll(ends[1][0:ROWS4], shift_e, 1)
+    if beside is not None:
+        beside = roll(beside[0:ROWS4], shift, 1)
 
     def tile(t):
         x = strip[8 * t : 8 * t + 8]
         xe, xw = roll(x, -1, 1), roll(x, 1, 1)
-        if ends is not None:
-            xe = jnp.where(lane == 127, east[8 * t : 8 * t + 8], xe)
-            xw = jnp.where(lane == 0, west[8 * t : 8 * t + 8], xw)
+        if side == 0:
+            xw = jnp.where(lane == 0, beside[8 * t : 8 * t + 8], xw)
+        elif side == 1:
+            xe = jnp.where(lane == 127, beside[8 * t : 8 * t + 8], xe)
         return x, xe, xw
 
     x12, e12, w12 = tile(12)
@@ -199,7 +199,7 @@
 def inner_steps(fields, w, area, mask, land, north, south, res, ends, mid, halo, mw5, beside):
     top = lax.axis_index("lat") == lax.axis_size("lat") - 1
     for s, tiles in enumerate(
-        (lat_strip(south, None, 0, 0, None), lat_strip(north, None, 0, 0, top))
+        (lat_strip(south, None), lat_strip(north, top))
     ):
         for t in range(12):
             halo[s, 8 * t : 8 * t + 8] = tiles[t]
@@ -285,34 +285,27 @@
     return dot(lo, matrix[0:128]) + dot(jnp.concatenate([hi, mid], axis=1), matrix)
 
 
-def outer_kernel(pack, got_west, got_east, north, south, inner_a, inner_b, ends_a, ends_b, matrix, out_hbm,
-                 side, wide, halo, z, res, sem):
+def side_columns(s, pack, got, north, south, ends, matrix, side, wide, halo):
     top = lax.axis_index("lat") == lax.axis_size("lat") - 1
-    west, east = got_west[...], got_east[...]
-    west = jnp.concatenate([west, roll(west, -2, 1)], axis=0)
-    east = jnp.concatenate([east, roll(east, 2, 1)], axis=0)
-    own = pack[...]
-    early = runs_early()
-    ends = jnp.where(early, ends_a[...], ends_b[...])
+    beside, own = got[...], pack[...]
+    beside = jnp.concatenate([beside, roll(beside, 2 if s else -2, 1)], axis=0)
     lane = lanes((128, 128))
-    j = lane % 4
-    span = 128 + 2 * PAD
-
-    def fill(s, strip, above, below):
-        side[s, PAD : PAD + 128] = strip
-        side[s, 0:PAD] = jnp.broadcast_to(below, (PAD, 128))
-        side[s, PAD + 128 : span] = jnp.broadcast_to(above, (PAD, 128))
+    j, j1 = lane % 4, lanes((1, 128)) % 4
+
+    def fill(strip, above, below):
+        side[PAD : PAD + 128] = strip
+        side[0:PAD] = jnp.broadcast_to(below, (PAD, 128))
+        side[PAD + 128 : 128 + 2 * PAD] = jnp.broadcast_to(above, (PAD, 128))
 
     def widen(n):
-        for s in range(2):
-            wide[s, :, 0 : 128 * n] = spread(side[s], matrix[:, 0 : 128 * n])
-
-    def update(s, r):
+        wide[:, 0 : 128 * n] = spread(side[...], matrix[:, 0 : 128 * n])
+
+    def update(r):
         def rep(n, d=0):
-            return wide[s, PAD + r + d : PAD + r + d + CHUNK, 128 * n : 128 * n + 128]
+            return wide[PAD + r + d : PAD + r + d + CHUNK, 128 * n : 128 * n + 128]
 
         def at(d):
-            return side[s, PAD + r + d : PAD + r + d + CHUNK]
+            return side[PAD + r + d : PAD + r + d + CHUNK]
 
         m, v, x = rep(6), rep(2), at(0)
         me, mw, mn, ms = m * rep(3), m * rep(4), m * rep(5), m * rep(5, -1)
@@ -320,27 +313,25 @@
         c = coefs(rep(0), rep(1), v + rep(2, 1), v + rep(2, -1), me, mw, mn, ms, base)
         return apply(c, x, roll(x, -1, 1), roll(x, 1, 1), at(1), at(-1))
 
-    j1 = lanes((1, 128)) % 4
-
     def as_row(turned, columns, shift):
         parts = [roll(turned[c : c + 1], shift + d, 1) for c, d in zip(columns, (-2, -1, 0, 1))]
         low = jnp.where(j1 == 0, parts[0], parts[1])
         return jnp.where(j1 < 2, low, jnp.where(j1 == 2, parts[2], parts[3]))
 
-    three = jnp.where(lane < 112, roll(own, -8, 1), jnp.where(lane < 120, west, roll(east, 8, 1)))
-    turned = three.T
+    turned = jnp.where(lane < 112, roll(own, -8, 1), beside).T
     above, below = as_row(turned, range(104, 108), 0), as_row(turned, range(108, 112), 1)
-    fill(0, jnp.where(j < 2, west, own),
-         jnp.where(j1 == 1, roll(turned[113:114], -1, 1), above),
-         jnp.where(j1 == 1, turned[117:118], below))
-    fill(1, jnp.where(j < 2, own, east),
-         jnp.where(j1 == 2, turned[122:123], above),
-         jnp.where(j1 == 2, roll(turned[126:127], 1, 1), below))
+    if s == 0:
+        above = jnp.where(j1 == 1, roll(turned[113:114], -1, 1), above)
+        below = jnp.where(j1 == 1, turned[117:118], below)
+        fill(jnp.where(j < 2, beside, own), above, below)
+    else:
+        above = jnp.where(j1 == 2, turned[114:115], above)
+        below = jnp.where(j1 == 2, roll(turned[118:119], 1, 1), below)
+        fill(jnp.where(j < 2, own, beside), above, below)
     widen(7)
 
-    packs = (west, east)
-    low = lat_strip(south, packs, 11, 9, None)
-    high = lat_strip(north, packs, 15, 13, top)
+    low = lat_strip(south, None, s, beside, (11, 9)[s])
+    high = lat_strip(north, top, s, beside, (15, 13)[s])
     ring = rows_of((8, 128)) % 4 == 2
     for t in range(12):
         halo[8 * t : 8 * t + 8] = jnp.where(ring, high[t], low[t])
@@ -349,15 +340,27 @@
     outer = (126, 127, 0, 1)
     above, below = as_row(turned, outer, 0), as_row(turned, outer, 1)
 
-    new = [[update(s, r) for r in range(0, 128, CHUNK)] for s in range(2)]
-    edge = (j == 0) | (j == 3)
-    for s in range(2):
-        strip = jnp.where(edge, roll(ends, 1 - 2 * s, 1), jnp.concatenate(new[s], axis=0))
-        fill(s, strip, above, below)
+    new = jnp.concatenate([update(r) for r in range(0, 128, CHUNK)], axis=0)
+    fill(jnp.where((j == 0) | (j == 3), roll(ends, 1 - 2 * s, 1), new), above, below)
     widen(3)
+    return update
+
+
+def west_kernel(pack, got_west, north, south, ends_a, ends_b, matrix, z, *scratch):
+    ends = jnp.where(runs_early(), ends_a[...], ends_b[...])
+    update = side_columns(0, pack, got_west, north, south, ends, matrix, *scratch)
+    for r in range(0, 128, CHUNK):
+        z[r : r + CHUNK] = update(r)
+
+
+def last_kernel(pack, got_east, north, south, ends_a, ends_b, matrix, z_west, inner_a, inner_b, out_hbm,
+                side, wide, halo, z, res, sem):
+    early = runs_early()
+    ends = jnp.where(early, ends_a[...], ends_b[...])
+    update = side_columns(1, pack, got_east, north, south, ends, matrix, side, wide, halo)
     jj = lanes((CHUNK, 128)) % 4
     for r in range(0, 128, CHUNK):
-        z[r : r + CHUNK] = jnp.where(jj < 2, update(1, r), update(0, r))
+        z[r : r + CHUNK] = jnp.where(jj < 2, update(r), z_west[r : r + CHUNK])
 
     outs = []
     outer = (lanes((CHUNK, 128)) < 2) | (lanes((CHUNK, 128)) >= 126)
@@ -468,23 +471,38 @@
         got_east = lax.ppermute(to_west, axes, lon_pairs(nlon, nlat, -1))
     inner_b, ends_b = inner_call(False)
 
+    matrix = jnp.asarray(spread_matrix(), jnp.bfloat16)
+    strip_scratch = [
+        pltpu.VMEM((padded, 128), F32),
+        pltpu.VMEM((padded, 7 * 128), F32),
+        pltpu.VMEM((128, 128), F32),
+    ]
+    z_west = pl.pallas_call(
+        west_kernel,
+        out_shape=tile,
+        in_specs=[vmem()] * 7,
+        out_specs=vmem(),
+        scratch_shapes=strip_scratch,
+        compiler_params=params,
+        cost_estimate=cost(2 << 20, 10 << 20),
+        name="west",
+    )(pack, got_west, north, south, ends_a, ends_b, matrix)
+
     return pl.pallas_call(
-        outer_kernel,
+        last_kernel,
         out_shape=state,
         in_specs=[vmem()] * 10,
         out_specs=pl.BlockSpec(memory_space=pltpu.HBM),
-        scratch_shapes=[
-            pltpu.VMEM((2, padded, 128), F32),
-            pltpu.VMEM((2, padded, 7 * 128), F32),
-            pltpu.VMEM((128, 128), F32),
+        scratch_shapes=strip_scratch
+        + [
             pltpu.VMEM((128, 128), F32),
             pltpu.VMEM((6, 4, 128, 128), F32),
             pltpu.SemaphoreType.DMA((4,)),
         ],
         compiler_params=params,
         cost_estimate=cost(4 << 20, 1 << 20),
-        name="outer",
-    )(pack, got_west, got_east, north, south, inner_a, inner_b, ends_a, ends_b, jnp.asarray(spread_matrix(), jnp.bfloat16))
+        name="last",
+    )(pack, got_east, north, south, ends_a, ends_b, matrix, z_west, inner_a, inner_b)
 
 
 def solution(mesh):

time: 30.9 us -> 31.1 us (level)
  the two profiles are of different devices: /device:TPU:124 before, /device:TPU:28 now
where the time goes in v8:
time: 31.1 us; the launch traced here: 30.9 us
  starting transfers between devices  21.6 us (69%)
  Pallas kernels  8.16 us (26%)
  between operations  0.93 us (3%)
    ppermute x1, starting transfers between devices, local(): got_even = lax.ppermute(to_even, axes, lat_pairs(nlon, nlat, False))  11.4 us
    ppermute x1, starting transfers between devices, local(): got_east = lax.ppermute(to_west, axes, lon_pairs(nlon, nlat, -1))  4.27 us
    ppermute x1, starting transfers between devices, local(): got_west = lax.ppermute(to_east, axes, lon_pairs(nlon, nlat, 1))  3.82 us
    pallas_call x2, Pallas kernels, inner_call(): pl.pallas_call(functools.partial(inner_kernel, early), out_shape=(state,...  2.87 us
    pallas_call x1, Pallas kernels, local(): pl.pallas_call(last_kernel, out_shape=state, in_specs=[vmem()] * 10, out_...  2.45 us
    ppermute x1, starting transfers between devices, local(): got_odd = lax.ppermute(to_odd, axes, lat_pairs(nlon, nlat, True))  2.09 us
    pallas_call x1, Pallas kernels, local(): pl.pallas_call(rows_kernel, out_shape=(rows, rows), in_specs=[pl.BlockSpe...  1.05 us
    pallas_call x1, Pallas kernels, local(): pl.pallas_call(west_kernel, out_shape=tile, in_specs=[vmem()] * 7, out_sp...  0.87 us
  transfers between devices with their start and end apart: 4, of which 1 were waited for; matrix products, arithmetic and copies ran while one was open for 0% of the time, Pallas kernels for 14%

profile of v8, /device:TPU:28, one launch (start us, length us, event | category | flops | bytes accessed | tf_op | source)
XLA Modules:
  0.0 30.9 jit_solution(8186304995984021140)
XLA Ops:
  0.0 0.0 copy-start.4
  0.0 0.0 copy-start.3
  0.0 0.0 copy-start.1
  0.0 0.0 copy-start
  0.8 1.0 %rows.1 = (f32[56,128]{1,0:T(8,128)S(1)}, f32[56,128]{1,0:T(8,128)S(1)}) custom-call(f32[24,128,128]{2,1,0:T(8,128)} %bitcast.1, f32[2,128,128]{2,1,0:T(8,128)} %w.7, f32[128,128]{1,0:T(8,128)} %area.7, s32[128,128]{1,0:T(8,128)} %mask.7, s32[1,1]{1,0:T(1,128)S(6)} %copy.7.land), custom_call_target="tpu_custom_call" | custom-call | flops 65536 | bytes 262144 | tf_op jit(solution)/shard_map/rows/pallas_call | solution.py:399
  1.9 2.1 %collective-permute-start = (f32[56,128]{1,0:T(8,128)S(1)}, f32[56,128]{1,0:T(8,128)S(1)}, u32[]{:S(2)}, u32[]{:S(2)}) collective-permute-start(f32[56,128]{1,0:T(8,128)S(1)} %get-tuple-element.19.to_odd), channel_id=1, source_target_pairs={{1,2},{2,1},{3,4},{4,3},{5,6},{6,5},{7,8},{8,7},{9,10},{10,9},{11,... | collective-permute-start | bytes 86024 | tf_op jit(solution)/shard_map/lat_odd/ppermute | solution.py:418
  4.0 11.4 %collective-permute-start.1 = (f32[56,128]{1,0:T(8,128)S(1)}, f32[56,128]{1,0:T(8,128)S(1)}, u32[]{:S(2)}, u32[]{:S(2)}) collective-permute-start(f32[56,128]{1,0:T(8,128)S(1)} %get-tuple-element.20.to_even), channel_id=1, source_target_pairs={{0,1},{1,0},{2,3},{3,2},{4,5},{5,4},{6,7},{7,6},{8,9},{9,8},{10,11... | collective-permute-start | bytes 86024 | tf_op jit(solution)/shard_map/lat_even/ppermute | solution.py:420
  15.4 0.0 copy-done.4
  15.4 0.0 copy-done.3
  15.4 0.0 copy-done.1
  15.4 0.0 copy-done
  15.4 0.5 %columns.1.pack = f32[128,128]{1,0:T(8,128)S(1)} custom-call(f32[24,128,128]{2,1,0:T(8,128)S(1)} %bitcast.2, f32[2,128,128]{2,1,0:T(8,128)S(1)} %copy-done.1, f32[128,128]{1,0:T(8,128)S(1)} %copy-done.3, s32[128,128]{1,0:T(8,128)S(1)} %copy-done.4, s32[1,1]{1,0:T(1,128)S(6)} %copy.7.land), custom_call_target="tpu_custom_call" | custom-call | flops 1048576 | bytes 2097152 | tf_op jit(solution)/shard_map/columns/pallas_call | solution.py:423
  16.0 0.0 collective-permute-done.got_odd
  16.0 0.2 collective-permute-done.1.got_even
  16.2 0.4 %strips.1 = (f32[128,128]{1,0:T(8,128)S(1)}, f32[64,128]{1,0:T(8,128)S(1)}, f32[64,128]{1,0:T(8,128)S(1)}, f32[112,128]{1,0:T(8,128)S(1)}, f32[112,128]{1,0:T(8,128)S(1)}) custom-call(f32[56,128]{1,0:T(8,128)S(1)} %get-tuple-element.19.to_odd, f32[56,128]{1,0:T(8,128)S(1)} %get-tuple-element.20.to_even, f32[56,128]{1,0:T(8,128)S(1)} %collective-permute-done.got_odd, ...), custom_call_target="tpu_custom_call" | custom-call | flops 262144 | bytes 262144 | tf_op jit(solution)/shard_map/strips/pallas_call | solution.py:433
  16.6 3.8 %collective-permute-start.3 = (f32[64,128]{1,0:T(8,128)S(1)}, f32[64,128]{1,0:T(8,128)S(1)}, u32[]{:S(2)}, u32[]{:S(2)}) collective-permute-start(f32[64,128]{1,0:T(8,128)S(1)} %get-tuple-element.30), channel_id=1, source_target_pairs={{0,16},{1,17},{2,18},{3,19},{4,20},{5,21},{6,22},{7,23},{8,24},{9,... | collective-permute-start | bytes 98312 | tf_op jit(solution)/shard_map/lon_east/ppermute | solution.py:445
  20.4 0.0 copy-start.2
  20.4 4.3 %collective-permute-start.2 = (f32[64,128]{1,0:T(8,128)S(1)}, f32[64,128]{1,0:T(8,128)S(1)}, u32[]{:S(2)}, u32[]{:S(2)}) collective-permute-start(f32[64,128]{1,0:T(8,128)S(1)} %get-tuple-element.27), channel_id=1, source_target_pairs={{0,496},{1,497},{2,498},{3,499},{4,500},{5,501},{6,502},{7,503},{8... | collective-permute-start | bytes 98312 | tf_op jit(solution)/shard_map/lon_west/ppermute | solution.py:471
  24.7 2.8 %inner_late.1 = (f32[6,4,128,128]{3,2,1,0:T(8,128)S(1)}, f32[128,128]{1,0:T(8,128)S(1)}) custom-call(f32[6,4,128,128]{3,2,1,0:T(8,128)S(1)} %copy-done, f32[2,128,128]{2,1,0:T(8,128)S(1)} %copy-done.1, f32[128,128]{1,0:T(8,128)S(1)} %copy-done.3, s32[128,128]{1,0:T(8,128)S(1)} %copy-done.4, s32[1,1]{1,0:T(1,128)S(6)} %copy.7.land, ...), custom_call_target="tpu_custom_call" | custom-call | flops 20971520 | bytes 4194304 | tf_op jit(solution)/shard_map/inner_late/pallas_call | solution.py:452
  27.6 0.0 collective-permute-done.3.got_west
  27.6 0.0 copy-done.2
  27.6 0.9 %west.1.z_west = f32[128,128]{1,0:T(8,128)S(1)} custom-call(f32[128,128]{1,0:T(8,128)S(1)} %get-tuple-element.21.pack, f32[64,128]{1,0:T(8,128)S(1)} %collective-permute-done.3.got_west, f32[112,128]{1,0:T(8,128)S(1)} %get-tuple-element.23.north, f32[112,128]{1,0:T(8,128)S(1)} %get-tuple-element.24.south, f32[128,128]{1,0:T(8,128)S(1)} %get-tuple-element.28.ends_a, ...), custom_call_target="tpu_custom_call" | custom-call | flops 10485760 | bytes 2097152 | tf_op jit(solution)/shard_map/west/pallas_call | solution.py:480
  28.5 0.0 collective-permute-done.2.got_east
  28.5 2.5 %last.1 = f32[6,4,128,128]{3,2,1,0:T(8,128)} custom-call(f32[128,128]{1,0:T(8,128)S(1)} %get-tuple-element.21.pack, f32[64,128]{1,0:T(8,128)S(1)} %collective-permute-done.2.got_east, f32[112,128]{1,0:T(8,128)S(1)} %get-tuple-element.23.north, f32[112,128]{1,0:T(8,128)S(1)} %get-tuple-element.24.south, f32[128,128]{1,0:T(8,128)S(1)} %get-tuple-element.28.ends_a, ...), custom_call_target="tpu_custom_call" | custom-call | flops 1048576 | bytes 4194304 | tf_op jit(solution)/shard_map/last/pallas_call | solution.py:491
  (1 shorter events, 0.0 us)
Async XLA Ops:
  0.0 15.4 %copy-start.4 = (s32[128,128]{1,0:T(8,128)S(1)}, s32[128,128]{1,0:T(8,128)}, u32[]{:S(2)}) copy-start(s32[128,128]{1,0:T(8,128)} %mask.7) | copy-start | bytes 196612
  0.0 15.4 %copy-start.3 = (f32[128,128]{1,0:T(8,128)S(1)}, f32[128,128]{1,0:T(8,128)}, u32[]{:S(2)}) copy-start(f32[128,128]{1,0:T(8,128)} %area.7) | copy-start | bytes 196612
  0.0 15.4 %copy-start.1 = (f32[2,128,128]{2,1,0:T(8,128)S(1)}, f32[2,128,128]{2,1,0:T(8,128)}, u32[]{:S(2)}) copy-start(f32[2,128,128]{2,1,0:T(8,128)} %w.7) | copy-start | bytes 393220
  0.0 15.4 %copy-start = (f32[6,4,128,128]{3,2,1,0:T(8,128)S(1)}, f32[6,4,128,128]{3,2,1,0:T(8,128)}, u32[]{:S(2)}) copy-start(f32[6,4,128,128]{3,2,1,0:T(8,128)} %fields.3) | copy-start | bytes 4718596
  1.9 14.1 %collective-permute-start = (f32[56,128]{1,0:T(8,128)S(1)}, f32[56,128]{1,0:T(8,128)S(1)}, u32[]{:S(2)}, u32[]{:S(2)}) collective-permute-start(f32[56,128]{1,0:T(8,128)S(1)} %get-tuple-element.19.to_odd), channel_id=1, source_target_pairs={{1,2},{2,1},{3,4},{4,3},{5,6},{6,5},{7,8},{8,7},{9,10},{10,9},{11,... | collective-permute-start | bytes 86024 | tf_op jit(solution)/shard_map/lat_odd/ppermute | solution.py:418
  4.0 12.2 %collective-permute-start.1 = (f32[56,128]{1,0:T(8,128)S(1)}, f32[56,128]{1,0:T(8,128)S(1)}, u32[]{:S(2)}, u32[]{:S(2)}) collective-permute-start(f32[56,128]{1,0:T(8,128)S(1)} %get-tuple-element.20.to_even), channel_id=1, source_target_pairs={{0,1},{1,0},{2,3},{3,2},{4,5},{5,4},{6,7},{7,6},{8,9},{9,8},{10,11... | collective-permute-start | bytes 86024 | tf_op jit(solution)/shard_map/lat_even/ppermute | solution.py:420
  16.6 11.0 %collective-permute-start.3 = (f32[64,128]{1,0:T(8,128)S(1)}, f32[64,128]{1,0:T(8,128)S(1)}, u32[]{:S(2)}, u32[]{:S(2)}) collective-permute-start(f32[64,128]{1,0:T(8,128)S(1)} %get-tuple-element.30), channel_id=1, source_target_pairs={{0,16},{1,17},{2,18},{3,19},{4,20},{5,21},{6,22},{7,23},{8,24},{9,... | collective-permute-start | bytes 98312 | tf_op jit(solution)/shard_map/lon_east/ppermute | solution.py:445
  20.4 7.2 %copy-start.2 = (bf16[256,896]{1,0:T(8,128)(2,1)S(1)}, bf16[256,896]{1,0:T(8,128)(2,1)}, u32[]{:S(2)}) copy-start(bf16[256,896]{1,0:T(8,128)(2,1)} %constant.2.clone.matrix) | copy-start | bytes 1376260
  20.4 8.0 %collective-permute-start.2 = (f32[64,128]{1,0:T(8,128)S(1)}, f32[64,128]{1,0:T(8,128)S(1)}, u32[]{:S(2)}, u32[]{:S(2)}) collective-permute-start(f32[64,128]{1,0:T(8,128)S(1)} %get-tuple-element.27), channel_id=1, source_target_pairs={{0,496},{1,497},{2,498},{3,499},{4,500},{5,501},{6,502},{7,503},{8... | collective-permute-start | bytes 98312 | tf_op jit(solution)/shard_map/lon_west/ppermute | solution.py:471

commit v9 on v8

--- a/solution.py
+++ b/solution.py
@@ -346,21 +346,21 @@
     return update
 
 
-def west_kernel(pack, got_west, north, south, ends_a, ends_b, matrix, z, *scratch):
+def east_kernel(pack, got_east, north, south, ends_a, ends_b, matrix, z, *scratch):
     ends = jnp.where(runs_early(), ends_a[...], ends_b[...])
-    update = side_columns(0, pack, got_west, north, south, ends, matrix, *scratch)
+    update = side_columns(1, pack, got_east, north, south, ends, matrix, *scratch)
     for r in range(0, 128, CHUNK):
         z[r : r + CHUNK] = update(r)
 
 
-def last_kernel(pack, got_east, north, south, ends_a, ends_b, matrix, z_west, inner_a, inner_b, out_hbm,
+def last_kernel(pack, got_west, north, south, ends_a, ends_b, matrix, z_east, inner_a, inner_b, out_hbm,
                 side, wide, halo, z, res, sem):
     early = runs_early()
     ends = jnp.where(early, ends_a[...], ends_b[...])
-    update = side_columns(1, pack, got_east, north, south, ends, matrix, side, wide, halo)
+    update = side_columns(0, pack, got_west, north, south, ends, matrix, side, wide, halo)
     jj = lanes((CHUNK, 128)) % 4
     for r in range(0, 128, CHUNK):
-        z[r : r + CHUNK] = jnp.where(jj < 2, update(r), z_west[r : r + CHUNK])
+        z[r : r + CHUNK] = jnp.where(jj < 2, z_east[r : r + CHUNK], update(r))
 
     outs = []
     outer = (lanes((CHUNK, 128)) < 2) | (lanes((CHUNK, 128)) >= 126)
@@ -441,9 +441,6 @@
         name="strips",
     )(to_odd, to_even, got_odd, got_even, pack)
 
-    with jax.named_scope("lon_east"):
-        got_west = lax.ppermute(to_east, axes, lon_pairs(nlon, nlat, 1))
-
     padded = 128 + 2 * PAD
     state = shape((6, 4, 128, 128), F32)
     inputs = (fields, weights, area, mask, land, north, south)
@@ -466,9 +463,11 @@
         )(*inputs)
 
     inner_a, ends_a = inner_call(True)
-    to_west, inner_a, ends_a = lax.optimization_barrier((to_west, inner_a, ends_a))
+    to_west, to_east, inner_a, ends_a = lax.optimization_barrier((to_west, to_east, inner_a, ends_a))
     with jax.named_scope("lon_west"):
         got_east = lax.ppermute(to_west, axes, lon_pairs(nlon, nlat, -1))
+    with jax.named_scope("lon_east"):
+        got_west = lax.ppermute(to_east, axes, lon_pairs(nlon, nlat, 1))
     inner_b, ends_b = inner_call(False)
 
     matrix = jnp.asarray(spread_matrix(), jnp.bfloat16)
@@ -477,16 +476,16 @@
         pltpu.VMEM((padded, 7 * 128), F32),
         pltpu.VMEM((128, 128), F32),
     ]
-    z_west = pl.pallas_call(
-        west_kernel,
+    z_east = pl.pallas_call(
+        east_kernel,
         out_shape=tile,
         in_specs=[vmem()] * 7,
         out_specs=vmem(),
         scratch_shapes=strip_scratch,
         compiler_params=params,
         cost_estimate=cost(2 << 20, 10 << 20),
-        name="west",
-    )(pack, got_west, north, south, ends_a, ends_b, matrix)
+        name="east",
+    )(pack, got_east, north, south, ends_a, ends_b, matrix)
 
     return pl.pallas_call(
         last_kernel,
@@ -502,7 +501,7 @@
         compiler_params=params,
         cost_estimate=cost(4 << 20, 1 << 20),
         name="last",
-    )(pack, got_east, north, south, ends_a, ends_b, matrix, z_west, inner_a, inner_b)
+    )(pack, got_west, north, south, ends_a, ends_b, matrix, z_east, inner_a, inner_b)
 
 
 def solution(mesh):

time: 31.1 us -> 33.8 us (1.087)
  the two profiles are of different devices: /device:TPU:28 before, /device:TPU:4 now
where the time goes in v9:
time: 33.8 us; the launch traced here: 33.6 us
  starting transfers between devices  17.5 us (52%)
  Pallas kernels  8.14 us (24%)
  waiting for transfers between devices  7.05 us (21%)
  between operations  0.92 us (3%)
    ppermute x1, starting transfers between devices, local(): got_east = lax.ppermute(to_west, axes, lon_pairs(nlon, nlat, -1))  9.34 us
    ppermute x1, waiting for transfers between devices, local(): got_west = lax.ppermute(to_east, axes, lon_pairs(nlon, nlat, 1))  5.07 us
    ppermute x1, starting transfers between devices, local(): got_odd = lax.ppermute(to_odd, axes, lat_pairs(nlon, nlat, True))  4.31 us
    pallas_call x2, Pallas kernels, inner_call(): pl.pallas_call(functools.partial(inner_kernel, early), out_shape=(state,...  2.87 us
    pallas_call x1, Pallas kernels, local(): pl.pallas_call(last_kernel, out_shape=state, in_specs=[vmem()] * 10, out_...  2.44 us
    ppermute x1, waiting for transfers between devices, local(): got_odd = lax.ppermute(to_odd, axes, lat_pairs(nlon, nlat, True))  1.97 us
    ppermute x1, starting transfers between devices, local(): got_even = lax.ppermute(to_even, axes, lat_pairs(nlon, nlat, False))  1.92 us
    ppermute x1, starting transfers between devices, local(): got_west = lax.ppermute(to_east, axes, lon_pairs(nlon, nlat, 1))  1.92 us
  transfers between devices with their start and end apart: 4, of which 2 were waited for; matrix products, arithmetic and copies ran while one was open for 0% of the time, Pallas kernels for 4%

profile of v9, /device:TPU:4, one launch (start us, length us, event | category | flops | bytes accessed | tf_op | source)
XLA Modules:
  0.0 33.6 jit_solution(15529586836543834673)
XLA Ops:
  0.0 0.0 copy-start.4
  0.0 0.0 copy-start.3
  0.0 0.0 copy-start.1
  0.0 0.0 copy-start
  0.8 1.0 %rows.1 = (f32[56,128]{1,0:T(8,128)S(1)}, f32[56,128]{1,0:T(8,128)S(1)}) custom-call(f32[24,128,128]{2,1,0:T(8,128)} %bitcast.1, f32[2,128,128]{2,1,0:T(8,128)} %w.7, f32[128,128]{1,0:T(8,128)} %area.7, s32[128,128]{1,0:T(8,128)} %mask.7, s32[1,1]{1,0:T(1,128)S(6)} %copy.7.land), custom_call_target="tpu_custom_call" | custom-call | flops 65536 | bytes 262144 | tf_op jit(solution)/shard_map/rows/pallas_call | solution.py:399
  1.9 4.3 %collective-permute-start = (f32[56,128]{1,0:T(8,128)S(1)}, f32[56,128]{1,0:T(8,128)S(1)}, u32[]{:S(2)}, u32[]{:S(2)}) collective-permute-start(f32[56,128]{1,0:T(8,128)S(1)} %get-tuple-element.20.to_odd), channel_id=1, source_target_pairs={{1,2},{2,1},{3,4},{4,3},{5,6},{6,5},{7,8},{8,7},{9,10},{10,9},{11,... | collective-permute-start | bytes 86024 | tf_op jit(solution)/shard_map/lat_odd/ppermute | solution.py:418
  6.2 1.9 %collective-permute-start.1 = (f32[56,128]{1,0:T(8,128)S(1)}, f32[56,128]{1,0:T(8,128)S(1)}, u32[]{:S(2)}, u32[]{:S(2)}) collective-permute-start(f32[56,128]{1,0:T(8,128)S(1)} %get-tuple-element.21.to_even), channel_id=1, source_target_pairs={{0,1},{1,0},{2,3},{3,2},{4,5},{5,4},{6,7},{7,6},{8,9},{9,8},{10,11... | collective-permute-start | bytes 86024 | tf_op jit(solution)/shard_map/lat_even/ppermute | solution.py:420
  8.1 0.0 copy-done.4
  8.1 0.0 copy-done.3
  8.1 0.0 copy-done.1
  8.1 0.0 copy-done
  8.1 0.5 %columns.1.pack = f32[128,128]{1,0:T(8,128)S(1)} custom-call(f32[24,128,128]{2,1,0:T(8,128)S(1)} %bitcast.2, f32[2,128,128]{2,1,0:T(8,128)S(1)} %copy-done.1, f32[128,128]{1,0:T(8,128)S(1)} %copy-done.3, s32[128,128]{1,0:T(8,128)S(1)} %copy-done.4, s32[1,1]{1,0:T(1,128)S(6)} %copy.7.land), custom_call_target="tpu_custom_call" | custom-call | flops 1048576 | bytes 2097152 | tf_op jit(solution)/shard_map/columns/pallas_call | solution.py:423
  8.7 2.0 %collective-permute-done.got_odd = f32[56,128]{1,0:T(8,128)S(1)} collective-permute-done((f32[56,128]{1,0:T(8,128)S(1)}, f32[56,128]{1,0:T(8,128)S(1)}, u32[]{:S(2)}, u32[]{:S(2)}) %collective-permute-start) | collective-permute-done | bytes 28704 | tf_op jit(solution)/shard_map/lat_odd/ppermute | solution.py:418
  10.7 0.0 collective-permute-done.1.got_even
  10.7 0.4 %strips.1 = (f32[128,128]{1,0:T(8,128)S(1)}, f32[64,128]{1,0:T(8,128)S(1)}, f32[64,128]{1,0:T(8,128)S(1)}, f32[112,128]{1,0:T(8,128)S(1)}, f32[112,128]{1,0:T(8,128)S(1)}) custom-call(f32[56,128]{1,0:T(8,128)S(1)} %get-tuple-element.20.to_odd, f32[56,128]{1,0:T(8,128)S(1)} %get-tuple-element.21.to_even, f32[56,128]{1,0:T(8,128)S(1)} %collective-permute-done.got_odd, ...), custom_call_target="tpu_custom_call" | custom-call | flops 262144 | bytes 262144 | tf_op jit(solution)/shard_map/strips/pallas_call | solution.py:433
  11.0 0.0 copy-start.2
  11.1 2.8 %inner_early.1 = (f32[6,4,128,128]{3,2,1,0:T(8,128)S(1)}, f32[128,128]{1,0:T(8,128)S(1)}) custom-call(f32[6,4,128,128]{3,2,1,0:T(8,128)S(1)} %copy-done, f32[2,128,128]{2,1,0:T(8,128)S(1)} %copy-done.1, f32[128,128]{1,0:T(8,128)S(1)} %copy-done.3, s32[128,128]{1,0:T(8,128)S(1)} %copy-done.4, s32[1,1]{1,0:T(1,128)S(6)} %copy.7.land, ...), custom_call_target="tpu_custom_call" | custom-call | flops 20971520 | bytes 4194304 | tf_op jit(solution)/shard_map/inner_early/pallas_call | solution.py:449
  13.9 9.3 %collective-permute-start.3 = (f32[64,128]{1,0:T(8,128)S(1)}, f32[64,128]{1,0:T(8,128)S(1)}, u32[]{:S(2)}, u32[]{:S(2)}) collective-permute-start(f32[64,128]{1,0:T(8,128)S(1)} %get-tuple-element.32), channel_id=1, source_target_pairs={{0,496},{1,497},{2,498},{3,499},{4,500},{5,501},{6,502},{7,503},{8... | collective-permute-start | bytes 98312 | tf_op jit(solution)/shard_map/lon_west/ppermute | solution.py:468
  23.3 1.9 %collective-permute-start.2 = (f32[64,128]{1,0:T(8,128)S(1)}, f32[64,128]{1,0:T(8,128)S(1)}, u32[]{:S(2)}, u32[]{:S(2)}) collective-permute-start(f32[64,128]{1,0:T(8,128)S(1)} %get-tuple-element.29), channel_id=1, source_target_pairs={{0,16},{1,17},{2,18},{3,19},{4,20},{5,21},{6,22},{7,23},{8,24},{9,... | collective-permute-start | bytes 98312 | tf_op jit(solution)/shard_map/lon_east/ppermute | solution.py:470
  25.2 0.0 collective-permute-done.3.got_east
  25.2 0.0 copy-done.2
  25.2 0.9 %east.1.z_east = f32[128,128]{1,0:T(8,128)S(1)} custom-call(f32[128,128]{1,0:T(8,128)S(1)} %get-tuple-element.22.pack, f32[64,128]{1,0:T(8,128)S(1)} %collective-permute-done.3.got_east, f32[112,128]{1,0:T(8,128)S(1)} %get-tuple-element.25.north, f32[112,128]{1,0:T(8,128)S(1)} %get-tuple-element.26.south, f32[128,128]{1,0:T(8,128)S(1)} %get-tuple-element.30.ends_a, ...), custom_call_target="tpu_custom_call" | custom-call | flops 10485760 | bytes 2097152 | tf_op jit(solution)/shard_map/east/pallas_call | solution.py:479
  26.1 5.1 %collective-permute-done.2.got_west = f32[64,128]{1,0:T(8,128)S(1)} collective-permute-done((f32[64,128]{1,0:T(8,128)S(1)}, f32[64,128]{1,0:T(8,128)S(1)}, u32[]{:S(2)}, u32[]{:S(2)}) %collective-permute-start.2) | collective-permute-done | bytes 32800 | tf_op jit(solution)/shard_map/lon_east/ppermute | solution.py:470
  31.2 2.4 %last.1 = f32[6,4,128,128]{3,2,1,0:T(8,128)} custom-call(f32[128,128]{1,0:T(8,128)S(1)} %get-tuple-element.22.pack, f32[64,128]{1,0:T(8,128)S(1)} %collective-permute-done.2.got_west, f32[112,128]{1,0:T(8,128)S(1)} %get-tuple-element.25.north, f32[112,128]{1,0:T(8,128)S(1)} %get-tuple-element.26.south, f32[128,128]{1,0:T(8,128)S(1)} %get-tuple-element.30.ends_a, ...), custom_call_target="tpu_custom_call" | custom-call | flops 1048576 | bytes 4194304 | tf_op jit(solution)/shard_map/last/pallas_call | solution.py:490
  (1 shorter events, 0.0 us)
Async XLA Ops:
  0.0 8.1 %copy-start.4 = (s32[128,128]{1,0:T(8,128)S(1)}, s32[128,128]{1,0:T(8,128)}, u32[]{:S(2)}) copy-start(s32[128,128]{1,0:T(8,128)} %mask.7) | copy-start | bytes 196612
  0.0 8.1 %copy-start.3 = (f32[128,128]{1,0:T(8,128)S(1)}, f32[128,128]{1,0:T(8,128)}, u32[]{:S(2)}) copy-start(f32[128,128]{1,0:T(8,128)} %area.7) | copy-start | bytes 196612
  0.0 8.1 %copy-start.1 = (f32[2,128,128]{2,1,0:T(8,128)S(1)}, f32[2,128,128]{2,1,0:T(8,128)}, u32[]{:S(2)}) copy-start(f32[2,128,128]{2,1,0:T(8,128)} %w.7) | copy-start | bytes 393220
  0.0 8.1 %copy-start = (f32[6,4,128,128]{3,2,1,0:T(8,128)S(1)}, f32[6,4,128,128]{3,2,1,0:T(8,128)}, u32[]{:S(2)}) copy-start(f32[6,4,128,128]{3,2,1,0:T(8,128)} %fields.3) | copy-start | bytes 4718596
  1.9 8.8 %collective-permute-start = (f32[56,128]{1,0:T(8,128)S(1)}, f32[56,128]{1,0:T(8,128)S(1)}, u32[]{:S(2)}, u32[]{:S(2)}) collective-permute-start(f32[56,128]{1,0:T(8,128)S(1)} %get-tuple-element.20.to_odd), channel_id=1, source_target_pairs={{1,2},{2,1},{3,4},{4,3},{5,6},{6,5},{7,8},{8,7},{9,10},{10,9},{11,... | collective-permute-start | bytes 86024 | tf_op jit(solution)/shard_map/lat_odd/ppermute | solution.py:418
  6.2 4.5 %collective-permute-start.1 = (f32[56,128]{1,0:T(8,128)S(1)}, f32[56,128]{1,0:T(8,128)S(1)}, u32[]{:S(2)}, u32[]{:S(2)}) collective-permute-start(f32[56,128]{1,0:T(8,128)S(1)} %get-tuple-element.21.to_even), channel_id=1, source_target_pairs={{0,1},{1,0},{2,3},{3,2},{4,5},{5,4},{6,7},{7,6},{8,9},{9,8},{10,11... | collective-permute-start | bytes 86024 | tf_op jit(solution)/shard_map/lat_even/ppermute | solution.py:420
  11.0 14.2 %copy-start.2 = (bf16[256,896]{1,0:T(8,128)(2,1)S(1)}, bf16[256,896]{1,0:T(8,128)(2,1)}, u32[]{:S(2)}) copy-start(bf16[256,896]{1,0:T(8,128)(2,1)} %constant.2.clone.matrix) | copy-start | bytes 1376260
  13.9 11.3 %collective-permute-start.3 = (f32[64,128]{1,0:T(8,128)S(1)}, f32[64,128]{1,0:T(8,128)S(1)}, u32[]{:S(2)}, u32[]{:S(2)}) collective-permute-start(f32[64,128]{1,0:T(8,128)S(1)} %get-tuple-element.32), channel_id=1, source_target_pairs={{0,496},{1,497},{2,498},{3,499},{4,500},{5,501},{6,502},{7,503},{8... | collective-permute-start | bytes 98312 | tf_op jit(solution)/shard_map/lon_west/ppermute | solution.py:468
  23.3 7.9 %collective-permute-start.2 = (f32[64,128]{1,0:T(8,128)S(1)}, f32[64,128]{1,0:T(8,128)S(1)}, u32[]{:S(2)}, u32[]{:S(2)}) collective-permute-start(f32[64,128]{1,0:T(8,128)S(1)} %get-tuple-element.29), channel_id=1, source_target_pairs={{0,16},{1,17},{2,18},{3,19},{4,20},{5,21},{6,22},{7,23},{8,24},{9,... | collective-permute-start | bytes 98312 | tf_op jit(solution)/shard_map/lon_east/ppermute | solution.py:470

commit v10 on v8

--- a/solution.py
+++ b/solution.py
@@ -186,8 +186,7 @@
 
 
 def runs_early():
-    first = lax.axis_index("lon") % (lax.axis_size("lon") // 2) == 0
-    return first & (lax.axis_index("lat") < lax.axis_size("lat") - 2)
+    return lax.axis_index("lon") % (lax.axis_size("lon") // 2) == 0
 
 
 def inner_kernel(early, fields, w, area, mask, land, north, south, *refs):
@@ -441,9 +440,6 @@
         name="strips",
     )(to_odd, to_even, got_odd, got_even, pack)
 
-    with jax.named_scope("lon_east"):
-        got_west = lax.ppermute(to_east, axes, lon_pairs(nlon, nlat, 1))
-
     padded = 128 + 2 * PAD
     state = shape((6, 4, 128, 128), F32)
     inputs = (fields, weights, area, mask, land, north, south)
@@ -466,7 +462,9 @@
         )(*inputs)
 
     inner_a, ends_a = inner_call(True)
-    to_west, inner_a, ends_a = lax.optimization_barrier((to_west, inner_a, ends_a))
+    to_west, to_east, inner_a, ends_a = lax.optimization_barrier((to_west, to_east, inner_a, ends_a))
+    with jax.named_scope("lon_east"):
+        got_west = lax.ppermute(to_east, axes, lon_pairs(nlon, nlat, 1))
     with jax.named_scope("lon_west"):
         got_east = lax.ppermute(to_west, axes, lon_pairs(nlon, nlat, -1))
     inner_b, ends_b = inner_call(False)

time: 31.1 us -> 31.7 us (1.019)
  waiting for transfers between devices: 0.24 us -> 0.89 us
    ppermute x1, starting transfers between devices: 3.82 us -> 1.92 us  [local(): got_west = lax.ppermute(to_east, axes, lon_pairs(nlon, nlat, 1))]
    ppermute x1, starting transfers between devices: 4.27 us -> 6.03 us  [local(): got_east = lax.ppermute(to_west, axes, lon_pairs(nlon, nlat, -1))]
    ppermute x1, waiting for transfers between devices: 0.01 us -> 0.65 us  [local(): got_east = lax.ppermute(to_west, axes, lon_pairs(nlon, nlat, -1))]
  transfers between devices with their start and end apart: 4 -> 4, of which waited for: 1 -> 2; matrix products, arithmetic and copies ran while one was open for 0% -> 0% of each run, Pallas kernels for 14% -> 5%
where the time goes in v10:
time: 31.7 us; the launch traced here: 31.5 us
  starting transfers between devices  21.5 us (68%)
  Pallas kernels  8.21 us (26%)
  between operations  0.93 us (3%)
  waiting for transfers between devices  0.89 us (3%)
    ppermute x1, starting transfers between devices, local(): got_even = lax.ppermute(to_even, axes, lat_pairs(nlon, nlat, False))  11.4 us
    ppermute x1, starting transfers between devices, local(): got_east = lax.ppermute(to_west, axes, lon_pairs(nlon, nlat, -1))  6.03 us
    pallas_call x2, Pallas kernels, inner_call(): pl.pallas_call(functools.partial(inner_kernel, early), out_shape=(state,...  2.87 us
    pallas_call x1, Pallas kernels, local(): pl.pallas_call(last_kernel, out_shape=state, in_specs=[vmem()] * 10, out_...  2.5 us
    ppermute x1, starting transfers between devices, local(): got_odd = lax.ppermute(to_odd, axes, lat_pairs(nlon, nlat, True))  2.09 us
    ppermute x1, starting transfers between devices, local(): got_west = lax.ppermute(to_east, axes, lon_pairs(nlon, nlat, 1))  1.92 us
    pallas_call x1, Pallas kernels, local(): pl.pallas_call(rows_kernel, out_shape=(rows, rows), in_specs=[pl.BlockSpe...  1.05 us
    pallas_call x1, Pallas kernels, local(): pl.pallas_call(west_kernel, out_shape=tile, in_specs=[vmem()] * 7, out_sp...  0.87 us
  transfers between devices with their start and end apart: 4, of which 2 were waited for; matrix products, arithmetic and copies ran while one was open for 0% of the time, Pallas kernels for 5%

profile of v10, /device:TPU:28, one launch (start us, length us, event | category | flops | bytes accessed | tf_op | source)
XLA Modules:
  0.0 31.5 jit_solution(4035782556492246410)
XLA Ops:
  0.0 0.0 copy-start.4
  0.0 0.0 copy-start.3
  0.0 0.0 copy-start.1
  0.0 0.0 copy-start
  0.8 1.0 %rows.1 = (f32[56,128]{1,0:T(8,128)S(1)}, f32[56,128]{1,0:T(8,128)S(1)}) custom-call(f32[24,128,128]{2,1,0:T(8,128)} %bitcast.1, f32[2,128,128]{2,1,0:T(8,128)} %w.7, f32[128,128]{1,0:T(8,128)} %area.7, s32[128,128]{1,0:T(8,128)} %mask.7, s32[1,1]{1,0:T(1,128)S(6)} %copy.7.land), custom_call_target="tpu_custom_call" | custom-call | flops 65536 | bytes 262144 | tf_op jit(solution)/shard_map/rows/pallas_call | solution.py:398
  1.9 2.1 %collective-permute-start = (f32[56,128]{1,0:T(8,128)S(1)}, f32[56,128]{1,0:T(8,128)S(1)}, u32[]{:S(2)}, u32[]{:S(2)}) collective-permute-start(f32[56,128]{1,0:T(8,128)S(1)} %get-tuple-element.20.to_odd), channel_id=1, source_target_pairs={{1,2},{2,1},{3,4},{4,3},{5,6},{6,5},{7,8},{8,7},{9,10},{10,9},{11,... | collective-permute-start | bytes 86024 | tf_op jit(solution)/shard_map/lat_odd/ppermute | solution.py:417
  4.0 11.4 %collective-permute-start.1 = (f32[56,128]{1,0:T(8,128)S(1)}, f32[56,128]{1,0:T(8,128)S(1)}, u32[]{:S(2)}, u32[]{:S(2)}) collective-permute-start(f32[56,128]{1,0:T(8,128)S(1)} %get-tuple-element.21.to_even), channel_id=1, source_target_pairs={{0,1},{1,0},{2,3},{3,2},{4,5},{5,4},{6,7},{7,6},{8,9},{9,8},{10,11... | collective-permute-start | bytes 86024 | tf_op jit(solution)/shard_map/lat_even/ppermute | solution.py:419
  15.4 0.0 copy-done.4
  15.4 0.0 copy-done.3
  15.4 0.0 copy-done.1
  15.4 0.0 copy-done
  15.4 0.5 %columns.1.pack = f32[128,128]{1,0:T(8,128)S(1)} custom-call(f32[24,128,128]{2,1,0:T(8,128)S(1)} %bitcast.2, f32[2,128,128]{2,1,0:T(8,128)S(1)} %copy-done.1, f32[128,128]{1,0:T(8,128)S(1)} %copy-done.3, s32[128,128]{1,0:T(8,128)S(1)} %copy-done.4, s32[1,1]{1,0:T(1,128)S(6)} %copy.7.land), custom_call_target="tpu_custom_call" | custom-call | flops 1048576 | bytes 2097152 | tf_op jit(solution)/shard_map/columns/pallas_call | solution.py:422
  16.0 0.0 collective-permute-done.got_odd
  16.0 0.2 collective-permute-done.1.got_even
  16.2 0.4 %strips.1 = (f32[128,128]{1,0:T(8,128)S(1)}, f32[64,128]{1,0:T(8,128)S(1)}, f32[64,128]{1,0:T(8,128)S(1)}, f32[112,128]{1,0:T(8,128)S(1)}, f32[112,128]{1,0:T(8,128)S(1)}) custom-call(f32[56,128]{1,0:T(8,128)S(1)} %get-tuple-element.20.to_odd, f32[56,128]{1,0:T(8,128)S(1)} %get-tuple-element.21.to_even, f32[56,128]{1,0:T(8,128)S(1)} %collective-permute-done.got_odd, ...), custom_call_target="tpu_custom_call" | custom-call | flops 262144 | bytes 262144 | tf_op jit(solution)/shard_map/strips/pallas_call | solution.py:432
  16.6 0.0 copy-start.2
  16.6 2.8 %inner_early.1 = (f32[6,4,128,128]{3,2,1,0:T(8,128)S(1)}, f32[128,128]{1,0:T(8,128)S(1)}) custom-call(f32[6,4,128,128]{3,2,1,0:T(8,128)S(1)} %copy-done, f32[2,128,128]{2,1,0:T(8,128)S(1)} %copy-done.1, f32[128,128]{1,0:T(8,128)S(1)} %copy-done.3, s32[128,128]{1,0:T(8,128)S(1)} %copy-done.4, s32[1,1]{1,0:T(1,128)S(6)} %copy.7.land, ...), custom_call_target="tpu_custom_call" | custom-call | flops 20971520 | bytes 4194304 | tf_op jit(solution)/shard_map/inner_early/pallas_call | solution.py:448
  19.4 1.9 %collective-permute-start.3 = (f32[64,128]{1,0:T(8,128)S(1)}, f32[64,128]{1,0:T(8,128)S(1)}, u32[]{:S(2)}, u32[]{:S(2)}) collective-permute-start(f32[64,128]{1,0:T(8,128)S(1)} %get-tuple-element.32), channel_id=1, source_target_pairs={{0,16},{1,17},{2,18},{3,19},{4,20},{5,21},{6,22},{7,23},{8,24},{9,... | collective-permute-start | bytes 98312 | tf_op jit(solution)/shard_map/lon_east/ppermute | solution.py:467
  21.4 6.0 %collective-permute-start.2 = (f32[64,128]{1,0:T(8,128)S(1)}, f32[64,128]{1,0:T(8,128)S(1)}, u32[]{:S(2)}, u32[]{:S(2)}) collective-permute-start(f32[64,128]{1,0:T(8,128)S(1)} %get-tuple-element.29), channel_id=1, source_target_pairs={{0,496},{1,497},{2,498},{3,499},{4,500},{5,501},{6,502},{7,503},{8... | collective-permute-start | bytes 98312 | tf_op jit(solution)/shard_map/lon_west/ppermute | solution.py:469
  27.4 0.0 collective-permute-done.3.got_west
  27.5 0.0 copy-done.2
  27.5 0.9 %west.1.z_west = f32[128,128]{1,0:T(8,128)S(1)} custom-call(f32[128,128]{1,0:T(8,128)S(1)} %get-tuple-element.22.pack, f32[64,128]{1,0:T(8,128)S(1)} %collective-permute-done.3.got_west, f32[112,128]{1,0:T(8,128)S(1)} %get-tuple-element.25.north, f32[112,128]{1,0:T(8,128)S(1)} %get-tuple-element.26.south, f32[128,128]{1,0:T(8,128)S(1)} %get-tuple-element.30.ends_a, ...), custom_call_target="tpu_custom_call" | custom-call | flops 10485760 | bytes 2097152 | tf_op jit(solution)/shard_map/west/pallas_call | solution.py:478
  28.3 0.7 %collective-permute-done.2.got_east = f32[64,128]{1,0:T(8,128)S(1)} collective-permute-done((f32[64,128]{1,0:T(8,128)S(1)}, f32[64,128]{1,0:T(8,128)S(1)}, u32[]{:S(2)}, u32[]{:S(2)}) %collective-permute-start.2) | collective-permute-done | bytes 32800 | tf_op jit(solution)/shard_map/lon_west/ppermute | solution.py:469
  29.0 2.5 %last.1 = f32[6,4,128,128]{3,2,1,0:T(8,128)} custom-call(f32[128,128]{1,0:T(8,128)S(1)} %get-tuple-element.22.pack, f32[64,128]{1,0:T(8,128)S(1)} %collective-permute-done.2.got_east, f32[112,128]{1,0:T(8,128)S(1)} %get-tuple-element.25.north, f32[112,128]{1,0:T(8,128)S(1)} %get-tuple-element.26.south, f32[128,128]{1,0:T(8,128)S(1)} %get-tuple-element.30.ends_a, ...), custom_call_target="tpu_custom_call" | custom-call | flops 1048576 | bytes 4194304 | tf_op jit(solution)/shard_map/last/pallas_call | solution.py:489
  (1 shorter events, 0.0 us)
Async XLA Ops:
  0.0 15.4 %copy-start.4 = (s32[128,128]{1,0:T(8,128)S(1)}, s32[128,128]{1,0:T(8,128)}, u32[]{:S(2)}) copy-start(s32[128,128]{1,0:T(8,128)} %mask.7) | copy-start | bytes 196612
  0.0 15.4 %copy-start.3 = (f32[128,128]{1,0:T(8,128)S(1)}, f32[128,128]{1,0:T(8,128)}, u32[]{:S(2)}) copy-start(f32[128,128]{1,0:T(8,128)} %area.7) | copy-start | bytes 196612
  0.0 15.4 %copy-start.1 = (f32[2,128,128]{2,1,0:T(8,128)S(1)}, f32[2,128,128]{2,1,0:T(8,128)}, u32[]{:S(2)}) copy-start(f32[2,128,128]{2,1,0:T(8,128)} %w.7) | copy-start | bytes 393220
  0.0 15.4 %copy-start = (f32[6,4,128,128]{3,2,1,0:T(8,128)S(1)}, f32[6,4,128,128]{3,2,1,0:T(8,128)}, u32[]{:S(2)}) copy-start(f32[6,4,128,128]{3,2,1,0:T(8,128)} %fields.3) | copy-start | bytes 4718596
  1.9 14.1 %collective-permute-start = (f32[56,128]{1,0:T(8,128)S(1)}, f32[56,128]{1,0:T(8,128)S(1)}, u32[]{:S(2)}, u32[]{:S(2)}) collective-permute-start(f32[56,128]{1,0:T(8,128)S(1)} %get-tuple-element.20.to_odd), channel_id=1, source_target_pairs={{1,2},{2,1},{3,4},{4,3},{5,6},{6,5},{7,8},{8,7},{9,10},{10,9},{11,... | collective-permute-start | bytes 86024 | tf_op jit(solution)/shard_map/lat_odd/ppermute | solution.py:417
  4.0 12.2 %collective-permute-start.1 = (f32[56,128]{1,0:T(8,128)S(1)}, f32[56,128]{1,0:T(8,128)S(1)}, u32[]{:S(2)}, u32[]{:S(2)}) collective-permute-start(f32[56,128]{1,0:T(8,128)S(1)} %get-tuple-element.21.to_even), channel_id=1, source_target_pairs={{0,1},{1,0},{2,3},{3,2},{4,5},{5,4},{6,7},{7,6},{8,9},{9,8},{10,11... | collective-permute-start | bytes 86024 | tf_op jit(solution)/shard_map/lat_even/ppermute | solution.py:419
  16.6 10.9 %copy-start.2 = (bf16[256,896]{1,0:T(8,128)(2,1)S(1)}, bf16[256,896]{1,0:T(8,128)(2,1)}, u32[]{:S(2)}) copy-start(bf16[256,896]{1,0:T(8,128)(2,1)} %constant.2.clone.matrix) | copy-start | bytes 1376260
  19.4 8.0 %collective-permute-start.3 = (f32[64,128]{1,0:T(8,128)S(1)}, f32[64,128]{1,0:T(8,128)S(1)}, u32[]{:S(2)}, u32[]{:S(2)}) collective-permute-start(f32[64,128]{1,0:T(8,128)S(1)} %get-tuple-element.32), channel_id=1, source_target_pairs={{0,16},{1,17},{2,18},{3,19},{4,20},{5,21},{6,22},{7,23},{8,24},{9,... | collective-permute-start | bytes 98312 | tf_op jit(solution)/shard_map/lon_east/ppermute | solution.py:467
  21.4 7.6 %collective-permute-start.2 = (f32[64,128]{1,0:T(8,128)S(1)}, f32[64,128]{1,0:T(8,128)S(1)}, u32[]{:S(2)}, u32[]{:S(2)}) collective-permute-start(f32[64,128]{1,0:T(8,128)S(1)} %get-tuple-element.29), channel_id=1, source_target_pairs={{0,496},{1,497},{2,498},{3,499},{4,500},{5,501},{6,502},{7,503},{8... | collective-permute-start | bytes 98312 | tf_op jit(solution)/shard_map/lon_west/ppermute | solution.py:469
